TPU v7x, 256 devices: a whole 4x4x8 slice. The times are simulated.
256 devices in a mesh: dp: 32 (over y_lo, z, core), proto: 8 (over x, y_hi).
Axes of the slice: x: 4, y: 4 (y_hi: 2, y_lo: 2; y = y_hi * 2 + y_lo), z: 8, core: 2. Of those that a mesh axis runs over, the one named last changes fastest.
Arguments:
- feature_matrix: bfloat16 [8192, 128], P('dp'), may hold values from -64 to 64
- tangent_embed: bfloat16 [8192, 128], P('dp'), may hold values from -2 to 2
- anchor_matrix: bfloat16 [65536, 128], P('proto'), may hold values from -4 to 4
- anchor_perturbation: bfloat16 [65536, 128], P('proto'), may hold values from -0.5 to 0.5
- codes: bfloat16 [8192, 65536], P('dp', 'proto'), may hold values from 0 to 3, as said below
- partner_lookup: int32 [8192], P('dp'), may hold values from 0 to 8191, as said below
Outputs:
- hvp_embed: bfloat16 [8192, 128], P('dp')
- hvp_proto: bfloat16 [65536, 128], P('proto')
Inputs may be any that keep to these rules, and one draw needn't show every extreme that they name: partner_lookup[partner_lookup[i]] = i and partner_lookup[i] != i for every crop i. `codes`: positive.
All inputs are finite; a program needn't handle non-finite values.
Results may differ from a plain program's by a relative error of at most 0.0051.
Values may be sent and summed in bfloat16 or wider, within the bound.
No kernel may reach another device: no remote copies, remote signals or barrier semaphores. Data moves between devices by JAX's collectives and lax.ppermute only.
A program may use at most 128 MiB of HBM per device.

v0:
```python
import jax
import jax.numpy as jnp
from jax import lax
from jax.sharding import PartitionSpec as P

softening_constant = 0.1


def aggregated_elements(left, right):
    return lax.dot_general(
        left, right, (((1,), (1,)), ((), ())), preferred_element_type=jnp.float32
    )


def reduce_along_samples(left, right):
    return lax.dot_general(
        left, right, (((0,), (0,)), ((), ())), preferred_element_type=jnp.float32
    )


def body(feature_matrix, tangent_embed, anchor_matrix, anchor_perturbation, codes, partner_lookup):
    collected_features, gathered_tan = (
        lax.all_gather(feature_matrix, "dp", axis=0, tiled=True),
        lax.all_gather(tangent_embed, "dp", axis=0, tiled=True),
    )
    traded_contributions = jnp.take(collected_features, partner_lookup, axis=0)
    swapped_tan = jnp.take(gathered_tan, partner_lookup, axis=0)
    unscaled_affinity = (
        aggregated_elements(traded_contributions, anchor_matrix) / softening_constant
    )
    similarity_direction = (
        aggregated_elements(swapped_tan, anchor_matrix)
        + aggregated_elements(traded_contributions, anchor_perturbation)
    ) / softening_constant
    local_max = jnp.max(unscaled_affinity, axis=1)
    local_mass = jnp.sum(codes, axis=1, dtype=jnp.float32)
    row_max = lax.pmax(local_max, "proto")
    exponent = jnp.exp(unscaled_affinity - row_max[:, None])
    softmax_total, weighted, line_sum_norm = lax.psum(
        (jnp.sum(exponent, axis=1), jnp.sum(exponent * similarity_direction, axis=1), local_mass),
        "proto",
    )
    model_likelihood = exponent / softmax_total[:, None]
    mean_code_vector = weighted / softmax_total
    outer_patch_multiplier = (
        softening_constant
        * line_sum_norm[:, None]
        * model_likelihood
        * (similarity_direction - mean_code_vector[:, None])
    ).astype(jnp.bfloat16)
    right_crop_factor = (
        softening_constant * (line_sum_norm[:, None] * model_likelihood - codes.astype(jnp.float32))
    ).astype(jnp.bfloat16)
    partial_embed = jnp.dot(
        outer_patch_multiplier, anchor_matrix, preferred_element_type=jnp.float32
    ) + jnp.dot(right_crop_factor, anchor_perturbation, preferred_element_type=jnp.float32)
    incomplete_anchor_grad = reduce_along_samples(
        outer_patch_multiplier, traded_contributions
    ) + reduce_along_samples(right_crop_factor, swapped_tan)
    hvp_proto = lax.psum(incomplete_anchor_grad, "dp").astype(jnp.bfloat16)
    summed = lax.psum(partial_embed, "proto").astype(jnp.bfloat16)
    gathered_out = lax.all_gather(summed, "dp", axis=0, tiled=True)
    hvp_embed = jnp.take(gathered_out, partner_lookup, axis=0)
    return (hvp_embed, hvp_proto)


def solution(mesh):
    in_specs = (
        P("dp", None),
        P("dp", None),
        P("proto", None),
        P("proto", None),
        P("dp", "proto"),
        P("dp"),
    )
    out_specs = (P("dp", None), P("proto", None))
    return jax.shard_map(body, mesh=mesh, in_specs=in_specs, out_specs=out_specs, check_vma=False)
```

profile of v0, /device:TPU:8, one launch (start us, length us, event | category | flops | bytes accessed | tf_op | source)
XLA Modules:
  0.0 401.0 jit_solution(2757636841518823086)
XLA Ops:
  7.2 0.7 all-gather.6.cloned.1.call-update
  8.0 0.7 all-gather.4.cloned.1.call-update
  8.7 0.0 all-gather.8.cloned.1.call-start
  8.7 0.7 compare_select_fusion
  9.4 0.7 compare_and_fusion
  10.1 2.8 convert_reduce_fusion
  12.9 63.6 %all-gather.6.cloned.1.call-done = bf16[8192,128]{1,0:T(8,128)(2,1)} async-done(((bf16[256,128]{1,0:T(8,128)(2,1)}), bf16[8192,128]{1,0:T(8,128)(2,1)}) %all-gather.6.cloned.1.call-update) | async-done | bytes 2097168 | tf_op jit(solution)/shard_map/all_gather | solution.py:24
  76.6 2.6 gather_fusion.1
  79.2 4.5 %fusion.5 = f32[256,8192]{1,0:T(8,128)} fusion(bf16[8192,128]{1,0:T(8,128)(2,1)S(1)} %copy-done, bf16[256,128]{1,0:T(8,128)(2,1)S(1)} %gather_fusion.1, pred[256]{0:T(512)(128)(4,1)S(1)} %compare_and_fusion), kind=kOutput, calls=%fused_computation.20 | convolution fusion | flops 536903680 | bytes 10551552 | tf_op jit(solution)/shard_map/dot_general | solution.py:10
  83.7 58.8 %all-gather.4.cloned.1.call-done = bf16[8192,128]{1,0:T(8,128)(2,1)} async-done(((bf16[256,128]{1,0:T(8,128)(2,1)}), bf16[8192,128]{1,0:T(8,128)(2,1)}) %all-gather.4.cloned.1.call-update) | async-done | bytes 2097168 | tf_op jit(solution)/shard_map/all_gather | solution.py:23
  142.5 2.6 gather_fusion
  145.1 4.5 %fusion.9 = (f32[256]{0:T(256)S(1)}, f32[256,8192]{1,0:T(8,128)}) fusion(bf16[8192,128]{1,0:T(8,128)(2,1)S(1)} %copy-done, bf16[256,128]{1,0:T(8,128)(2,1)S(1)} %gather_fusion, pred[256]{0:T(512)(128)(4,1)S(1)} %compare_and_fusion), kind=kOutput, calls=%fused_computation.28 | convolution fusion | flops 541097728 | bytes 10552576 | tf_op jit(solution)/shard_map/dot_general | solution.py:10
  149.6 23.3 %pmax.7 = f32[256]{0:T(256)S(1)} all-reduce(f32[256]{0:T(256)S(1)} %get-tuple-element.10), channel_id=1, replica_groups=mesh['dp'=32,'proto'=8] {'proto'}, use_global_device_ids=true, to_apply=%region_3.5 | all-reduce | flops 256 | bytes 2048 | tf_op jit(solution)/shard_map/pmax | solution.py:37
  172.8 10.1 %fusion.4 = (f32[256]{0:T(256)S(1)}, f32[256]{0:T(256)S(1)}, f32[256,8192]{1,0:T(8,128)}) fusion(f32[256,8192]{1,0:T(8,128)} %get-tuple-element.11, f32[256]{0:T(256)S(1)} %pmax.7, f32[256,8192]{1,0:T(8,128)} %fusion.5, bf16[8192,128]{1,0:T(8,128)(2,1)} %param.11, bf16[256,128]{1,0:T(8,128)(2,1)S(1)} %gather_fusion, pred[256]{0:T(512)(128)(4,1)S(1)} %compare_and_fusion), kind=kOutput, calls=%fused_computation.15 | convolution fusion | flops 549486080 | bytes 27331840 | tf_op jit(solution)/shard_map/dot_general | solution.py:10
  182.9 19.1 %all-reduce = (f32[256]{0:T(256)S(1)}, f32[256]{0:T(256)S(1)}, f32[256]{0:T(256)S(1)}) all-reduce(f32[256]{0:T(256)S(1)} %get-tuple-element.4, f32[256]{0:T(256)S(1)} %get-tuple-element.3, f32[256]{0:T(256)S(1)} %convert_reduce_fusion), channel_id=1, replica_groups=mesh['dp'=32,'proto'=8] {'proto'}, use_global_device_ids=true, to_apply=%region_7.9 | all-reduce | flops 768 | bytes 6144 | tf_op jit(solution)/shard_map/psum | solution.py:39
  202.1 9.7 %fusion.2 = (bf16[256,8192]{1,0:T(8,128)(2,1)S(1)}, bf16[256,8192]{1,0:T(8,128)(2,1)S(1)}) fusion(bf16[256,8192]{1,0:T(8,128)(2,1)} %param.12, f32[256]{0:T(256)S(1)} %get-tuple-element.7, f32[256]{0:T(256)S(1)} %get-tuple-element.6, f32[256,8192]{1,0:T(8,128)} %get-tuple-element.11, f32[256]{0:T(256)S(1)} %pmax.7, f32[256,8192]{1,0:T(8,128)} %get-tuple-element.12, ...), kind=kLoop, calls=%fused_computation.10 | loop fusion | flops 23068672 | bytes 29365248 | tf_op jit(solution)/shard_map/convert_element_type | solution.py:53
  211.7 1.3 fusion.10
  213.0 1.4 fusion.8
  214.4 3.4 convolution_add_fusion.1
  217.8 1.4 convolution_add_fusion.2
  219.1 41.9 %all-reduce.3 = bf16[256,128]{1,0:T(8,128)(2,1)} all-reduce(f32[256,128]{1,0:T(8,128)S(1)} %convolution_add_fusion.2), channel_id=1, replica_groups=mesh['dp'=32,'proto'=8] {'proto'}, use_global_device_ids=true, to_apply=%region_8.10 | all-reduce | flops 32768 | bytes 196608 | tf_op jit(solution)/shard_map/psum | solution.py:61
  261.0 130.1 %all-reduce.4 = bf16[8192,128]{1,0:T(8,128)(2,1)} all-reduce(f32[8192,128]{1,0:T(8,128)} %convolution_add_fusion.1), channel_id=1, replica_groups=mesh['dp'=32,'proto'=8] {'dp'}, use_global_device_ids=true, to_apply=%region_9.11 | all-reduce | flops 1048576 | bytes 6291456 | tf_op jit(solution)/shard_map/psum | solution.py:60
  391.1 2.6 gather_fusion.2
  393.7 0.7 broadcast_select_fusion.2
  (11 shorter events, 0.1 us)
Async XLA Ops:
  7.2 72.0 %copy-start = (bf16[8192,128]{1,0:T(8,128)(2,1)S(1)}, bf16[8192,128]{1,0:T(8,128)(2,1)}, u32[]{:S(2)}) copy-start(bf16[8192,128]{1,0:T(8,128)(2,1)} %param.10) | copy-start | bytes 6291460
  7.2 69.4 %all-gather.6.cloned.1.call-start = ((), (), s32[]{:S(2)}) async-start(), calls=%async_computation.1 | async-start | bytes 2162688 | tf_op jit(solution)/shard_map/all_gather | solution.py:24
  7.9 134.6 %all-gather.4.cloned.1.call-start = ((), (), s32[]{:S(2)}) async-start(), calls=%async_computation | async-start | bytes 2162688 | tf_op jit(solution)/shard_map/all_gather | solution.py:23
  8.7 382.5 %all-gather.8.cloned.1.call-start = ((), (), s32[]{:S(2)}) async-start(), calls=%async_computation.2 | async-start | bytes 2162688 | tf_op jit(solution)/shard_map/all_gather | solution.py:62
  214.4 3.4 copy-start.1
Sparse Core Ops, SparseCore 0:
  9.8 66.6 all-gather.5
  78.4 63.9 all-gather.3
  261.1 60.5 all-gather.7
where the time goes:
time: 401 us
  blocking collectives  214 us (53%)
  waiting for transfers between devices  124 us (31%)
  matrix products  26.5 us (7%)
  other arithmetic  14.6 us (4%)
  between operations  13.8 us (3%)
  local copies, waits for them, and re-layouts  7.78 us (2%)
    psum x1, blocking collectives, body(): hvp_proto = lax.psum(incomplete_anchor_grad, 'dp').astype(jnp.bfloat16)  130 us
    all_gather x1, waiting for transfers between devices, body(): lax.all_gather(tangent_embed, 'dp', axis=0, tiled=True)  63.6 us
    all_gather x1, waiting for transfers between devices, body(): lax.all_gather(feature_matrix, 'dp', axis=0, tiled=True)  58.8 us
    psum x1, blocking collectives, body(): summed = lax.psum(partial_embed, 'proto').astype(jnp.bfloat16)  41.9 us
    pmax x1, blocking collectives, body(): row_max = lax.pmax(local_max, 'proto')  23.3 us
    dot_general x3, matrix products, aggregated_elements(): lax.dot_general(left, right, (((1,), (1,)), ((), ())), preferred_element_...  19.1 us
    psum x1, blocking collectives, body(): lax.psum((jnp.sum(exponent, axis=1), jnp.sum(exponent * similarity_direct...  19.1 us
    convert_element_type x1, other arithmetic, body(): right_crop_factor = (softening_constant * (line_sum_norm[:, None] * model...  9.65 us
  transfers between devices with their start and end apart: 3, of which 2 were waited for; matrix products, arithmetic and copies ran while one was open for 3% of the time, Pallas kernels for 0%

commit v1 on v0

v1 whole, which is shorter than its diff:
```python
import jax
import jax.numpy as jnp
from jax import lax
from jax.experimental import pallas as pl
from jax.experimental.pallas import tpu as pltpu
from jax.sharding import PartitionSpec as P

F32 = jnp.float32
BF16 = jnp.bfloat16
NT = (((1,), (1,)), ((), ()))
TN = (((0,), (0,)), ((), ()))
D = 128
ROWS = 256
LOCAL = 8192
DP = 32
PR = 8
SUB = ROWS // PR
CN = 2048
NCH = LOCAL // CN
SCALE = 0.1
VMEM = pl.BlockSpec(memory_space=pltpu.VMEM)
SMEM = pl.BlockSpec(memory_space=pltpu.SMEM)
GRANT = 56 * 1024 * 1024


def split3(x):
    hi = x.astype(BF16).astype(F32)
    mid = (x - hi).astype(BF16).astype(F32)
    lo = (x - hi - mid).astype(BF16).astype(F32)
    return hi, mid, lo


def codes_kernel(q_ref, codes_ref, pert_ref, tan_ref, h_ref, blk_ref, acc):
    step = pl.program_id(0)

    @pl.when(step == 0)
    def _():
        acc[...] = jnp.zeros_like(acc)

    rhs = jnp.concatenate([pert_ref[...], jnp.ones((CN, D), BF16)], axis=1)
    acc[...] += jnp.dot(codes_ref[...], rhs, preferred_element_type=F32)

    @pl.when(step == NCH - 1)
    def _():
        h_ref[...] = acc[:, :D]
        mass = jnp.transpose(acc[:, D:])[0:1, :]
        hi, mid, lo = split3(mass)
        parts = jnp.concatenate([hi, mid, lo, jnp.zeros((5, ROWS), F32)], axis=0)
        parts = jnp.concatenate([parts[:, :D], parts[:, D:]], axis=0).astype(BF16)
        rows = tan_ref[pl.ds(pl.multiple_of(q_ref[0] * SUB, SUB), SUB), :]
        block = jnp.concatenate([rows, parts], axis=0)
        for i in range(DP):
            blk_ref[i] = block


def codes_pass(q, codes, pert, tan):
    return pl.pallas_call(
        codes_kernel,
        grid=(NCH,),
        in_specs=[
            SMEM,
            pl.BlockSpec((ROWS, CN), lambda c: (0, c)),
            pl.BlockSpec((CN, D), lambda c: (c, 0)),
            pl.BlockSpec((ROWS, D), lambda c: (0, 0)),
        ],
        out_specs=[
            pl.BlockSpec((ROWS, D), lambda c: (0, 0)),
            pl.BlockSpec((DP, SUB + 16, D), lambda c: (0, 0, 0)),
        ],
        out_shape=[
            jax.ShapeDtypeStruct((ROWS, D), F32),
            jax.ShapeDtypeStruct((DP, SUB + 16, D), BF16),
        ],
        scratch_shapes=[pltpu.VMEM((ROWS, 2 * D), F32)],
        cost_estimate=pl.CostEstimate(flops=2 * ROWS * LOCAL * 256, bytes_accessed=7 << 20, transcendentals=0),
        name="codes_pass",
    )(q, codes, pert, tan)


RG = 16


def score_kernel(f_ref, tan_ref, a_ref, p_ref, e_ref, u_ref, cst_ref, st_ref, x_ref, w_ref, s_sc, t_sc, run):
    step = pl.program_id(0)
    f = f_ref[...]
    s_sc[...] = lax.dot_general(f, a_ref[...], NT, preferred_element_type=F32)
    left = jnp.concatenate([tan_ref[...], f], axis=1)
    right = jnp.concatenate([a_ref[...], p_ref[...]], axis=1)
    t_sc[...] = lax.dot_general(left, right, NT, preferred_element_type=F32)

    @pl.when(step == 0)
    def _():
        run[0] = jnp.full((ROWS, D), -jnp.inf, F32)
        run[1] = jnp.zeros((ROWS, D), F32)
        run[2] = jnp.zeros((ROWS, D), F32)
        x_ref[...] = jnp.zeros_like(x_ref)
        w_ref[...] = jnp.zeros_like(w_ref)

    for g in range(ROWS // RG):
        rows = slice(g * RG, (g + 1) * RG)
        s = s_sc[rows, :]
        t = t_sc[rows, :] * (1.0 / SCALE)
        top = jnp.max(s, axis=1, keepdims=True)
        e = jnp.exp((s - top) * (1.0 / SCALE))
        z = jnp.sum(e, axis=1, keepdims=True)
        et = jnp.sum(e * t, axis=1, keepdims=True)
        mean = et / z
        e_ref[rows, :] = e.astype(BF16)
        u_ref[rows, :] = (e * (t - mean)).astype(BF16)
        lane = lax.broadcasted_iota(jnp.int32, (RG, D), 1)
        cst_ref[0, rows, :] = jnp.where(lane == 0, top * (1.0 / SCALE), mean)
        run_new = jnp.broadcast_to(z, (RG, D))
        st_ref[0, rows, :] = jnp.broadcast_to(top * (1.0 / SCALE), (RG, D))
        st_ref[1, rows, :] = run_new
        st_ref[2, rows, :] = jnp.broadcast_to(et, (RG, D))

    top = st_ref[0]
    z = st_ref[1]
    et = st_ref[2]
    mean = et / z
    old = run[0]
    new = jnp.maximum(old, top)
    alpha = jnp.exp(old - new)
    beta = jnp.exp(top - new)
    e = e_ref[...]
    ea = jnp.dot(e, a_ref[...], preferred_element_type=F32)
    ep = jnp.dot(e, p_ref[...], preferred_element_type=F32)
    ua = jnp.dot(u_ref[...], a_ref[...], preferred_element_type=F32)
    x_ref[...] = x_ref[...] * alpha + beta * (ua + ep + mean * ea)
    w_ref[...] = w_ref[...] * alpha + beta * ea
    run[0] = new
    run[1] = run[1] * alpha + beta * z
    run[2] = run[2] * alpha + beta * et
    st_ref[...] = run[...]


def score_pass(f, tan, a, p):
    return pl.pallas_call(
        score_kernel,
        grid=(NCH,),
        in_specs=[
            pl.BlockSpec((ROWS, D), lambda c: (0, 0)),
            pl.BlockSpec((ROWS, D), lambda c: (0, 0)),
            pl.BlockSpec((CN, D), lambda c: (c, 0)),
            pl.BlockSpec((CN, D), lambda c: (c, 0)),
        ],
        out_specs=[
            pl.BlockSpec((ROWS, CN), lambda c: (0, c)),
            pl.BlockSpec((ROWS, CN), lambda c: (0, c)),
            pl.BlockSpec((1, ROWS, D), lambda c: (c, 0, 0)),
            pl.BlockSpec((3, ROWS, D), lambda c: (0, 0, 0)),
            pl.BlockSpec((ROWS, D), lambda c: (0, 0)),
            pl.BlockSpec((ROWS, D), lambda c: (0, 0)),
        ],
        out_shape=[
            jax.ShapeDtypeStruct((ROWS, LOCAL), BF16),
            jax.ShapeDtypeStruct((ROWS, LOCAL), BF16),
            jax.ShapeDtypeStruct((NCH, ROWS, D), F32),
            jax.ShapeDtypeStruct((3, ROWS, D), F32),
            jax.ShapeDtypeStruct((ROWS, D), F32),
            jax.ShapeDtypeStruct((ROWS, D), F32),
        ],
        scratch_shapes=[
            pltpu.VMEM((ROWS, CN), F32),
            pltpu.VMEM((ROWS, CN), F32),
            pltpu.VMEM((3, ROWS, D), F32),
        ],
        compiler_params=pltpu.CompilerParams(vmem_limit_bytes=GRANT),
        cost_estimate=pl.CostEstimate(flops=14 * ROWS * LOCAL * D * 2, bytes_accessed=12 << 20, transcendentals=ROWS * LOCAL),
        name="score_pass",
    )(f, tan, a, p)


STAT = 16


def pick_kernel(q_ref, tab_ref, part_ref, st_ref, pay_ref):
    q = q_ref[0]
    partner = part_ref[...]
    group = partner // ROWS
    row = partner % ROWS
    mine = (row // SUB) == q
    column = jnp.where(mine, group * SUB + row % SUB, -1)
    hot = (lax.broadcasted_iota(jnp.int32, (ROWS, DP * SUB), 1) == column).astype(F32).astype(BF16)
    table = tab_ref[:, :SUB, :].reshape(DP * SUB, D)
    rows = jnp.dot(hot, table, preferred_element_type=F32).astype(BF16)

    hot_group = (lax.broadcasted_iota(jnp.int32, (ROWS, DP), 1) == group).astype(F32).astype(BF16)
    mass_rows = tab_ref[:, SUB:, :].astype(F32)
    mass = jnp.zeros((ROWS, ROWS), F32)
    for k in (2, 1, 0):
        piece = jnp.concatenate([mass_rows[:, k, :], mass_rows[:, 8 + k, :]], axis=1).astype(BF16)
        mass = mass + jnp.dot(hot_group, piece, preferred_element_type=F32)
    here = lax.broadcasted_iota(jnp.int32, (ROWS, ROWS), 1) == row
    mass = jnp.sum(jnp.where(here, mass, 0.0), axis=1, keepdims=True)

    lane = lax.broadcasted_iota(jnp.int32, (ROWS, D), 1)
    values = (st_ref[0], st_ref[1], st_ref[2], jnp.broadcast_to(mass, (ROWS, D)))
    cols = jnp.zeros((ROWS, D), F32)
    for v, value in enumerate(values):
        for k, piece in enumerate(split3(value)):
            cols = jnp.where(lane == v * 3 + k, piece, cols)
    flat = jnp.transpose(cols)[:STAT, :]
    flat = jnp.concatenate([flat[:, :D], flat[:, D:]], axis=0).astype(BF16)
    payload = jnp.concatenate([rows, flat], axis=0)
    for i in range(PR):
        pay_ref[i] = payload


def pick(q, tab, partner, st):
    return pl.pallas_call(
        pick_kernel,
        in_specs=[SMEM, VMEM, VMEM, VMEM],
        out_specs=VMEM,
        out_shape=jax.ShapeDtypeStruct((PR, ROWS + 2 * STAT, D), BF16),
        compiler_params=pltpu.CompilerParams(vmem_limit_bytes=GRANT),
        name="pick",
    )(q, tab, partner, st)


def proto_kernel(c_ref, rec_ref, f_ref, tan_ref, st_ref, cst_ref, x_ref, w_ref, u_ref, e_ref, codes_ref,
                 mine_ref, send_ref, emb_ref, coef, swt):
    step = pl.program_id(0)

    @pl.when(step == 0)
    def _():
        total = jnp.zeros((ROWS, D), F32)
        flats = []
        for i in range(PR):
            total = total + rec_ref[i, :ROWS, :].astype(F32)
            flat = rec_ref[i, ROWS:, :].astype(F32)
            flats.append(jnp.concatenate([flat[:STAT], flat[STAT:]], axis=1))
        swt[...] = (total * SCALE).astype(BF16)
        cols = jnp.transpose(jnp.concatenate(flats, axis=0))
        value = [[(cols[:, i * STAT + 3 * v : i * STAT + 3 * v + 1]
                   + cols[:, i * STAT + 3 * v + 1 : i * STAT + 3 * v + 2])
                  + cols[:, i * STAT + 3 * v + 2 : i * STAT + 3 * v + 3] for v in range(4)] for i in range(PR)]
        top = value[0][0]
        for i in range(1, PR):
            top = jnp.maximum(top, value[i][0])
        z = jnp.zeros((ROWS, 1), F32)
        et = jnp.zeros((ROWS, 1), F32)
        mass = jnp.zeros((ROWS, 1), F32)
        for i in range(PR):
            shift = jnp.exp(value[i][0] - top)
            z = z + shift * value[i][1]
            et = et + shift * value[i][2]
            mass = mass + value[i][3]
        mean = et / z
        weight = SCALE * mass / z
        top = jnp.broadcast_to(top, (ROWS, D))
        mean = jnp.broadcast_to(mean, (ROWS, D))
        weight = jnp.broadcast_to(weight, (ROWS, D))
        coef[0] = top
        coef[1] = mean
        coef[2] = weight
        emb_ref[...] = weight * jnp.exp(st_ref[0] - top) * (x_ref[...] - mean * w_ref[...])

    f = f_ref[...].astype(F32)
    tan = tan_ref[...].astype(F32)
    top_c = jnp.broadcast_to(cst_ref[0, :, 0:1], (ROWS, D))
    mean_c = jnp.broadcast_to(cst_ref[0, :, 1:2], (ROWS, D))
    weight = coef[2] * jnp.exp(top_c - coef[0])
    f1 = (weight * f).astype(BF16)
    f2 = (weight * ((mean_c - coef[1]) * f + tan)).astype(BF16)
    res = lax.dot_general(u_ref[...], f1, TN, preferred_element_type=F32)
    res = res + lax.dot_general(e_ref[...], f2, TN, preferred_element_type=F32)
    res = res - lax.dot_general(codes_ref[...], swt[...], TN, preferred_element_type=F32)
    first = c_ref[0] == 0
    for b in range(CN // (2 * ROWS)):
        even = res[2 * b * ROWS : (2 * b + 1) * ROWS]
        odd = res[(2 * b + 1) * ROWS : (2 * b + 2) * ROWS]
        mine_ref[b] = jnp.where(first, even, odd)
        send_ref[b] = jnp.where(first, odd, even).astype(BF16)


def proto_pass(core, rec, f, tan, st, cst, x, w, u, e, codes):
    nb = CN // (2 * ROWS)
    whole2 = pl.BlockSpec((ROWS, D), lambda c: (0, 0))
    return pl.pallas_call(
        proto_kernel,
        grid=(NCH,),
        in_specs=[
            SMEM,
            pl.BlockSpec((PR, ROWS + 2 * STAT, D), lambda c: (0, 0, 0)),
            whole2,
            whole2,
            pl.BlockSpec((3, ROWS, D), lambda c: (0, 0, 0)),
            pl.BlockSpec((1, ROWS, D), lambda c: (c, 0, 0)),
            whole2,
            whole2,
            pl.BlockSpec((ROWS, CN), lambda c: (0, c)),
            pl.BlockSpec((ROWS, CN), lambda c: (0, c)),
            pl.BlockSpec((ROWS, CN), lambda c: (0, c)),
        ],
        out_specs=[
            pl.BlockSpec((nb, ROWS, D), lambda c: (c, 0, 0)),
            pl.BlockSpec((nb, ROWS, D), lambda c: (c, 0, 0)),
            pl.BlockSpec((ROWS, D), lambda c: (0, 0)),
        ],
        out_shape=[
            jax.ShapeDtypeStruct((16, ROWS, D), F32),
            jax.ShapeDtypeStruct((16, ROWS, D), BF16),
            jax.ShapeDtypeStruct((ROWS, D), F32),
        ],
        scratch_shapes=[pltpu.VMEM((3, ROWS, D), F32), pltpu.VMEM((ROWS, D), BF16)],
        compiler_params=pltpu.CompilerParams(vmem_limit_bytes=GRANT),
        cost_estimate=pl.CostEstimate(flops=6 * ROWS * LOCAL * D * 2, bytes_accessed=15 << 20, transcendentals=0),
        name="proto_pass",
    )(core, rec, f, tan, st, cst, x, w, u, e, codes)


CORE_PERM = [(i, i ^ 1) for i in range(DP)]
Y_PERM = [(i, i ^ 16) for i in range(DP)]
Z_GROUPS = [[y * 16 + z * 2 + c for z in range(8)] for y in range(2) for c in range(2)]


def exchange(x, axis, groups=None):
    return lax.all_to_all(x, axis, 0, 0, axis_index_groups=groups, tiled=True)


def body(feature_matrix, tangent_embed, anchor_matrix, anchor_perturbation, codes, partner_lookup):
    dp = lax.axis_index("dp")
    q = lax.axis_index("proto")
    core = dp % 2
    y = dp // 16
    partner = partner_lookup.reshape(ROWS, 1)
    qs = q.reshape(1)

    h_part, block = codes_pass(qs, codes, anchor_perturbation, tangent_embed)
    table = exchange(block, "dp")
    e, u, cst, st, x, w = score_pass(feature_matrix, tangent_embed, anchor_matrix, anchor_perturbation)
    h_rows = jnp.sum(exchange(h_part.reshape(PR, SUB, D), "proto"), axis=0)
    h_table = exchange(jnp.broadcast_to(h_rows.astype(BF16)[None], (DP, SUB, D)), "dp").reshape(DP * SUB, D)

    payload = pick(qs, table, partner, st)
    received = exchange(payload, "proto")
    mine, send, embed = proto_pass(core.reshape(1), received, feature_matrix, tangent_embed, st, cst, x, w, u, e, codes)

    got = lax.ppermute(send, "dp", CORE_PERM)
    half = (mine + got.astype(F32)).reshape(2, 8, ROWS, D)
    other = lax.dynamic_index_in_dim(half, 1 - y, 0, keepdims=False).astype(BF16)
    own = lax.dynamic_index_in_dim(half, y, 0, keepdims=False)
    quarter = own + lax.ppermute(other, "dp", Y_PERM).astype(F32)
    pieces = exchange(quarter.astype(BF16), "dp", Z_GROUPS)
    final = jnp.sum(pieces.astype(F32), axis=0).astype(BF16)

    along_z = exchange(jnp.broadcast_to(final[None], (8, ROWS, D)), "dp", Z_GROUPS)
    from_y = lax.ppermute(along_z, "dp", Y_PERM)
    plane = jnp.where(y == 0, jnp.stack([along_z, from_y]), jnp.stack([from_y, along_z])).reshape(16, ROWS, D)
    from_core = lax.ppermute(plane, "dp", CORE_PERM)
    pair = jnp.where(core == 0, jnp.stack([plane, from_core], 1), jnp.stack([from_core, plane], 1))
    hvp_proto = pair.reshape(LOCAL, D)

    group = partner // ROWS
    row = partner % ROWS
    column = jnp.where(row // SUB == q, group * SUB + row % SUB, -1)
    hot = (lax.broadcasted_iota(jnp.int32, (ROWS, DP * SUB), 1) == column).astype(BF16)
    h_mine = jnp.dot(hot, h_table, preferred_element_type=F32)
    embed = embed - SCALE * h_mine
    part = jnp.sum(exchange(embed.reshape(PR, SUB, D), "proto"), axis=0).astype(BF16)
    hvp_embed = exchange(jnp.broadcast_to(part[None], (PR, SUB, D)), "proto").reshape(ROWS, D)
    return (hvp_embed, hvp_proto)


def solution(mesh):
    in_specs = (
        P("dp", None),
        P("dp", None),
        P("proto", None),
        P("proto", None),
        P("dp", "proto"),
        P("dp"),
    )
    out_specs = (P("dp", None), P("proto", None))
    return jax.shard_map(body, mesh=mesh, in_specs=in_specs, out_specs=out_specs, check_vma=False)
```

time: 401 us -> 190 us (0.47)
  blocking collectives: 214 us -> 63.1 us
  waiting for transfers between devices: 124 us -> 55.9 us
  Pallas kernels: 0 us -> 31.5 us
  starting transfers between devices: 0.11 us -> 28.2 us
  matrix products: 26.5 us -> 0.35 us
  between operations: 13.8 us -> 0.8 us
  other arithmetic: 14.6 us -> 3.71 us
    psum x3 -> x0, blocking collectives: 191 us -> none  [the longest x1 130 us: body(): hvp_proto = lax.psum(incomplete_anchor_grad, 'dp').astype(jnp.bfloat16)]
    all_gather x3 -> x0, waiting for transfers between devices: 122 us -> none  [the longest x1 63.6 us: body(): lax.all_gather(tangent_embed, 'dp', axis=0, tiled=True)]
    all_to_all x0 -> x4, blocking collectives: none -> 63.1 us  [exchange(): return lax.all_to_all(x, axis, 0, 0, axis_index_groups=groups, tiled=True)]
    all_to_all x0 -> x4, waiting for transfers between devices: none -> 31.6 us  [exchange(): return lax.all_to_all(x, axis, 0, 0, axis_index_groups=groups, tiled=True)]
    pallas_call x0 -> x4, Pallas kernels: none -> 31.5 us  [the longest x1 12.2 us: score_pass(): pl.pallas_call(score_kernel, grid=(NCH,), in_specs=[pl.BlockSpec((ROWS, D...]
    dot_general x7 -> x1, matrix products: 26.5 us -> 0.35 us  [body(): h_mine = jnp.dot(hot, h_table, preferred_element_type=F32)]
    all_to_all x0 -> x4, starting transfers between devices: none -> 24.8 us  [exchange(): return lax.all_to_all(x, axis, 0, 0, axis_index_groups=groups, tiled=True)]
    ppermute x0 -> x4, waiting for transfers between devices: none -> 24.3 us  [the longest x1 12.2 us: body(): quarter = own + lax.ppermute(other, 'dp', Y_PERM).astype(F32)]
  transfers between devices with their start and end apart: 3 -> 8, of which waited for: 2 -> 7; matrix products, arithmetic and copies ran while one was open for 3% -> 1% of each run, Pallas kernels for 0% -> 6%
where the time goes in v1:
time: 190 us; the launch traced here: 188 us
  blocking collectives  63.1 us (33%)
  waiting for transfers between devices  55.9 us (29%)
  Pallas kernels  31.5 us (17%)
  starting transfers between devices  28.2 us (15%)
  local copies, waits for them, and re-layouts  4.55 us (2%)
  other arithmetic  3.71 us (2%)
    all_to_all x4, blocking collectives, exchange(): return lax.all_to_all(x, axis, 0, 0, axis_index_groups=groups, tiled=True)  63.1 us
    all_to_all x4, waiting for transfers between devices, exchange(): return lax.all_to_all(x, axis, 0, 0, axis_index_groups=groups, tiled=True)  31.6 us
    all_to_all x4, starting transfers between devices, exchange(): return lax.all_to_all(x, axis, 0, 0, axis_index_groups=groups, tiled=True)  24.8 us
    pallas_call x1, Pallas kernels, score_pass(): pl.pallas_call(score_kernel, grid=(NCH,), in_specs=[pl.BlockSpec((ROWS, D...  12.2 us
    ppermute x1, waiting for transfers between devices, body(): quarter = own + lax.ppermute(other, 'dp', Y_PERM).astype(F32)  12.2 us
    pallas_call x1, Pallas kernels, proto_pass(): pl.pallas_call(proto_kernel, grid=(NCH,), in_specs=[SMEM, pl.BlockSpec((P...  11.1 us
    ppermute x1, waiting for transfers between devices, body(): from_y = lax.ppermute(along_z, 'dp', Y_PERM)  9.27 us
    pallas_call x1, Pallas kernels, codes_pass(): pl.pallas_call(codes_kernel, grid=(NCH,), in_specs=[SMEM, pl.BlockSpec((R...  5.38 us
  transfers between devices with their start and end apart: 8, of which 7 were waited for; matrix products, arithmetic and copies ran while one was open for 1% of the time, Pallas kernels for 6%

profile of v1, /device:TPU:8, one launch (start us, length us, event | category | flops | bytes accessed | tf_op | source)
XLA Modules:
  0.0 188.2 jit_solution(8697494083862558412)
XLA Ops:
  0.6 5.4 %codes_pass.1 = (f32[256,128]{1,0:T(8,128)}, bf16[32,48,128]{2,1,0:T(8,128)(2,1)}) custom-call(s32[1]{0:T(128)} %bitcast.1.q_ref, bf16[256,8192]{1,0:T(8,128)(2,1)} %codes_ref.3, bf16[8192,128]{1,0:T(8,128)(2,1)} %p_ref.1, bf16[256,128]{1,0:T(8,128)(2,1)} %tan_ref.5), custom_call_target="tpu_custom_call" | custom-call | flops 1073741824 | bytes 7340032 | tf_op jit(solution)/shard_map/codes_pass/pallas_call | solution.py:57
  6.0 10.1 %all-to-all-start = ((bf16[32,48,128]{2,1,0:T(8,128)(2,1)}), bf16[32,48,128]{2,1,0:T(8,128)(2,1)S(1)}, u32[]{:S(2)}, u32[]{:S(2)}) async-start(bf16[32,48,128]{2,1,0:T(8,128)(2,1)} %get-tuple-element.13), calls=%async_computation | async-start | bytes 786432 | tf_op jit(solution)/shard_map/all_to_all | solution.py:319
  16.9 12.2 %score_pass.1 = (bf16[256,8192]{1,0:T(8,128)(2,1)}, bf16[256,8192]{1,0:T(8,128)(2,1)}, f32[4,256,128]{2,1,0:T(8,128)}, f32[3,256,128]{2,1,0:T(8,128)}, f32[256,128]{1,0:T(8,128)}, /*index=5*/f32[256,128]{1,0:T(8,128)}) custom-call(bf16[256,128]{1,0:T(8,128)(2,1)} %f_ref.3, bf16[256,128]{1,0:T(8,128)(2,1)} %tan_ref.5, bf16[8192,128]{1,0:T(8,128)(2,1)} %a_ref.1, ...), custom_call_target="tpu_custom_call" | custom-call | flops 7516192768 | bytes 12582912 | tf_op jit(solution)/shard_map/score_pass/pallas_call | solution.py:138
  29.2 1.5 all-to-all-done.tab_ref
  31.4 2.8 %pick.1 = bf16[8,288,128]{2,1,0:T(8,128)(2,1)} custom-call(s32[1]{0:T(128)} %bitcast.1.q_ref, bf16[32,48,128]{2,1,0:T(8,128)(2,1)} %copy-done.1, s32[256,1]{1,0:T(8,128)} %copy.8.part_ref, f32[3,256,128]{2,1,0:T(8,128)} %get-tuple-element.14.st_ref), custom_call_target="tpu_custom_call" | custom-call | tf_op jit(solution)/shard_map/pick/pallas_call | solution.py:211
  34.2 6.0 %all-to-all-start.1 = ((bf16[8,288,128]{2,1,0:T(8,128)(2,1)}), bf16[8,288,128]{2,1,0:T(8,128)(2,1)S(1)}, u32[]{:S(2)}, u32[]{:S(2)}) async-start(bf16[8,288,128]{2,1,0:T(8,128)(2,1)} %pick.1), calls=%async_computation.1 | async-start | bytes 1179648 | tf_op jit(solution)/shard_map/all_to_all | solution.py:319
  40.3 10.6 %all-to-all-done.1.rec_ref = bf16[8,288,128]{2,1,0:T(8,128)(2,1)S(1)} async-done(((bf16[8,288,128]{2,1,0:T(8,128)(2,1)}), bf16[8,288,128]{2,1,0:T(8,128)(2,1)S(1)}, u32[]{:S(2)}, u32[]{:S(2)}) %all-to-all-start.1) | async-done | bytes 589856 | tf_op jit(solution)/shard_map/all_to_all | solution.py:319
  50.9 0.8 copy-done
  51.7 11.1 %proto_pass.1 = (f32[16,256,128]{2,1,0:T(8,128)}, bf16[16,256,128]{2,1,0:T(8,128)(2,1)}, f32[256,128]{1,0:T(8,128)}) custom-call(s32[1]{0:T(128)} %bitcast.c_ref, bf16[8,288,128]{2,1,0:T(8,128)(2,1)} %copy-done, bf16[256,128]{1,0:T(8,128)(2,1)} %f_ref.3, bf16[256,128]{1,0:T(8,128)(2,1)} %tan_ref.5, f32[3,256,128]{2,1,0:T(8,128)} %get-tuple-element.14.st_ref, ...), custom_call_target="tpu_custom_call" | custom-call | flops 3221225472 | bytes 15728640 | tf_op jit(solution)/shard_map/proto_pass/pallas_call | solution.py:280
  63.0 2.8 %collective-permute-done = bf16[16,256,128]{2,1,0:T(8,128)(2,1)S(1)} collective-permute-done((bf16[16,256,128]{2,1,0:T(8,128)(2,1)}, bf16[16,256,128]{2,1,0:T(8,128)(2,1)S(1)}, u32[]{:S(2)}, u32[]{:S(2)}) %collective-permute-start) | collective-permute-done | bytes 1048608 | tf_op jit(solution)/shard_map/ppermute | solution.py:340
  65.8 1.8 convert_add_fusion
  67.7 2.1 %collective-permute-start.1 = (bf16[8,256,128]{2,1,0:T(8,128)(2,1)S(1)}, bf16[8,256,128]{2,1,0:T(8,128)(2,1)S(1)}, u32[]{:S(2)}, u32[]{:S(2)}) collective-permute-start(bf16[8,256,128]{2,1,0:T(8,128)(2,1)S(1)} %fusion.2), channel_id=1, source_target_pairs={{0,128},{8,136},{16,144},{24,152},{32,160},{40,168},{48,176},{56,1... | collective-permute-start | bytes 1572872 | tf_op jit(solution)/shard_map/ppermute | solution.py:344
  69.8 12.2 %collective-permute-done.1 = bf16[8,256,128]{2,1,0:T(8,128)(2,1)S(1)} collective-permute-done((bf16[8,256,128]{2,1,0:T(8,128)(2,1)S(1)}, bf16[8,256,128]{2,1,0:T(8,128)(2,1)S(1)}, u32[]{:S(2)}, u32[]{:S(2)}) %collective-permute-start.1) | collective-permute-done | bytes 524320 | tf_op jit(solution)/shard_map/ppermute | solution.py:344
  82.1 22.8 %all_to_all.40 = bf16[8,256,128]{2,1,0:T(8,128)(2,1)S(1)} all-to-all(bf16[8,256,128]{2,1,0:T(8,128)(2,1)S(1)} %fusion.1), channel_id=1, replica_groups={{0,16,32,48,64,80,96,112},{8,24,40,56,72,88,104,120},{128,144,160,176,1..., dimensions={0} | all-to-all | bytes 1048576 | tf_op jit(solution)/shard_map/all_to_all | solution.py:319
  105.1 18.5 %all_to_all.41 = bf16[8,256,128]{2,1,0:T(8,128)(2,1)S(1)} all-to-all(bf16[8,256,128]{2,1,0:T(8,128)(2,1)S(1)} %broadcast_in_dim.10), channel_id=1, replica_groups={{0,16,32,48,64,80,96,112},{8,24,40,56,72,88,104,120},{128,144,160,176,1..., dimensions={0} | all-to-all | bytes 1048576 | tf_op jit(solution)/shard_map/all_to_all | solution.py:319
  123.6 1.1 collective-permute-start.2
  124.7 9.3 %collective-permute-done.2 = bf16[8,256,128]{2,1,0:T(8,128)(2,1)S(1)} collective-permute-done((bf16[8,256,128]{2,1,0:T(8,128)(2,1)S(1)}, bf16[8,256,128]{2,1,0:T(8,128)(2,1)S(1)}, u32[]{:S(2)}, u32[]{:S(2)}) %collective-permute-start.2) | collective-permute-done | bytes 524320 | tf_op jit(solution)/shard_map/ppermute | solution.py:349
  134.2 11.4 %all_to_all.42 = f32[8,32,128]{2,1,0:T(8,128)S(1)} all-to-all(f32[8,32,128]{2,1,0:T(8,128)S(1)} %bitcast.31), channel_id=1, replica_groups=mesh['dp'=32,'proto'=8] {'proto'}, dimensions={0} | all-to-all | bytes 262144 | tf_op jit(solution)/shard_map/all_to_all | solution.py:319
  146.4 5.3 %all-to-all-start.3 = ((bf16[32,32,128]{2,1,0:T(8,128)(2,1)}), bf16[32,32,128]{2,1,0:T(8,128)(2,1)S(1)}, u32[]{:S(2)}, u32[]{:S(2)}) async-start(bf16[32,32,128]{2,1,0:T(8,128)(2,1)} %broadcast_in_dim.7), calls=%async_computation.3 | async-start | bytes 524288 | tf_op jit(solution)/shard_map/all_to_all | solution.py:319
  151.8 11.8 %all-to-all-done.3 = bf16[32,32,128]{2,1,0:T(8,128)(2,1)S(1)} async-done(((bf16[32,32,128]{2,1,0:T(8,128)(2,1)}), bf16[32,32,128]{2,1,0:T(8,128)(2,1)S(1)}, u32[]{:S(2)}, u32[]{:S(2)}) %all-to-all-start.3) | async-done | bytes 262176 | tf_op jit(solution)/shard_map/all_to_all | solution.py:319
  163.9 10.4 %all_to_all.43 = f32[8,32,128]{2,1,0:T(8,128)S(1)} all-to-all(f32[8,32,128]{2,1,0:T(8,128)S(1)} %bitcast.32), channel_id=1, replica_groups=mesh['dp'=32,'proto'=8] {'proto'}, dimensions={0} | all-to-all | bytes 262144 | tf_op jit(solution)/shard_map/all_to_all | solution.py:319
  175.0 3.4 %all-to-all-start.5 = ((bf16[8,32,128]{2,1,0:T(8,128)(2,1)}), bf16[8,32,128]{2,1,0:T(8,128)(2,1)S(1)}, u32[]{:S(2)}, u32[]{:S(2)}) async-start(bf16[8,32,128]{2,1,0:T(8,128)(2,1)} %broadcast_in_dim.8), calls=%async_computation.5 | async-start | bytes 131072 | tf_op jit(solution)/shard_map/all_to_all | solution.py:319
  178.4 7.7 %all-to-all-done.5 = bf16[8,32,128]{2,1,0:T(8,128)(2,1)S(1)} async-done(((bf16[8,32,128]{2,1,0:T(8,128)(2,1)}), bf16[8,32,128]{2,1,0:T(8,128)(2,1)S(1)}, u32[]{:S(2)}, u32[]{:S(2)}) %all-to-all-start.5) | async-done | bytes 65568 | tf_op jit(solution)/shard_map/all_to_all | solution.py:319
  186.1 1.5 maximum_select_fusion
  (25 shorter events, 4.7 us)
Async XLA Ops:
  0.6 15.5 %copy-start.3 = (s32[256]{0:T(256)S(1)}, s32[256]{0:T(256)}, u32[]{:S(2)}) copy-start(s32[256]{0:T(256)} %param.11) | copy-start | bytes 3076
  6.0 24.6 %all-to-all-start = ((bf16[32,48,128]{2,1,0:T(8,128)(2,1)}), bf16[32,48,128]{2,1,0:T(8,128)(2,1)S(1)}, u32[]{:S(2)}, u32[]{:S(2)}) async-start(bf16[32,48,128]{2,1,0:T(8,128)(2,1)} %get-tuple-element.13), calls=%async_computation | async-start | bytes 786432 | tf_op jit(solution)/shard_map/all_to_all | solution.py:319
  30.7 0.8 copy-start.1
  34.2 16.7 %all-to-all-start.1 = ((bf16[8,288,128]{2,1,0:T(8,128)(2,1)}), bf16[8,288,128]{2,1,0:T(8,128)(2,1)S(1)}, u32[]{:S(2)}, u32[]{:S(2)}) async-start(bf16[8,288,128]{2,1,0:T(8,128)(2,1)} %pick.1), calls=%async_computation.1 | async-start | bytes 1179648 | tf_op jit(solution)/shard_map/all_to_all | solution.py:319
  50.9 0.8 copy-start
  62.9 2.9 %collective-permute-start = (bf16[16,256,128]{2,1,0:T(8,128)(2,1)}, bf16[16,256,128]{2,1,0:T(8,128)(2,1)S(1)}, u32[]{:S(2)}, u32[]{:S(2)}) collective-permute-start(bf16[16,256,128]{2,1,0:T(8,128)(2,1)} %get-tuple-element.23), channel_id=1, source_target_pairs={{0,8},{8,0},{16,24},{24,16},{32,40},{40,32},{48,56},{56,48},{64,72... | collective-permute-start | bytes 3145736 | tf_op jit(solution)/shard_map/ppermute | solution.py:340
  67.7 14.3 %collective-permute-start.1 = (bf16[8,256,128]{2,1,0:T(8,128)(2,1)S(1)}, bf16[8,256,128]{2,1,0:T(8,128)(2,1)S(1)}, u32[]{:S(2)}, u32[]{:S(2)}) collective-permute-start(bf16[8,256,128]{2,1,0:T(8,128)(2,1)S(1)} %fusion.2), channel_id=1, source_target_pairs={{0,128},{8,136},{16,144},{24,152},{32,160},{40,168},{48,176},{56,1... | collective-permute-start | bytes 1572872 | tf_op jit(solution)/shard_map/ppermute | solution.py:344
  104.9 29.3 %copy-start.2 = (f32[256,128]{1,0:T(8,128)S(1)}, f32[256,128]{1,0:T(8,128)}, u32[]{:S(2)}) copy-start(f32[256,128]{1,0:T(8,128)} %get-tuple-element.21) | copy-start | bytes 393220
  105.1 58.5 %copy-start.4 = (f32[256,128]{1,0:T(8,128)S(1)}, f32[256,128]{1,0:T(8,128)}, u32[]{:S(2)}) copy-start(f32[256,128]{1,0:T(8,128)} %get-tuple-element.20) | copy-start | bytes 393220
  123.6 10.4 %collective-permute-start.2 = (bf16[8,256,128]{2,1,0:T(8,128)(2,1)S(1)}, bf16[8,256,128]{2,1,0:T(8,128)(2,1)S(1)}, u32[]{:S(2)}, u32[]{:S(2)}) collective-permute-start(bf16[8,256,128]{2,1,0:T(8,128)(2,1)S(1)} %all_to_all.41), channel_id=1, source_target_pairs={{0,128},{8,136},{16,144},{24,152},{32,160},{40,168},{48,176},{56,1... | collective-permute-start | bytes 1572872 | tf_op jit(solution)/shard_map/ppermute | solution.py:349
  134.1 51.9 %collective-permute-start.3 = (bf16[16,256,128]{2,1,0:T(8,128)(2,1)S(1)}, bf16[16,256,128]{2,1,0:T(8,128)(2,1)S(1)}, u32[]{:S(2)}, u32[]{:S(2)}) collective-permute-start(bf16[16,256,128]{2,1,0:T(8,128)(2,1)S(1)} %bitcast.23), channel_id=1, source_target_pairs={{0,8},{8,0},{16,24},{24,16},{32,40},{40,32},{48,56},{56,48},{64,72... | collective-permute-start | bytes 3145736 | tf_op jit(solution)/shard_map/ppermute | solution.py:351
  146.4 17.1 %all-to-all-start.3 = ((bf16[32,32,128]{2,1,0:T(8,128)(2,1)}), bf16[32,32,128]{2,1,0:T(8,128)(2,1)S(1)}, u32[]{:S(2)}, u32[]{:S(2)}) async-start(bf16[32,32,128]{2,1,0:T(8,128)(2,1)} %broadcast_in_dim.7), calls=%async_computation.3 | async-start | bytes 524288 | tf_op jit(solution)/shard_map/all_to_all | solution.py:319
  175.0 11.0 %all-to-all-start.5 = ((bf16[8,32,128]{2,1,0:T(8,128)(2,1)}), bf16[8,32,128]{2,1,0:T(8,128)(2,1)S(1)}, u32[]{:S(2)}, u32[]{:S(2)}) async-start(bf16[8,32,128]{2,1,0:T(8,128)(2,1)} %broadcast_in_dim.8), calls=%async_computation.5 | async-start | bytes 131072 | tf_op jit(solution)/shard_map/all_to_all | solution.py:319

commit v2 on v1

v2 whole, which is shorter than its diff:
```python
import jax
import jax.numpy as jnp
from jax import lax
from jax.experimental import pallas as pl
from jax.experimental.pallas import tpu as pltpu
from jax.sharding import PartitionSpec as P

F32 = jnp.float32
BF16 = jnp.bfloat16
NT = (((1,), (1,)), ((), ()))
TN = (((0,), (0,)), ((), ()))
D = 128
ROWS = 256
LOCAL = 8192
DP = 32
PR = 8
SUB = ROWS // PR
CN = 2048
NCH = LOCAL // CN
SCALE = 0.1
RG = 16
INV = 10.0
LOG2E = 1.4426950408889634
VMEM = pl.BlockSpec(memory_space=pltpu.VMEM)
SMEM = pl.BlockSpec(memory_space=pltpu.SMEM)
GRANT = 56 * 1024 * 1024


def split3(x):
    hi = x.astype(BF16).astype(F32)
    mid = (x - hi).astype(BF16).astype(F32)
    lo = (x - hi - mid).astype(BF16).astype(F32)
    return hi, mid, lo


def mass_kernel(q_ref, codes_ref, tan_ref, blk_ref, acc):
    step = pl.program_id(0)

    @pl.when(step == 0)
    def _():
        acc[...] = jnp.zeros_like(acc)

    for g in range(ROWS // RG):
        rows = slice(g * RG, (g + 1) * RG)
        x = codes_ref[rows, :].astype(F32)
        total = x[:, :D]
        for k in range(1, CN // D):
            total = total + x[:, k * D : (k + 1) * D]
        acc[rows, :] += total

    @pl.when(step == NCH - 1)
    def _():
        mass = jnp.sum(jnp.transpose(acc[...]), axis=0, keepdims=True)
        hi, mid, lo = split3(mass)
        parts = jnp.concatenate([hi, mid, lo, jnp.zeros((5, ROWS), F32)], axis=0)
        parts = jnp.concatenate([parts[:, :D], parts[:, D:]], axis=0).astype(BF16)
        rows = tan_ref[pl.ds(pl.multiple_of(q_ref[0] * SUB, SUB), SUB), :]
        block = jnp.concatenate([rows, parts], axis=0)
        for i in range(DP):
            blk_ref[i] = block


def mass_pass(q, codes, tan):
    return pl.pallas_call(
        mass_kernel,
        grid=(NCH,),
        in_specs=[
            SMEM,
            pl.BlockSpec((ROWS, CN), lambda c: (0, c)),
            pl.BlockSpec((ROWS, D), lambda c: (0, 0)),
        ],
        out_specs=pl.BlockSpec((DP, SUB + 16, D), lambda c: (0, 0, 0)),
        out_shape=jax.ShapeDtypeStruct((DP, SUB + 16, D), BF16),
        scratch_shapes=[pltpu.VMEM((ROWS, D), F32)],
        cost_estimate=pl.CostEstimate(flops=ROWS * LOCAL, bytes_accessed=5 << 20, transcendentals=0),
        name="mass_pass",
    )(q, codes, tan)


def h_kernel(codes_ref, pert_ref, h_ref, acc):
    step = pl.program_id(0)

    @pl.when(step == 0)
    def _():
        acc[...] = jnp.zeros_like(acc)

    acc[...] += jnp.dot(codes_ref[...], pert_ref[...], preferred_element_type=F32)

    @pl.when(step == NCH - 1)
    def _():
        h_ref[...] = acc[...].astype(BF16)


def h_pass(codes, pert):
    return pl.pallas_call(
        h_kernel,
        grid=(NCH,),
        in_specs=[
            pl.BlockSpec((ROWS, CN), lambda c: (0, c)),
            pl.BlockSpec((CN, D), lambda c: (c, 0)),
        ],
        out_specs=pl.BlockSpec((ROWS, D), lambda c: (0, 0)),
        out_shape=jax.ShapeDtypeStruct((ROWS, D), BF16),
        scratch_shapes=[pltpu.VMEM((ROWS, D), F32)],
        cost_estimate=pl.CostEstimate(flops=2 * ROWS * LOCAL * D * 2, bytes_accessed=7 << 20, transcendentals=0),
        name="h_pass",
    )(codes, pert)


def score_kernel(f_ref, tan_ref, a_ref, p_ref, e_ref, u_ref, cst_ref, st_ref, s_sc, t_sc, run):
    step = pl.program_id(0)
    f = f_ref[...]
    s_sc[...] = lax.dot_general(f, a_ref[...], NT, preferred_element_type=F32)
    left = jnp.concatenate([tan_ref[...], f], axis=1)
    right = jnp.concatenate([a_ref[...], p_ref[...]], axis=1)
    t_sc[...] = lax.dot_general(left, right, NT, preferred_element_type=F32)

    @pl.when(step == 0)
    def _():
        run[0] = jnp.full((ROWS, D), -jnp.inf, F32)
        run[1] = jnp.zeros((ROWS, D), F32)
        run[2] = jnp.zeros((ROWS, D), F32)

    lane = lax.broadcasted_iota(jnp.int32, (RG, D), 1)
    for g in range(ROWS // RG):
        rows = slice(g * RG, (g + 1) * RG)
        s = s_sc[rows, :]
        t = t_sc[rows, :]
        top = jnp.max(s, axis=1, keepdims=True)
        e = jnp.exp2((s - top) * (INV * LOG2E))
        z = jnp.sum(e, axis=1, keepdims=True)
        et = jnp.sum(e * t, axis=1, keepdims=True)
        mean = et / z
        e_ref[rows, :] = e.astype(BF16)
        u_ref[rows, :] = (e * (t - mean)).astype(BF16)
        top = top * INV
        cst_ref[0, rows, :] = jnp.where(lane == 0, top, mean * INV)
        old = run[0, rows, :]
        new = jnp.maximum(old, top)
        alpha = jnp.exp(old - new)
        beta = jnp.exp(top - new)
        z_run = run[1, rows, :] * alpha + beta * z
        et_run = run[2, rows, :] * alpha + beta * (et * INV)
        run[0, rows, :] = new
        run[1, rows, :] = z_run
        run[2, rows, :] = et_run
        st_ref[rows, :] = jnp.where(lane == 0, new, jnp.where(lane == 1, z_run, et_run))


def score_pass(f, tan, a, p):
    return pl.pallas_call(
        score_kernel,
        grid=(NCH,),
        in_specs=[
            pl.BlockSpec((ROWS, D), lambda c: (0, 0)),
            pl.BlockSpec((ROWS, D), lambda c: (0, 0)),
            pl.BlockSpec((CN, D), lambda c: (c, 0)),
            pl.BlockSpec((CN, D), lambda c: (c, 0)),
        ],
        out_specs=[
            pl.BlockSpec((ROWS, CN), lambda c: (0, c)),
            pl.BlockSpec((ROWS, CN), lambda c: (0, c)),
            pl.BlockSpec((1, ROWS, D), lambda c: (c, 0, 0)),
            pl.BlockSpec((ROWS, D), lambda c: (0, 0)),
        ],
        out_shape=[
            jax.ShapeDtypeStruct((ROWS, LOCAL), BF16),
            jax.ShapeDtypeStruct((ROWS, LOCAL), BF16),
            jax.ShapeDtypeStruct((NCH, ROWS, D), F32),
            jax.ShapeDtypeStruct((ROWS, D), F32),
        ],
        scratch_shapes=[
            pltpu.VMEM((ROWS, CN), F32),
            pltpu.VMEM((ROWS, CN), F32),
            pltpu.VMEM((3, ROWS, D), F32),
        ],
        cost_estimate=pl.CostEstimate(flops=10 * ROWS * LOCAL * D * 2, bytes_accessed=12 << 20, transcendentals=ROWS * LOCAL),
        name="score_pass",
    )(f, tan, a, p)


def embed_kernel(e_ref, u_ref, a_ref, p_ref, cst_ref, st_ref, x_ref, w_ref):
    @pl.when(pl.program_id(0) == 0)
    def _():
        x_ref[...] = jnp.zeros_like(x_ref)
        w_ref[...] = jnp.zeros_like(w_ref)

    e = e_ref[...]
    both = jnp.dot(e, jnp.concatenate([a_ref[...], p_ref[...]], axis=1), preferred_element_type=F32)
    ua = jnp.dot(u_ref[...], a_ref[...], preferred_element_type=F32)
    ea = both[:, :D]
    beta = jnp.exp(cst_ref[0, :, 0:1] - st_ref[:, 0:1])
    mean = cst_ref[0, :, 1:2]
    x_ref[...] += beta * (INV * ua + both[:, D:] + mean * ea)
    w_ref[...] += beta * ea


def embed_pass(e, u, a, p, cst, st):
    return pl.pallas_call(
        embed_kernel,
        grid=(NCH,),
        in_specs=[
            pl.BlockSpec((ROWS, CN), lambda c: (0, c)),
            pl.BlockSpec((ROWS, CN), lambda c: (0, c)),
            pl.BlockSpec((CN, D), lambda c: (c, 0)),
            pl.BlockSpec((CN, D), lambda c: (c, 0)),
            pl.BlockSpec((1, ROWS, D), lambda c: (c, 0, 0)),
            pl.BlockSpec((ROWS, D), lambda c: (0, 0)),
        ],
        out_specs=[
            pl.BlockSpec((ROWS, D), lambda c: (0, 0)),
            pl.BlockSpec((ROWS, D), lambda c: (0, 0)),
        ],
        out_shape=[jax.ShapeDtypeStruct((ROWS, D), F32)] * 2,
        cost_estimate=pl.CostEstimate(flops=6 * ROWS * LOCAL * D * 2, bytes_accessed=12 << 20, transcendentals=0),
        name="embed_pass",
    )(e, u, a, p, cst, st)


STAT = 16
PAY = ROWS + 2 * STAT + SUB


def pick_kernel(q_ref, tab_ref, part_ref, st_ref, h_ref, pay_ref):
    q = q_ref[0]
    partner = part_ref[...]
    group = partner // ROWS
    row = partner % ROWS
    mine = (row // SUB) == q
    column = jnp.where(mine, group * SUB + row % SUB, -1)
    hot = (lax.broadcasted_iota(jnp.int32, (ROWS, DP * SUB), 1) == column).astype(F32).astype(BF16)
    table = tab_ref[:, :SUB, :].reshape(DP * SUB, D)
    rows = jnp.dot(hot, table, preferred_element_type=F32).astype(BF16)

    hot_group = (lax.broadcasted_iota(jnp.int32, (ROWS, DP), 1) == group).astype(F32).astype(BF16)
    mass_rows = tab_ref[:, SUB:, :].astype(F32)
    mass = jnp.zeros((ROWS, ROWS), F32)
    for k in (2, 1, 0):
        piece = jnp.concatenate([mass_rows[:, k, :], mass_rows[:, 8 + k, :]], axis=1).astype(BF16)
        mass = mass + jnp.dot(hot_group, piece, preferred_element_type=F32)
    here = lax.broadcasted_iota(jnp.int32, (ROWS, ROWS), 1) == row
    mass = jnp.sum(jnp.where(here, mass, 0.0), axis=1, keepdims=True)

    lane = lax.broadcasted_iota(jnp.int32, (ROWS, D), 1)
    stats = jnp.where(lane == 3, mass, st_ref[...])
    flat = jnp.transpose(stats)[:4, :]
    hi, mid, lo = split3(flat)
    flat = jnp.concatenate([hi, mid, lo, jnp.zeros((STAT - 12, ROWS), F32)], axis=0)
    flat = jnp.concatenate([flat[:, :D], flat[:, D:]], axis=0).astype(BF16)
    payload = jnp.concatenate([rows, flat], axis=0)
    for i in range(PR):
        pay_ref[i, : ROWS + 2 * STAT, :] = payload
        pay_ref[i, ROWS + 2 * STAT :, :] = h_ref[i * SUB : (i + 1) * SUB, :]


def pick(q, tab, partner, st, h):
    return pl.pallas_call(
        pick_kernel,
        in_specs=[SMEM, VMEM, VMEM, VMEM, VMEM],
        out_specs=VMEM,
        out_shape=jax.ShapeDtypeStruct((PR, PAY, D), BF16),
        name="pick",
    )(q, tab, partner, st, h)


def stats_kernel(rec_ref, f_ref, tan_ref, st_ref, cst_ref, f12_ref, swt_ref, gst_ref, h_ref):
    total = jnp.zeros((ROWS, D), F32)
    h = jnp.zeros((SUB, D), F32)
    flats = []
    for i in range(PR):
        total = total + rec_ref[i, :ROWS, :].astype(F32)
        flat = rec_ref[i, ROWS : ROWS + 2 * STAT, :].astype(F32)
        flat = jnp.concatenate([flat[:STAT], flat[STAT:]], axis=1)
        flats.append((flat[0:4] + flat[4:8]) + flat[8:12])
        h = h + rec_ref[i, ROWS + 2 * STAT :, :].astype(F32)
    swt_ref[...] = (total * SCALE).astype(BF16)
    h_ref[...] = h.astype(BF16)
    top = flats[0][0:1]
    for i in range(1, PR):
        top = jnp.maximum(top, flats[i][0:1])
    z = jnp.zeros((1, ROWS), F32)
    et = jnp.zeros((1, ROWS), F32)
    mass = jnp.zeros((1, ROWS), F32)
    for i in range(PR):
        shift = jnp.exp(flats[i][0:1] - top)
        z = z + shift * flats[i][1:2]
        et = et + shift * flats[i][2:3]
        mass = mass + flats[i][3:4]
    rows = jnp.concatenate([top, et / z, SCALE * mass / z, jnp.zeros((D - 3, ROWS), F32)], axis=0)
    cols = jnp.transpose(rows)
    gst_ref[...] = cols
    top = cols[:, 0:1]
    mean = cols[:, 1:2]
    weight = cols[:, 2:3]
    f = f_ref[...].astype(F32)
    tan = tan_ref[...].astype(F32)
    for c in range(NCH):
        scale = weight * jnp.exp(cst_ref[c, :, 0:1] - top)
        f12_ref[c, :, :D] = (INV * scale * f).astype(BF16)
        f12_ref[c, :, D:] = (scale * ((cst_ref[c, :, 1:2] - mean) * f + tan)).astype(BF16)


def stats_pass(rec, f, tan, st, cst):
    return pl.pallas_call(
        stats_kernel,
        in_specs=[VMEM] * 5,
        out_specs=[VMEM] * 4,
        out_shape=[
            jax.ShapeDtypeStruct((NCH, ROWS, 2 * D), BF16),
            jax.ShapeDtypeStruct((ROWS, D), BF16),
            jax.ShapeDtypeStruct((ROWS, D), F32),
            jax.ShapeDtypeStruct((SUB, D), BF16),
        ],
        name="stats_pass",
    )(rec, f, tan, st, cst)


def proto_kernel(s_ref, f12_ref, swt_ref, u_ref, e_ref, codes_ref, mine_ref, send_ref):
    f12 = f12_ref[0]
    res = lax.dot_general(u_ref[...], f12[:, :D], TN, preferred_element_type=F32)
    res = res + lax.dot_general(e_ref[...], f12[:, D:], TN, preferred_element_type=F32)
    res = res - lax.dot_general(codes_ref[...], swt_ref[...], TN, preferred_element_type=F32)
    first = s_ref[0] == 0
    for b in range(CN // (2 * ROWS)):
        even = res[2 * b * ROWS : (2 * b + 1) * ROWS]
        odd = res[(2 * b + 1) * ROWS : (2 * b + 2) * ROWS]
        mine_ref[b] = jnp.where(first, even, odd)
        send_ref[b] = jnp.where(first, odd, even).astype(BF16)


def proto_pass(scalars, f12, swt, u, e, codes):
    nb = CN // (2 * ROWS)
    steps = NCH // 2
    wide = pl.BlockSpec((ROWS, CN), lambda c, s: (0, s[1] * steps + c))
    return pl.pallas_call(
        proto_kernel,
        grid_spec=pltpu.PrefetchScalarGridSpec(
            num_scalar_prefetch=1,
            grid=(steps,),
            in_specs=[
                pl.BlockSpec((1, ROWS, 2 * D), lambda c, s: (s[1] * steps + c, 0, 0)),
                pl.BlockSpec((ROWS, D), lambda c, s: (0, 0)),
                wide,
                wide,
                wide,
            ],
            out_specs=[
                pl.BlockSpec((nb, ROWS, D), lambda c, s: (c, 0, 0)),
                pl.BlockSpec((nb, ROWS, D), lambda c, s: (c, 0, 0)),
            ],
        ),
        out_shape=[
            jax.ShapeDtypeStruct((8, ROWS, D), F32),
            jax.ShapeDtypeStruct((8, ROWS, D), BF16),
        ],
        cost_estimate=pl.CostEstimate(flops=3 * ROWS * LOCAL * D * 2, bytes_accessed=9 << 20, transcendentals=0),
        name="proto_pass",
    )(scalars, f12, swt, u, e, codes)


HR = 4 * SUB


def final_kernel(s_ref, pieces_ref, part_ref, x_ref, w_ref, st_ref, gst_ref, out_ref, emb_ref):
    total = pieces_ref[0, :ROWS, :].astype(F32)
    for i in range(1, 8):
        total = total + pieces_ref[i, :ROWS, :].astype(F32)
    total = total.astype(BF16)
    for i in range(8):
        out_ref[i] = total
    q = s_ref[0]
    core = s_ref[1]
    y = s_ref[2]
    partner = part_ref[...]
    group = partner // ROWS
    row = partner % ROWS
    c_rel = jnp.where(group % 2 == core, 0, 1)
    y_rel = jnp.where(group // 16 == y, 0, 1)
    column = ((group // 2) % 8) * HR + (y_rel * 2 + c_rel) * SUB + row % SUB
    column = jnp.where((row // SUB) == q, column, -1)
    hot = (lax.broadcasted_iota(jnp.int32, (ROWS, 8 * HR), 1) == column).astype(F32).astype(BF16)
    table = pieces_ref[:, ROWS:, :].reshape(8 * HR, D)
    h = jnp.dot(hot, table, preferred_element_type=F32)
    scale = gst_ref[:, 2:3] * jnp.exp(st_ref[:, 0:1] - gst_ref[:, 0:1])
    emb_ref[...] = scale * (x_ref[...] - gst_ref[:, 1:2] * w_ref[...]) - SCALE * h


def final_pass(scalars, pieces, partner, x, w, st, gst):
    return pl.pallas_call(
        final_kernel,
        in_specs=[SMEM] + [VMEM] * 6,
        out_specs=[VMEM] * 2,
        out_shape=[jax.ShapeDtypeStruct((8, ROWS, D), BF16), jax.ShapeDtypeStruct((ROWS, D), F32)],
        name="final_pass",
    )(scalars, pieces, partner, x, w, st, gst)


CORE_PERM = [(i, i ^ 1) for i in range(DP)]
Y_PERM = [(i, i ^ 16) for i in range(DP)]
Z_GROUPS = [[y * 16 + z * 2 + c for z in range(8)] for y in range(2) for c in range(2)]


def exchange(x, axis, groups=None):
    return lax.all_to_all(x, axis, 0, 0, axis_index_groups=groups, tiled=True)


def swap(x, bit):
    return lax.ppermute(x, "proto", [(i, i ^ bit) for i in range(PR)])


def body(feature_matrix, tangent_embed, anchor_matrix, anchor_perturbation, codes, partner_lookup):
    dp = lax.axis_index("dp")
    q = lax.axis_index("proto")
    core = dp % 2
    y = dp // 16
    partner = partner_lookup.reshape(ROWS, 1)
    qs = q.reshape(1)

    block = mass_pass(qs, codes, tangent_embed)
    table = exchange(block, "dp")
    e, u, cst, st = score_pass(feature_matrix, tangent_embed, anchor_matrix, anchor_perturbation)
    h_part = h_pass(codes, anchor_perturbation)

    received = exchange(pick(qs, table, partner, st, h_part), "proto")
    x, w = embed_pass(e, u, anchor_matrix, anchor_perturbation, cst, st)
    f12, swt, gst, h_own = stats_pass(received, feature_matrix, tangent_embed, st, cst)

    mine_far, send_far = proto_pass(jnp.stack([core, 1 - y]), f12, swt, u, e, codes)
    got_far = lax.ppermute(send_far, "dp", CORE_PERM)
    h_pair = jnp.concatenate([h_own, lax.ppermute(h_own, "dp", CORE_PERM)], axis=0)
    to_y = (mine_far + got_far.astype(F32)).astype(BF16)
    from_far = lax.ppermute(to_y, "dp", Y_PERM)
    h_four = jnp.concatenate([h_pair, lax.ppermute(h_pair, "dp", Y_PERM)], axis=0)
    mine_near, send_near = proto_pass(jnp.stack([core, y]), f12, swt, u, e, codes)
    got_near = lax.ppermute(send_near, "dp", CORE_PERM)
    quarter = (mine_near + got_near.astype(F32) + from_far.astype(F32)).astype(BF16)
    quarter = jnp.concatenate([quarter, jnp.broadcast_to(h_four[None], (8, HR, D))], axis=1)
    pieces = exchange(quarter, "dp", Z_GROUPS)
    final, embed = final_pass(jnp.stack([q, core, y]), pieces, partner, x, w, st, gst)

    embed = embed + swap(embed, 4)
    along_z = exchange(final, "dp", Z_GROUPS)
    embed = embed + swap(embed, 2)
    from_y = lax.ppermute(along_z, "dp", Y_PERM)
    embed = embed + swap(embed, 1)
    own_core = lax.ppermute(along_z, "dp", CORE_PERM)
    far_core = lax.ppermute(from_y, "dp", CORE_PERM)
    own = jnp.where(core == 0, jnp.stack([along_z, own_core], 1), jnp.stack([own_core, along_z], 1))
    far = jnp.where(core == 0, jnp.stack([from_y, far_core], 1), jnp.stack([far_core, from_y], 1))
    hvp_proto = jnp.where(y == 0, jnp.stack([own, far]), jnp.stack([far, own])).reshape(LOCAL, D)
    return (embed.astype(BF16), hvp_proto)


def solution(mesh):
    in_specs = (
        P("dp", None),
        P("dp", None),
        P("proto", None),
        P("proto", None),
        P("dp", "proto"),
        P("dp"),
    )
    out_specs = (P("dp", None), P("proto", None))
    return jax.shard_map(body, mesh=mesh, in_specs=in_specs, out_specs=out_specs, check_vma=False)
```

time: 190 us -> 164 us (0.86)
  blocking collectives: 63.1 us -> 21.5 us
  Pallas kernels: 31.5 us -> 45.9 us
  waiting for transfers between devices: 55.9 us -> 53.4 us
  starting transfers between devices: 28.2 us -> 30.3 us
    all_to_all x4 -> x1, blocking collectives: 63.1 us -> 21.5 us  [exchange(): return lax.all_to_all(x, axis, 0, 0, axis_index_groups=groups, tiled=True)]
    pallas_call x3 -> x8, Pallas kernels: 19.3 us -> 37.1 us  [the longest x2 11.9 us: proto_pass(): pl.pallas_call(proto_kernel, grid_spec=pltpu.PrefetchScalarGridSpec(num_s...]
    ppermute x3 -> x10, waiting for transfers between devices: 15.1 us -> 23.2 us  [the longest x3 11 us: swap(): return lax.ppermute(x, 'proto', [(i, i ^ bit) for i in range(PR)])]
    all_to_all x4 -> x3, waiting for transfers between devices: 31.6 us -> 26.1 us  [exchange(): return lax.all_to_all(x, axis, 0, 0, axis_index_groups=groups, tiled=True)]
    ppermute x1, waiting for transfers between devices: 9.27 us -> 4 us  [body(): from_y = lax.ppermute(along_z, 'dp', Y_PERM)]
    ppermute x3 -> x10, starting transfers between devices: 2.25 us -> 6.44 us  [the longest x3 3.74 us: swap(): return lax.ppermute(x, 'proto', [(i, i ^ bit) for i in range(PR)])]
    pallas_call x1, Pallas kernels: 12.2 us -> 8.78 us  [score_pass(): pl.pallas_call(score_kernel, grid=(NCH,), in_specs=[pl.BlockSpec((ROWS, D...]
    all_to_all x4 -> x3, starting transfers between devices: 24.8 us -> 22.8 us  [exchange(): return lax.all_to_all(x, axis, 0, 0, axis_index_groups=groups, tiled=True)]
  transfers between devices with their start and end apart: 8 -> 14, of which waited for: 7 -> 9; matrix products, arithmetic and copies ran while one was open for 1% -> 2% of each run, Pallas kernels for 6% -> 17%
where the time goes in v2:
time: 164 us; the launch traced here: 161 us
  waiting for transfers between devices  53.4 us (33%)
  Pallas kernels  45.9 us (28%)
  starting transfers between devices  30.3 us (18%)
  blocking collectives  21.5 us (13%)
  local copies, waits for them, and re-layouts  4.83 us (3%)
  other arithmetic  4.67 us (3%)
    all_to_all x3, waiting for transfers between devices, exchange(): return lax.all_to_all(x, axis, 0, 0, axis_index_groups=groups, tiled=True)  26.1 us
    all_to_all x3, starting transfers between devices, exchange(): return lax.all_to_all(x, axis, 0, 0, axis_index_groups=groups, tiled=True)  22.8 us
    all_to_all x1, blocking collectives, exchange(): return lax.all_to_all(x, axis, 0, 0, axis_index_groups=groups, tiled=True)  21.5 us
    pallas_call x2, Pallas kernels, proto_pass(): pl.pallas_call(proto_kernel, grid_spec=pltpu.PrefetchScalarGridSpec(num_s...  11.9 us
    ppermute x3, waiting for transfers between devices, swap(): return lax.ppermute(x, 'proto', [(i, i ^ bit) for i in range(PR)])  11 us
    ppermute x1, waiting for transfers between devices, body(): lax.ppermute(h_pair, 'dp', Y_PERM)  11 us
    pallas_call x1, Pallas kernels, score_pass(): pl.pallas_call(score_kernel, grid=(NCH,), in_specs=[pl.BlockSpec((ROWS, D...  8.78 us
    pallas_call x1, Pallas kernels, embed_pass(): pl.pallas_call(embed_kernel, grid=(NCH,), in_specs=[pl.BlockSpec((ROWS, C...  7.56 us
  transfers between devices with their start and end apart: 14, of which 9 were waited for; matrix products, arithmetic and copies ran while one was open for 2% of the time, Pallas kernels for 17%

profile of v2, /device:TPU:8, one launch (start us, length us, event | category | flops | bytes accessed | tf_op | source)
XLA Modules:
  0.0 161.4 jit_solution(7718802301523944896)
XLA Ops:
  0.6 4.0 %mass_pass.1 = bf16[32,48,128]{2,1,0:T(8,128)(2,1)} custom-call(s32[1]{0:T(128)} %bitcast.q_ref, bf16[256,8192]{1,0:T(8,128)(2,1)} %codes_ref.7, bf16[256,128]{1,0:T(8,128)(2,1)} %tan_ref.5), custom_call_target="tpu_custom_call" | custom-call | flops 2097152 | bytes 5242880 | tf_op jit(solution)/shard_map/mass_pass/pallas_call | solution.py:64
  4.7 10.1 %all-to-all-start = ((bf16[32,48,128]{2,1,0:T(8,128)(2,1)}), bf16[32,48,128]{2,1,0:T(8,128)(2,1)S(1)}, u32[]{:S(2)}, u32[]{:S(2)}) async-start(bf16[32,48,128]{2,1,0:T(8,128)(2,1)} %mass_pass.1), calls=%async_computation | async-start | bytes 786432 | tf_op jit(solution)/shard_map/all_to_all | solution.py:404
  15.6 4.8 %h_pass.1.h_ref = bf16[256,128]{1,0:T(8,128)(2,1)} custom-call(bf16[256,8192]{1,0:T(8,128)(2,1)} %codes_ref.7, bf16[8192,128]{1,0:T(8,128)(2,1)} %p_ref.3), custom_call_target="tpu_custom_call" | custom-call | flops 1073741824 | bytes 7340032 | tf_op jit(solution)/shard_map/h_pass/pallas_call | solution.py:95
  20.4 8.8 %score_pass.1 = (bf16[256,8192]{1,0:T(8,128)(2,1)}, bf16[256,8192]{1,0:T(8,128)(2,1)}, f32[4,256,128]{2,1,0:T(8,128)}, f32[256,128]{1,0:T(8,128)}) custom-call(bf16[256,128]{1,0:T(8,128)(2,1)} %f_ref.3, bf16[256,128]{1,0:T(8,128)(2,1)} %tan_ref.5, bf16[8192,128]{1,0:T(8,128)(2,1)} %a_ref.3, bf16[8192,128]{1,0:T(8,128)(2,1)} %p_ref.3), custom_call_target="tpu_custom_call" | custom-call | flops 5368709120 | bytes 12582912 | tf_op jit(solution)/shard_map/score_pass/pallas_call | solution.py:151
  30.1 2.7 %pick.1 = bf16[8,320,128]{2,1,0:T(8,128)(2,1)} custom-call(s32[1]{0:T(128)} %bitcast.q_ref, bf16[32,48,128]{2,1,0:T(8,128)(2,1)} %copy-done.2, s32[256,1]{1,0:T(8,128)} %copy.8.part_ref, f32[256,128]{1,0:T(8,128)} %get-tuple-element.18.st_ref, bf16[256,128]{1,0:T(8,128)(2,1)} %h_pass.1.h_ref), custom_call_target="tpu_custom_call" | custom-call | tf_op jit(solution)/shard_map/pick/pallas_call | solution.py:257
  32.8 6.0 %all-to-all-start.1 = ((bf16[8,320,128]{2,1,0:T(8,128)(2,1)}), bf16[8,320,128]{2,1,0:T(8,128)(2,1)S(1)}, u32[]{:S(2)}, u32[]{:S(2)}) async-start(bf16[8,320,128]{2,1,0:T(8,128)(2,1)} %pick.1), calls=%async_computation.1 | async-start | bytes 1310720 | tf_op jit(solution)/shard_map/all_to_all | solution.py:404
  39.4 11.7 %all-to-all-done.1.rec_ref = bf16[8,320,128]{2,1,0:T(8,128)(2,1)S(1)} async-done(((bf16[8,320,128]{2,1,0:T(8,128)(2,1)}), bf16[8,320,128]{2,1,0:T(8,128)(2,1)S(1)}, u32[]{:S(2)}, u32[]{:S(2)}) %all-to-all-start.1) | async-done | bytes 655392 | tf_op jit(solution)/shard_map/all_to_all | solution.py:404
  51.9 3.2 %stats_pass.1 = (bf16[4,256,256]{2,1,0:T(8,128)(2,1)}, bf16[256,128]{1,0:T(8,128)(2,1)}, f32[256,128]{1,0:T(8,128)}, bf16[32,128]{1,0:T(8,128)(2,1)}) custom-call(bf16[8,320,128]{2,1,0:T(8,128)(2,1)} %copy-done.1, bf16[256,128]{1,0:T(8,128)(2,1)} %f_ref.3, bf16[256,128]{1,0:T(8,128)(2,1)} %tan_ref.5, f32[256,128]{1,0:T(8,128)} %get-tuple-element.18.st_ref, ...), custom_call_target="tpu_custom_call" | custom-call | tf_op jit(solution)/shard_map/stats_pass/pallas_call | solution.py:304
  55.1 5.9 %proto_pass.3 = (f32[8,256,128]{2,1,0:T(8,128)}, bf16[8,256,128]{2,1,0:T(8,128)(2,1)}) custom-call(s32[2]{0:T(128)} %get-tuple-element.35.s_ref, bf16[4,256,256]{2,1,0:T(8,128)(2,1)} %get-tuple-element.20.f12_ref, bf16[256,128]{1,0:T(8,128)(2,1)} %get-tuple-element.21.swt_ref, bf16[256,8192]{1,0:T(8,128)(2,1)} %get-tuple-element.22.u_ref, ...), custom_call_target="tpu_custom_call" | custom-call | flops 1610612736 | bytes 9437184 | tf_op jit(solution)/shard_map/proto_pass/pallas_call | solution.py:335
  61.0 6.0 %proto_pass.2 = (f32[8,256,128]{2,1,0:T(8,128)}, bf16[8,256,128]{2,1,0:T(8,128)(2,1)}) custom-call(s32[2]{0:T(128)} %get-tuple-element.34.s_ref, bf16[4,256,256]{2,1,0:T(8,128)(2,1)} %get-tuple-element.20.f12_ref, bf16[256,128]{1,0:T(8,128)(2,1)} %get-tuple-element.21.swt_ref, bf16[256,8192]{1,0:T(8,128)(2,1)} %get-tuple-element.22.u_ref, ...), custom_call_target="tpu_custom_call" | custom-call | flops 1610612736 | bytes 9437184 | tf_op jit(solution)/shard_map/proto_pass/pallas_call | solution.py:335
  67.7 1.4 collective-permute-start.2
  69.1 1.2 collective-permute-done.3
  71.0 11.0 %collective-permute-done.4 = bf16[64,128]{1,0:T(8,128)(2,1)S(1)} collective-permute-done((bf16[64,128]{1,0:T(8,128)(2,1)S(1)}, bf16[64,128]{1,0:T(8,128)(2,1)S(1)}, u32[]{:S(2)}, u32[]{:S(2)}) %collective-permute-start.4) | collective-permute-done | bytes 16416 | tf_op jit(solution)/shard_map/ppermute | solution.py:433
  83.2 6.6 %all-to-all-start.2 = ((bf16[8,384,128]{2,1,0:T(8,128)(2,1)}), bf16[8,384,128]{2,1,0:T(8,128)(2,1)S(1)}, u32[]{:S(2)}, u32[]{:S(2)}) async-start(bf16[8,384,128]{2,1,0:T(8,128)(2,1)} %pad_maximum_fusion), calls=%async_computation.2 | async-start | bytes 1572864 | tf_op jit(solution)/shard_map/all_to_all | solution.py:404
  90.4 7.6 %embed_pass.1 = (f32[256,128]{1,0:T(8,128)}, f32[256,128]{1,0:T(8,128)}) custom-call(bf16[256,8192]{1,0:T(8,128)(2,1)} %get-tuple-element.23.e_ref, bf16[256,8192]{1,0:T(8,128)(2,1)} %get-tuple-element.22.u_ref, bf16[8192,128]{1,0:T(8,128)(2,1)} %a_ref.3, bf16[8192,128]{1,0:T(8,128)(2,1)} %p_ref.3, f32[4,256,128]{2,1,0:T(8,128)} %get-tuple-element.19.cst_ref, ...), custom_call_target="tpu_custom_call" | custom-call | flops 3221225472 | bytes 12582912 | tf_op jit(solution)/shard_map/embed_pass/pallas_call | solution.py:199
  98.0 14.3 %all-to-all-done.2.pieces_ref = bf16[8,384,128]{2,1,0:T(8,128)(2,1)S(1)} async-done(((bf16[8,384,128]{2,1,0:T(8,128)(2,1)}), bf16[8,384,128]{2,1,0:T(8,128)(2,1)S(1)}, u32[]{:S(2)}, u32[]{:S(2)}) %all-to-all-start.2) | async-done | bytes 786464 | tf_op jit(solution)/shard_map/all_to_all | solution.py:404
  113.1 3.0 %final_pass.1 = (bf16[8,256,128]{2,1,0:T(8,128)(2,1)}, f32[256,128]{1,0:T(8,128)}) custom-call(s32[3]{0:T(128)} %pad_add_fusion.s_ref, bf16[8,384,128]{2,1,0:T(8,128)(2,1)} %copy-done, s32[256,1]{1,0:T(8,128)} %copy.8.part_ref, f32[256,128]{1,0:T(8,128)} %get-tuple-element.29.x_ref, f32[256,128]{1,0:T(8,128)} %get-tuple-element.30.w_ref, ...), custom_call_target="tpu_custom_call" | custom-call | tf_op jit(solution)/shard_map/final_pass/pallas_call | solution.py:389
  116.1 21.5 %all_to_all.20 = bf16[8,256,128]{2,1,0:T(8,128)(2,1)S(1)} all-to-all(bf16[8,256,128]{2,1,0:T(8,128)(2,1)} %get-tuple-element.33), channel_id=1, replica_groups={{0,16,32,48,64,80,96,112},{8,24,40,56,72,88,104,120},{128,144,160,176,1..., dimensions={0} | all-to-all | bytes 1048576 | tf_op jit(solution)/shard_map/all_to_all | solution.py:404
  138.8 1.8 %collective-permute-start.5 = (f32[256,128]{1,0:T(8,128)}, f32[256,128]{1,0:T(8,128)S(1)}, u32[]{:S(2)}, u32[]{:S(2)}) collective-permute-start(f32[256,128]{1,0:T(8,128)} %get-tuple-element.32), channel_id=1, source_target_pairs={{0,4},{1,5},{2,6},{3,7},{4,0},{5,1},{6,2},{7,3},{8,12},{9,13},{10,... | collective-permute-start | bytes 393224 | tf_op jit(solution)/shard_map/ppermute | solution.py:408
  140.6 4.9 %collective-permute-done.5 = f32[256,128]{1,0:T(8,128)S(1)} collective-permute-done((f32[256,128]{1,0:T(8,128)}, f32[256,128]{1,0:T(8,128)S(1)}, u32[]{:S(2)}, u32[]{:S(2)}) %collective-permute-start.5) | collective-permute-done | bytes 131104 | tf_op jit(solution)/shard_map/ppermute | solution.py:408
  147.0 4.0 %collective-permute-done.9 = bf16[8,256,128]{2,1,0:T(8,128)(2,1)S(1)} collective-permute-done((bf16[8,256,128]{2,1,0:T(8,128)(2,1)S(1)}, bf16[8,256,128]{2,1,0:T(8,128)(2,1)S(1)}, u32[]{:S(2)}, u32[]{:S(2)}) %collective-permute-start.9) | collective-permute-done | bytes 524320 | tf_op jit(solution)/shard_map/ppermute | solution.py:444
  151.5 1.4 collective-permute-start.7
  152.9 5.6 %collective-permute-done.7 = f32[256,128]{1,0:T(8,128)S(1)} collective-permute-done((f32[256,128]{1,0:T(8,128)S(1)}, f32[256,128]{1,0:T(8,128)S(1)}, u32[]{:S(2)}, u32[]{:S(2)}) %collective-permute-start.7) | collective-permute-done | bytes 131104 | tf_op jit(solution)/shard_map/ppermute | solution.py:408
  159.9 1.5 copy.10
  (44 shorter events, 11.7 us)
Async XLA Ops:
  0.6 14.1 %copy-start.6 = (s32[256]{0:T(256)S(1)}, s32[256]{0:T(256)}, u32[]{:S(2)}) copy-start(s32[256]{0:T(256)} %param.11) | copy-start | bytes 3076
  4.7 24.6 %all-to-all-start = ((bf16[32,48,128]{2,1,0:T(8,128)(2,1)}), bf16[32,48,128]{2,1,0:T(8,128)(2,1)S(1)}, u32[]{:S(2)}, u32[]{:S(2)}) async-start(bf16[32,48,128]{2,1,0:T(8,128)(2,1)} %mass_pass.1), calls=%async_computation | async-start | bytes 786432 | tf_op jit(solution)/shard_map/all_to_all | solution.py:404
  29.3 0.8 copy-start.2
  32.8 18.3 %all-to-all-start.1 = ((bf16[8,320,128]{2,1,0:T(8,128)(2,1)}), bf16[8,320,128]{2,1,0:T(8,128)(2,1)S(1)}, u32[]{:S(2)}, u32[]{:S(2)}) async-start(bf16[8,320,128]{2,1,0:T(8,128)(2,1)} %pick.1), calls=%async_computation.1 | async-start | bytes 1310720 | tf_op jit(solution)/shard_map/all_to_all | solution.py:404
  51.1 0.8 copy-start.1
  61.0 6.6 %collective-permute-start.1 = (bf16[8,256,128]{2,1,0:T(8,128)(2,1)}, bf16[8,256,128]{2,1,0:T(8,128)(2,1)S(1)}, u32[]{:S(2)}, u32[]{:S(2)}) collective-permute-start(bf16[8,256,128]{2,1,0:T(8,128)(2,1)} %get-tuple-element.27), channel_id=1, source_target_pairs={{0,8},{8,0},{16,24},{24,16},{32,40},{40,32},{48,56},{56,48},{64,72... | collective-permute-start | bytes 1572872 | tf_op jit(solution)/shard_map/ppermute | solution.py:429
  61.0 6.6 %copy-start.4 = (f32[8,256,128]{2,1,0:T(8,128)S(1)}, f32[8,256,128]{2,1,0:T(8,128)}, u32[]{:S(2)}) copy-start(f32[8,256,128]{2,1,0:T(8,128)} %get-tuple-element.26) | copy-start | bytes 3145732
  67.0 2.1 %copy-start.5 = (bf16[32,128]{1,0:T(8,128)(2,1)S(1)}, bf16[32,128]{1,0:T(8,128)(2,1)}, u32[]{:S(2)}) copy-start(bf16[32,128]{1,0:T(8,128)(2,1)} %get-tuple-element.28) | copy-start | bytes 24580
  67.0 15.0 %copy-start.3 = (f32[8,256,128]{2,1,0:T(8,128)S(1)}, f32[8,256,128]{2,1,0:T(8,128)}, u32[]{:S(2)}) copy-start(f32[8,256,128]{2,1,0:T(8,128)} %get-tuple-element.24) | copy-start | bytes 3145732
  67.0 15.0 %collective-permute-start = (bf16[8,256,128]{2,1,0:T(8,128)(2,1)}, bf16[8,256,128]{2,1,0:T(8,128)(2,1)S(1)}, u32[]{:S(2)}, u32[]{:S(2)}) collective-permute-start(bf16[8,256,128]{2,1,0:T(8,128)(2,1)} %get-tuple-element.25), channel_id=1, source_target_pairs={{0,8},{8,0},{16,24},{24,16},{32,40},{40,32},{48,56},{56,48},{64,72... | collective-permute-start | bytes 1572872 | tf_op jit(solution)/shard_map/ppermute | solution.py:435
  67.7 14.3 %collective-permute-start.2 = (bf16[8,256,128]{2,1,0:T(8,128)(2,1)S(1)}, bf16[8,256,128]{2,1,0:T(8,128)(2,1)S(1)}, u32[]{:S(2)}, u32[]{:S(2)}) collective-permute-start(bf16[8,256,128]{2,1,0:T(8,128)(2,1)S(1)} %add_convert_fusion.1), channel_id=1, source_target_pairs={{0,128},{8,136},{16,144},{24,152},{32,160},{40,168},{48,176},{56,1... | collective-permute-start | bytes 1572872 | tf_op jit(solution)/shard_map/ppermute | solution.py:432
  69.1 1.2 collective-permute-start.3
  70.2 11.7 %collective-permute-start.4 = (bf16[64,128]{1,0:T(8,128)(2,1)S(1)}, bf16[64,128]{1,0:T(8,128)(2,1)S(1)}, u32[]{:S(2)}, u32[]{:S(2)}) collective-permute-start(bf16[64,128]{1,0:T(8,128)(2,1)S(1)} %pad_maximum_fusion.2), channel_id=1, source_target_pairs={{0,128},{8,136},{16,144},{24,152},{32,160},{40,168},{48,176},{56,1... | collective-permute-start | bytes 49160 | tf_op jit(solution)/shard_map/ppermute | solution.py:433
  83.2 29.1 %all-to-all-start.2 = ((bf16[8,384,128]{2,1,0:T(8,128)(2,1)}), bf16[8,384,128]{2,1,0:T(8,128)(2,1)S(1)}, u32[]{:S(2)}, u32[]{:S(2)}) async-start(bf16[8,384,128]{2,1,0:T(8,128)(2,1)} %pad_maximum_fusion), calls=%async_computation.2 | async-start | bytes 1572864 | tf_op jit(solution)/shard_map/all_to_all | solution.py:404
  112.3 0.9 copy-start
  137.7 13.4 %collective-permute-start.9 = (bf16[8,256,128]{2,1,0:T(8,128)(2,1)S(1)}, bf16[8,256,128]{2,1,0:T(8,128)(2,1)S(1)}, u32[]{:S(2)}, u32[]{:S(2)}) collective-permute-start(bf16[8,256,128]{2,1,0:T(8,128)(2,1)S(1)} %all_to_all.20), channel_id=1, source_target_pairs={{0,128},{8,136},{16,144},{24,152},{32,160},{40,168},{48,176},{56,1... | collective-permute-start | bytes 1572872 | tf_op jit(solution)/shard_map/ppermute | solution.py:444
  138.8 6.7 %collective-permute-start.5 = (f32[256,128]{1,0:T(8,128)}, f32[256,128]{1,0:T(8,128)S(1)}, u32[]{:S(2)}, u32[]{:S(2)}) collective-permute-start(f32[256,128]{1,0:T(8,128)} %get-tuple-element.32), channel_id=1, source_target_pairs={{0,4},{1,5},{2,6},{3,7},{4,0},{5,1},{6,2},{7,3},{8,12},{9,13},{10,... | collective-permute-start | bytes 393224 | tf_op jit(solution)/shard_map/ppermute | solution.py:408
  140.6 18.6 %collective-permute-start.8 = (bf16[8,256,128]{2,1,0:T(8,128)(2,1)S(1)}, bf16[8,256,128]{2,1,0:T(8,128)(2,1)S(1)}, u32[]{:S(2)}, u32[]{:S(2)}) collective-permute-start(bf16[8,256,128]{2,1,0:T(8,128)(2,1)S(1)} %all_to_all.20), channel_id=1, source_target_pairs={{0,8},{8,0},{16,24},{24,16},{32,40},{40,32},{48,56},{56,48},{64,72... | collective-permute-start | bytes 1572872 | tf_op jit(solution)/shard_map/ppermute | solution.py:446
  146.4 5.1 %collective-permute-start.6 = (f32[256,128]{1,0:T(8,128)S(1)}, f32[256,128]{1,0:T(8,128)S(1)}, u32[]{:S(2)}, u32[]{:S(2)}) collective-permute-start(f32[256,128]{1,0:T(8,128)S(1)} %add.27), channel_id=1, source_target_pairs={{0,2},{1,3},{2,0},{3,1},{4,6},{5,7},{6,4},{7,5},{8,10},{9,11},{10,... | collective-permute-start | bytes 393224 | tf_op jit(solution)/shard_map/ppermute | solution.py:408
  151.0 8.4 %collective-permute-start.10 = (bf16[8,256,128]{2,1,0:T(8,128)(2,1)S(1)}, bf16[8,256,128]{2,1,0:T(8,128)(2,1)S(1)}, u32[]{:S(2)}, u32[]{:S(2)}) collective-permute-start(bf16[8,256,128]{2,1,0:T(8,128)(2,1)S(1)} %collective-permute-done.9), channel_id=1, source_target_pairs={{0,8},{8,0},{16,24},{24,16},{32,40},{40,32},{48,56},{56,48},{64,72... | collective-permute-start | bytes 1572872 | tf_op jit(solution)/shard_map/ppermute | solution.py:447
  151.5 7.0 %collective-permute-start.7 = (f32[256,128]{1,0:T(8,128)S(1)}, f32[256,128]{1,0:T(8,128)S(1)}, u32[]{:S(2)}, u32[]{:S(2)}) collective-permute-start(f32[256,128]{1,0:T(8,128)S(1)} %add.28), channel_id=1, source_target_pairs={{0,1},{1,0},{2,3},{3,2},{4,5},{5,4},{6,7},{7,6},{8,9},{9,8},{10,11... | collective-permute-start | bytes 393224 | tf_op jit(solution)/shard_map/ppermute | solution.py:408

commit v3 on v2

--- a/solution.py
+++ b/solution.py
@@ -4,6 +4,7 @@
 from jax.experimental import pallas as pl
 from jax.experimental.pallas import tpu as pltpu
 from jax.sharding import PartitionSpec as P
+
 
 F32 = jnp.float32
 BF16 = jnp.bfloat16
@@ -23,7 +24,7 @@
 LOG2E = 1.4426950408889634
 VMEM = pl.BlockSpec(memory_space=pltpu.VMEM)
 SMEM = pl.BlockSpec(memory_space=pltpu.SMEM)
-GRANT = 56 * 1024 * 1024
+MB = 1024 * 1024
 
 
 def split3(x):
@@ -73,6 +74,7 @@
         out_shape=jax.ShapeDtypeStruct((DP, SUB + 16, D), BF16),
         scratch_shapes=[pltpu.VMEM((ROWS, D), F32)],
         cost_estimate=pl.CostEstimate(flops=ROWS * LOCAL, bytes_accessed=5 << 20, transcendentals=0),
+        compiler_params=pltpu.CompilerParams(vmem_limit_bytes=56 * MB),
         name="mass_pass",
     )(q, codes, tan)
 
@@ -103,6 +105,7 @@
         out_shape=jax.ShapeDtypeStruct((ROWS, D), BF16),
         scratch_shapes=[pltpu.VMEM((ROWS, D), F32)],
         cost_estimate=pl.CostEstimate(flops=2 * ROWS * LOCAL * D * 2, bytes_accessed=7 << 20, transcendentals=0),
+        compiler_params=pltpu.CompilerParams(vmem_limit_bytes=56 * MB),
         name="h_pass",
     )(codes, pert)
 
@@ -175,6 +178,7 @@
             pltpu.VMEM((3, ROWS, D), F32),
         ],
         cost_estimate=pl.CostEstimate(flops=10 * ROWS * LOCAL * D * 2, bytes_accessed=12 << 20, transcendentals=ROWS * LOCAL),
+        compiler_params=pltpu.CompilerParams(vmem_limit_bytes=56 * MB),
         name="score_pass",
     )(f, tan, a, p)
 
@@ -213,6 +217,7 @@
         ],
         out_shape=[jax.ShapeDtypeStruct((ROWS, D), F32)] * 2,
         cost_estimate=pl.CostEstimate(flops=6 * ROWS * LOCAL * D * 2, bytes_accessed=12 << 20, transcendentals=0),
+        compiler_params=pltpu.CompilerParams(vmem_limit_bytes=56 * MB),
         name="embed_pass",
     )(e, u, a, p, cst, st)
 
@@ -259,6 +264,7 @@
         in_specs=[SMEM, VMEM, VMEM, VMEM, VMEM],
         out_specs=VMEM,
         out_shape=jax.ShapeDtypeStruct((PR, PAY, D), BF16),
+        compiler_params=pltpu.CompilerParams(vmem_limit_bytes=10 * MB),
         name="pick",
     )(q, tab, partner, st, h)
 
@@ -311,6 +317,7 @@
             jax.ShapeDtypeStruct((ROWS, D), F32),
             jax.ShapeDtypeStruct((SUB, D), BF16),
         ],
+        compiler_params=pltpu.CompilerParams(vmem_limit_bytes=10 * MB),
         name="stats_pass",
     )(rec, f, tan, st, cst)
 
@@ -354,20 +361,35 @@
             jax.ShapeDtypeStruct((8, ROWS, D), BF16),
         ],
         cost_estimate=pl.CostEstimate(flops=3 * ROWS * LOCAL * D * 2, bytes_accessed=9 << 20, transcendentals=0),
+        compiler_params=pltpu.CompilerParams(vmem_limit_bytes=56 * MB),
         name="proto_pass",
     )(scalars, f12, swt, u, e, codes)
 
 
-HR = 4 * SUB
-
-
-def final_kernel(s_ref, pieces_ref, part_ref, x_ref, w_ref, st_ref, gst_ref, out_ref, emb_ref):
-    total = pieces_ref[0, :ROWS, :].astype(F32)
+HR = 2 * SUB
+
+
+def final_kernel(pieces_ref, out_ref):
+    total = pieces_ref[0].astype(F32)
     for i in range(1, 8):
-        total = total + pieces_ref[i, :ROWS, :].astype(F32)
+        total = total + pieces_ref[i].astype(F32)
     total = total.astype(BF16)
     for i in range(8):
         out_ref[i] = total
+
+
+def final_pass(pieces):
+    return pl.pallas_call(
+        final_kernel,
+        in_specs=[VMEM],
+        out_specs=VMEM,
+        out_shape=jax.ShapeDtypeStruct((8, ROWS, D), BF16),
+        compiler_params=pltpu.CompilerParams(vmem_limit_bytes=8 * MB),
+        name="final_pass",
+    )(pieces)
+
+
+def row_kernel(s_ref, near_ref, far_ref, part_ref, x_ref, w_ref, st_ref, gst_ref, emb_ref):
     q = s_ref[0]
     core = s_ref[1]
     y = s_ref[2]
@@ -375,24 +397,26 @@
     group = partner // ROWS
     row = partner % ROWS
     c_rel = jnp.where(group % 2 == core, 0, 1)
-    y_rel = jnp.where(group // 16 == y, 0, 1)
-    column = ((group // 2) % 8) * HR + (y_rel * 2 + c_rel) * SUB + row % SUB
-    column = jnp.where((row // SUB) == q, column, -1)
-    hot = (lax.broadcasted_iota(jnp.int32, (ROWS, 8 * HR), 1) == column).astype(F32).astype(BF16)
-    table = pieces_ref[:, ROWS:, :].reshape(8 * HR, D)
-    h = jnp.dot(hot, table, preferred_element_type=F32)
+    column = ((group // 2) % 8) * HR + c_rel * SUB + row % SUB
+    mine = (row // SUB) == q
+    h = jnp.zeros((ROWS, D), F32)
+    for table_ref, side in ((near_ref, y), (far_ref, 1 - y)):
+        col = jnp.where(jnp.logical_and(mine, group // 16 == side), column, -1)
+        hot = (lax.broadcasted_iota(jnp.int32, (ROWS, 8 * HR), 1) == col).astype(F32).astype(BF16)
+        h = h + jnp.dot(hot, table_ref[...].reshape(8 * HR, D), preferred_element_type=F32)
     scale = gst_ref[:, 2:3] * jnp.exp(st_ref[:, 0:1] - gst_ref[:, 0:1])
     emb_ref[...] = scale * (x_ref[...] - gst_ref[:, 1:2] * w_ref[...]) - SCALE * h
 
 
-def final_pass(scalars, pieces, partner, x, w, st, gst):
-    return pl.pallas_call(
-        final_kernel,
-        in_specs=[SMEM] + [VMEM] * 6,
-        out_specs=[VMEM] * 2,
-        out_shape=[jax.ShapeDtypeStruct((8, ROWS, D), BF16), jax.ShapeDtypeStruct((ROWS, D), F32)],
-        name="final_pass",
-    )(scalars, pieces, partner, x, w, st, gst)
+def row_pass(scalars, near, far, partner, x, w, st, gst):
+    return pl.pallas_call(
+        row_kernel,
+        in_specs=[SMEM] + [VMEM] * 7,
+        out_specs=VMEM,
+        out_shape=jax.ShapeDtypeStruct((ROWS, D), F32),
+        compiler_params=pltpu.CompilerParams(vmem_limit_bytes=8 * MB),
+        name="row_pass",
+    )(scalars, near, far, partner, x, w, st, gst)
 
 
 CORE_PERM = [(i, i ^ 1) for i in range(DP)]
@@ -408,7 +432,7 @@
     return lax.ppermute(x, "proto", [(i, i ^ bit) for i in range(PR)])
 
 
-def body(feature_matrix, tangent_embed, anchor_matrix, anchor_perturbation, codes, partner_lookup):
+def inner(feature_matrix, tangent_embed, anchor_matrix, anchor_perturbation, codes, partner_lookup):
     dp = lax.axis_index("dp")
     q = lax.axis_index("proto")
     core = dp % 2
@@ -423,6 +447,7 @@
 
     received = exchange(pick(qs, table, partner, st, h_part), "proto")
     x, w = embed_pass(e, u, anchor_matrix, anchor_perturbation, cst, st)
+    received, x, w = lax.optimization_barrier((received, x, w))
     f12, swt, gst, h_own = stats_pass(received, feature_matrix, tangent_embed, st, cst)
 
     mine_far, send_far = proto_pass(jnp.stack([core, 1 - y]), f12, swt, u, e, codes)
@@ -430,18 +455,24 @@
     h_pair = jnp.concatenate([h_own, lax.ppermute(h_own, "dp", CORE_PERM)], axis=0)
     to_y = (mine_far + got_far.astype(F32)).astype(BF16)
     from_far = lax.ppermute(to_y, "dp", Y_PERM)
-    h_four = jnp.concatenate([h_pair, lax.ppermute(h_pair, "dp", Y_PERM)], axis=0)
+    f12, swt, to_y = lax.optimization_barrier((f12, swt, to_y))
     mine_near, send_near = proto_pass(jnp.stack([core, y]), f12, swt, u, e, codes)
     got_near = lax.ppermute(send_near, "dp", CORE_PERM)
+    h_pair, mine_near = lax.optimization_barrier((h_pair, mine_near))
+    h_near = exchange(jnp.broadcast_to(h_pair[None], (8, HR, D)), "dp", Z_GROUPS)
     quarter = (mine_near + got_near.astype(F32) + from_far.astype(F32)).astype(BF16)
-    quarter = jnp.concatenate([quarter, jnp.broadcast_to(h_four[None], (8, HR, D))], axis=1)
+    quarter, h_near = lax.optimization_barrier((quarter, h_near))
+    h_far = lax.ppermute(h_near, "dp", Y_PERM)
     pieces = exchange(quarter, "dp", Z_GROUPS)
-    final, embed = final_pass(jnp.stack([q, core, y]), pieces, partner, x, w, st, gst)
-
+    embed = row_pass(jnp.stack([q, core, y]), h_near, h_far, partner, x, w, st, gst)
     embed = embed + swap(embed, 4)
+    pieces, embed = lax.optimization_barrier((pieces, embed))
+    final = final_pass(pieces)
+
+    swapped = swap(embed, 2)
     along_z = exchange(final, "dp", Z_GROUPS)
-    embed = embed + swap(embed, 2)
     from_y = lax.ppermute(along_z, "dp", Y_PERM)
+    embed = embed + swapped
     embed = embed + swap(embed, 1)
     own_core = lax.ppermute(along_z, "dp", CORE_PERM)
     far_core = lax.ppermute(from_y, "dp", CORE_PERM)
@@ -461,4 +492,4 @@
         P("dp"),
     )
     out_specs = (P("dp", None), P("proto", None))
-    return jax.shard_map(body, mesh=mesh, in_specs=in_specs, out_specs=out_specs, check_vma=False)
+    return jax.shard_map(inner, mesh=mesh, in_specs=in_specs, out_specs=out_specs, check_vma=False)

time: 164 us -> 147 us (0.90)
  waiting for transfers between devices: 53.4 us -> 40.7 us
  Pallas kernels: 45.9 us -> 41.2 us
  starting transfers between devices: 30.3 us -> 33.7 us
  blocking collectives: 21.5 us -> 18.1 us
    all_to_all x3 -> x4, waiting for transfers between devices: 26.1 us -> 14.1 us  [exchange(): return lax.all_to_all(x, axis, 0, 0, axis_index_groups=groups, tiled=True)]
    all_to_all x1, blocking collectives: 21.5 us -> 18.1 us  [exchange(): return lax.all_to_all(x, axis, 0, 0, axis_index_groups=groups, tiled=True)]
    convert_element_type x3, other arithmetic: 0.93 us -> 4.16 us  [the longest x1 2.18 us: inner(): (mine_near + got_near.astype(F32) + from_far.astype(F32)).astype(BF16)]
    all_to_all x3 -> x4, starting transfers between devices: 22.8 us -> 25.7 us  [exchange(): return lax.all_to_all(x, axis, 0, 0, axis_index_groups=groups, tiled=True)]
    pallas_call x1, Pallas kernels: 3.16 us -> 1 us  [stats_pass(): pl.pallas_call(stats_kernel, in_specs=[VMEM] * 5, out_specs=[VMEM] * 4, o...]
    pallas_call x1 -> x2, Pallas kernels: 2.99 us -> 1.32 us  [the longest x1 1.25 us: row_pass(): pl.pallas_call(row_kernel, in_specs=[SMEM] + [VMEM] * 7, out_specs=VMEM,...]
  transfers between devices with their start and end apart: 14 -> 15, of which waited for: 9 -> 10; matrix products, arithmetic and copies ran while one was open for 2% -> 3% of each run, Pallas kernels for 17% -> 20%
where the time goes in v3:
time: 147 us; the launch traced here: 145 us
  Pallas kernels  41.2 us (28%)
  waiting for transfers between devices  40.7 us (28%)
  starting transfers between devices  33.7 us (23%)
  blocking collectives  18.1 us (12%)
  other arithmetic  5.63 us (4%)
  local copies, waits for them, and re-layouts  4.66 us (3%)
    all_to_all x4, starting transfers between devices, exchange(): return lax.all_to_all(x, axis, 0, 0, axis_index_groups=groups, tiled=True)  25.7 us
    all_to_all x1, blocking collectives, exchange(): return lax.all_to_all(x, axis, 0, 0, axis_index_groups=groups, tiled=True)  18.1 us
    all_to_all x4, waiting for transfers between devices, exchange(): return lax.all_to_all(x, axis, 0, 0, axis_index_groups=groups, tiled=True)  14.1 us
    pallas_call x2, Pallas kernels, proto_pass(): pl.pallas_call(proto_kernel, grid_spec=pltpu.PrefetchScalarGridSpec(num_s...  11.7 us
    ppermute x3, waiting for transfers between devices, swap(): return lax.ppermute(x, 'proto', [(i, i ^ bit) for i in range(PR)])  11 us
    pallas_call x1, Pallas kernels, score_pass(): pl.pallas_call(score_kernel, grid=(NCH,), in_specs=[pl.BlockSpec((ROWS, D...  8.75 us
    pallas_call x1, Pallas kernels, embed_pass(): pl.pallas_call(embed_kernel, grid=(NCH,), in_specs=[pl.BlockSpec((ROWS, C...  7.93 us
    ppermute x1, waiting for transfers between devices, inner(): from_y = lax.ppermute(along_z, 'dp', Y_PERM)  7.81 us
  transfers between devices with their start and end apart: 15, of which 10 were waited for; matrix products, arithmetic and copies ran while one was open for 3% of the time, Pallas kernels for 20%

profile of v3, /device:TPU:8, one launch (start us, length us, event | category | flops | bytes accessed | tf_op | source)
XLA Modules:
  0.0 144.8 jit_solution(6813098878760895486)
XLA Ops:
  0.6 4.0 %mass_pass.1 = bf16[32,48,128]{2,1,0:T(8,128)(2,1)} custom-call(s32[1]{0:T(128)} %bitcast.q_ref, bf16[256,8192]{1,0:T(8,128)(2,1)} %codes_ref.7, bf16[256,128]{1,0:T(8,128)(2,1)} %tan_ref.5), custom_call_target="tpu_custom_call" | custom-call | flops 2097152 | bytes 5242880 | tf_op jit(solution)/shard_map/mass_pass/pallas_call | solution.py:65
  4.7 10.1 %all-to-all-start = ((bf16[32,48,128]{2,1,0:T(8,128)(2,1)}), bf16[32,48,128]{2,1,0:T(8,128)(2,1)S(1)}, u32[]{:S(2)}, u32[]{:S(2)}) async-start(bf16[32,48,128]{2,1,0:T(8,128)(2,1)} %mass_pass.1), calls=%async_computation | async-start | bytes 786432 | tf_op jit(solution)/shard_map/all_to_all | solution.py:428
  14.9 4.8 %h_pass.1.h_ref = bf16[256,128]{1,0:T(8,128)(2,1)} custom-call(bf16[256,8192]{1,0:T(8,128)(2,1)} %codes_ref.7, bf16[8192,128]{1,0:T(8,128)(2,1)} %p_ref.3), custom_call_target="tpu_custom_call" | custom-call | flops 1073741824 | bytes 7340032 | tf_op jit(solution)/shard_map/h_pass/pallas_call | solution.py:97
  19.8 8.8 %score_pass.1 = (bf16[256,8192]{1,0:T(8,128)(2,1)}, bf16[256,8192]{1,0:T(8,128)(2,1)}, f32[4,256,128]{2,1,0:T(8,128)}, f32[256,128]{1,0:T(8,128)}) custom-call(bf16[256,128]{1,0:T(8,128)(2,1)} %f_ref.3, bf16[256,128]{1,0:T(8,128)(2,1)} %tan_ref.5, bf16[8192,128]{1,0:T(8,128)(2,1)} %a_ref.3, bf16[8192,128]{1,0:T(8,128)(2,1)} %p_ref.3), custom_call_target="tpu_custom_call" | custom-call | flops 5368709120 | bytes 12582912 | tf_op jit(solution)/shard_map/score_pass/pallas_call | solution.py:154
  30.2 1.6 %pick.1 = bf16[8,320,128]{2,1,0:T(8,128)(2,1)} custom-call(s32[1]{0:T(128)} %bitcast.q_ref, bf16[32,48,128]{2,1,0:T(8,128)(2,1)S(1)} %all-to-all-done.tab_ref, s32[256,1]{1,0:T(8,128)S(1)} %copy.8.part_ref, f32[256,128]{1,0:T(8,128)S(1)} %copy-done, bf16[256,128]{1,0:T(8,128)(2,1)S(1)} %copy-done.6), custom_call_target="tpu_custom_call" | custom-call | tf_op jit(solution)/shard_map/pick/pallas_call | solution.py:262
  31.8 6.0 %all-to-all-start.1 = ((bf16[8,320,128]{2,1,0:T(8,128)(2,1)}), bf16[8,320,128]{2,1,0:T(8,128)(2,1)S(1)}, u32[]{:S(2)}, u32[]{:S(2)}) async-start(bf16[8,320,128]{2,1,0:T(8,128)(2,1)} %pick.1), calls=%async_computation.1 | async-start | bytes 1310720 | tf_op jit(solution)/shard_map/all_to_all | solution.py:428
  38.5 7.9 %embed_pass.1 = (f32[256,128]{1,0:T(8,128)}, f32[256,128]{1,0:T(8,128)}) custom-call(bf16[256,8192]{1,0:T(8,128)(2,1)} %get-tuple-element.28.e_ref, bf16[256,8192]{1,0:T(8,128)(2,1)} %get-tuple-element.29.u_ref, bf16[8192,128]{1,0:T(8,128)(2,1)} %a_ref.3, bf16[8192,128]{1,0:T(8,128)(2,1)} %p_ref.3, f32[4,256,128]{2,1,0:T(8,128)} %get-tuple-element.30.cst_ref, ...), custom_call_target="tpu_custom_call" | custom-call | flops 3221225472 | bytes 12582912 | tf_op jit(solution)/shard_map/embed_pass/pallas_call | solution.py:203
  46.5 3.0 %all-to-all-done.1.rec_ref = bf16[8,320,128]{2,1,0:T(8,128)(2,1)S(1)} async-done(((bf16[8,320,128]{2,1,0:T(8,128)(2,1)}), bf16[8,320,128]{2,1,0:T(8,128)(2,1)S(1)}, u32[]{:S(2)}, u32[]{:S(2)}) %all-to-all-start.1) | async-done | bytes 655392 | tf_op jit(solution)/shard_map/all_to_all | solution.py:428
  52.0 5.9 %proto_pass.2 = (f32[8,256,128]{2,1,0:T(8,128)}, bf16[8,256,128]{2,1,0:T(8,128)(2,1)}) custom-call(s32[2]{0:T(128)} %get-tuple-element.53.s_ref, bf16[4,256,256]{2,1,0:T(8,128)(2,1)} %copy-done.2, bf16[256,128]{1,0:T(8,128)(2,1)} %copy-done.4, bf16[256,8192]{1,0:T(8,128)(2,1)} %get-tuple-element.29.u_ref, bf16[256,8192]{1,0:T(8,128)(2,1)} %get-tuple-element.28.e_ref, ...), custom_call_target="tpu_custom_call" | custom-call | flops 1610612736 | bytes 9437184 | tf_op jit(solution)/shard_map/proto_pass/pallas_call | solution.py:342
  57.8 2.1 %collective-permute-done.1 = bf16[8,256,128]{2,1,0:T(8,128)(2,1)S(1)} collective-permute-done((bf16[8,256,128]{2,1,0:T(8,128)(2,1)}, bf16[8,256,128]{2,1,0:T(8,128)(2,1)S(1)}, u32[]{:S(2)}, u32[]{:S(2)}) %collective-permute-start.1) | collective-permute-done | bytes 524320 | tf_op jit(solution)/shard_map/ppermute | solution.py:454
  61.3 1.8 %collective-permute-start.3 = (bf16[8,256,128]{2,1,0:T(8,128)(2,1)S(1)}, bf16[8,256,128]{2,1,0:T(8,128)(2,1)S(1)}, u32[]{:S(2)}, u32[]{:S(2)}) collective-permute-start(bf16[8,256,128]{2,1,0:T(8,128)(2,1)S(1)} %add_convert_fusion.1), channel_id=1, source_target_pairs={{0,128},{8,136},{16,144},{24,152},{32,160},{40,168},{48,176},{56,1... | collective-permute-start | bytes 1572872 | tf_op jit(solution)/shard_map/ppermute | solution.py:457
  63.1 5.9 %proto_pass.3 = (f32[8,256,128]{2,1,0:T(8,128)}, bf16[8,256,128]{2,1,0:T(8,128)(2,1)}) custom-call(s32[2]{0:T(128)} %get-tuple-element.52.s_ref, bf16[4,256,256]{2,1,0:T(8,128)(2,1)} %copy-done.2, bf16[256,128]{1,0:T(8,128)(2,1)} %copy-done.4, bf16[256,8192]{1,0:T(8,128)(2,1)} %get-tuple-element.29.u_ref, bf16[256,8192]{1,0:T(8,128)(2,1)} %get-tuple-element.28.e_ref, ...), custom_call_target="tpu_custom_call" | custom-call | flops 1610612736 | bytes 9437184 | tf_op jit(solution)/shard_map/proto_pass/pallas_call | solution.py:342
  69.6 1.6 %collective-permute-done = bf16[32,128]{1,0:T(8,128)(2,1)S(1)} collective-permute-done((bf16[32,128]{1,0:T(8,128)(2,1)S(1)}, bf16[32,128]{1,0:T(8,128)(2,1)S(1)}, u32[]{:S(2)}, u32[]{:S(2)}) %collective-permute-start) | collective-permute-done | bytes 8224 | tf_op jit(solution)/shard_map/ppermute | solution.py:455
  71.9 6.1 %all-to-all-start.2 = ((bf16[8,64,128]{2,1,0:T(8,128)(2,1)}), bf16[8,64,128]{2,1,0:T(8,128)(2,1)S(1)}, u32[]{:S(2)}, u32[]{:S(2)}) async-start(bf16[8,64,128]{2,1,0:T(8,128)(2,1)} %broadcast_in_dim.2), calls=%async_computation.2 | async-start | bytes 262144 | tf_op jit(solution)/shard_map/all_to_all | solution.py:428
  78.0 2.2 %add_convert_fusion = bf16[8,256,128]{2,1,0:T(8,128)(2,1)} fusion(bf16[8,256,128]{2,1,0:T(8,128)(2,1)S(1)} %collective-permute-done.3, f32[8,256,128]{2,1,0:T(8,128)} %get-tuple-element.42, bf16[8,256,128]{2,1,0:T(8,128)(2,1)S(1)} %collective-permute-done.2), kind=kLoop, calls=%fused_computation.3 | loop fusion | flops 1310720 | bytes 2621440 | tf_op jit(solution)/shard_map/convert_element_type | solution.py:463
  80.1 7.2 %all-to-all-done.2.near_ref = bf16[8,64,128]{2,1,0:T(8,128)(2,1)S(1)} async-done(((bf16[8,64,128]{2,1,0:T(8,128)(2,1)}), bf16[8,64,128]{2,1,0:T(8,128)(2,1)S(1)}, u32[]{:S(2)}, u32[]{:S(2)}) %all-to-all-start.2) | async-done | bytes 131104 | tf_op jit(solution)/shard_map/all_to_all | solution.py:428
  87.3 3.5 %all-to-all-start.3 = ((bf16[8,256,128]{2,1,0:T(8,128)(2,1)}), bf16[8,256,128]{2,1,0:T(8,128)(2,1)S(1)}, u32[]{:S(2)}, u32[]{:S(2)}) async-start(bf16[8,256,128]{2,1,0:T(8,128)(2,1)} %add_convert_fusion), calls=%async_computation.3 | async-start | bytes 1048576 | tf_op jit(solution)/shard_map/all_to_all | solution.py:428
  91.8 4.1 %collective-permute-done.4.far_ref = bf16[8,64,128]{2,1,0:T(8,128)(2,1)S(1)} collective-permute-done((bf16[8,64,128]{2,1,0:T(8,128)(2,1)S(1)}, bf16[8,64,128]{2,1,0:T(8,128)(2,1)S(1)}, u32[]{:S(2)}, u32[]{:S(2)}) %collective-permute-start.4) | collective-permute-done | bytes 131104 | tf_op jit(solution)/shard_map/ppermute | solution.py:465
  97.1 2.0 %collective-permute-start.5 = (f32[256,128]{1,0:T(8,128)S(1)}, f32[256,128]{1,0:T(8,128)S(1)}, u32[]{:S(2)}, u32[]{:S(2)}) collective-permute-start(f32[256,128]{1,0:T(8,128)S(1)} %row_pass.1), channel_id=1, source_target_pairs={{0,4},{1,5},{2,6},{3,7},{4,0},{5,1},{6,2},{7,3},{8,12},{9,13},{10,... | collective-permute-start | bytes 393224 | tf_op jit(solution)/shard_map/ppermute | solution.py:432
  99.2 4.7 %collective-permute-done.5 = f32[256,128]{1,0:T(8,128)S(1)} collective-permute-done((f32[256,128]{1,0:T(8,128)S(1)}, f32[256,128]{1,0:T(8,128)S(1)}, u32[]{:S(2)}, u32[]{:S(2)}) %collective-permute-start.5) | collective-permute-done | bytes 131104 | tf_op jit(solution)/shard_map/ppermute | solution.py:432
  103.9 3.2 %all-to-all-done.3.pieces_ref = bf16[8,256,128]{2,1,0:T(8,128)(2,1)S(1)} async-done(((bf16[8,256,128]{2,1,0:T(8,128)(2,1)}), bf16[8,256,128]{2,1,0:T(8,128)(2,1)S(1)}, u32[]{:S(2)}, u32[]{:S(2)}) %all-to-all-start.3) | async-done | bytes 524320 | tf_op jit(solution)/shard_map/all_to_all | solution.py:428
  107.1 18.1 %all_to_all.25 = bf16[8,256,128]{2,1,0:T(8,128)(2,1)S(1)} all-to-all(bf16[8,256,128]{2,1,0:T(8,128)(2,1)S(1)} %final_pass.1), channel_id=1, replica_groups={{0,16,32,48,64,80,96,112},{8,24,40,56,72,88,104,120},{128,144,160,176,1..., dimensions={0} | all-to-all | bytes 1048576 | tf_op jit(solution)/shard_map/all_to_all | solution.py:428
  126.6 7.8 %collective-permute-done.9 = bf16[8,256,128]{2,1,0:T(8,128)(2,1)S(1)} collective-permute-done((bf16[8,256,128]{2,1,0:T(8,128)(2,1)S(1)}, bf16[8,256,128]{2,1,0:T(8,128)(2,1)S(1)}, u32[]{:S(2)}, u32[]{:S(2)}) %collective-permute-start.9) | collective-permute-done | bytes 524320 | tf_op jit(solution)/shard_map/ppermute | solution.py:474
  135.7 6.3 %collective-permute-done.7 = f32[256,128]{1,0:T(8,128)S(1)} collective-permute-done((f32[256,128]{1,0:T(8,128)S(1)}, f32[256,128]{1,0:T(8,128)S(1)}, u32[]{:S(2)}, u32[]{:S(2)}) %collective-permute-start.7) | collective-permute-done | bytes 131104 | tf_op jit(solution)/shard_map/ppermute | solution.py:432
  (53 shorter events, 15.4 us)
Async XLA Ops:
  0.6 14.1 %copy-start.10 = (s32[256]{0:T(256)S(1)}, s32[256]{0:T(256)}, u32[]{:S(2)}) copy-start(s32[256]{0:T(256)} %param.11) | copy-start | bytes 3076
  4.7 24.6 %all-to-all-start = ((bf16[32,48,128]{2,1,0:T(8,128)(2,1)}), bf16[32,48,128]{2,1,0:T(8,128)(2,1)S(1)}, u32[]{:S(2)}, u32[]{:S(2)}) async-start(bf16[32,48,128]{2,1,0:T(8,128)(2,1)} %mass_pass.1), calls=%async_computation | async-start | bytes 786432 | tf_op jit(solution)/shard_map/all_to_all | solution.py:428
  19.8 9.6 %copy-start.6 = (bf16[256,128]{1,0:T(8,128)(2,1)S(1)}, bf16[256,128]{1,0:T(8,128)(2,1)}, u32[]{:S(2)}) copy-start(bf16[256,128]{1,0:T(8,128)(2,1)} %h_pass.1.h_ref) | copy-start | bytes 196612
  29.3 0.9 copy-start
  31.8 17.6 %all-to-all-start.1 = ((bf16[8,320,128]{2,1,0:T(8,128)(2,1)}), bf16[8,320,128]{2,1,0:T(8,128)(2,1)S(1)}, u32[]{:S(2)}, u32[]{:S(2)}) async-start(bf16[8,320,128]{2,1,0:T(8,128)(2,1)} %pick.1), calls=%async_computation.1 | async-start | bytes 1310720 | tf_op jit(solution)/shard_map/all_to_all | solution.py:428
  38.5 10.9 %copy-start.1 = (f32[256,128]{1,0:T(8,128)S(1)}, f32[256,128]{1,0:T(8,128)}, u32[]{:S(2)}) copy-start(f32[256,128]{1,0:T(8,128)} %get-tuple-element.27.st_ref) | copy-start | bytes 393220
  38.5 10.9 %copy-start.3 = (f32[4,256,128]{2,1,0:T(8,128)S(1)}, f32[4,256,128]{2,1,0:T(8,128)}, u32[]{:S(2)}) copy-start(f32[4,256,128]{2,1,0:T(8,128)} %get-tuple-element.30.cst_ref) | copy-start | bytes 1572868
  38.5 10.9 %copy-start.5 = (bf16[256,128]{1,0:T(8,128)(2,1)S(1)}, bf16[256,128]{1,0:T(8,128)(2,1)}, u32[]{:S(2)}) copy-start(bf16[256,128]{1,0:T(8,128)(2,1)} %tan_ref.5) | copy-start | bytes 196612
  38.5 10.9 %copy-start.9 = (bf16[256,128]{1,0:T(8,128)(2,1)S(1)}, bf16[256,128]{1,0:T(8,128)(2,1)}, u32[]{:S(2)}) copy-start(bf16[256,128]{1,0:T(8,128)(2,1)} %f_ref.3) | copy-start | bytes 196612
  57.8 2.1 %collective-permute-start.1 = (bf16[8,256,128]{2,1,0:T(8,128)(2,1)}, bf16[8,256,128]{2,1,0:T(8,128)(2,1)S(1)}, u32[]{:S(2)}, u32[]{:S(2)}) collective-permute-start(bf16[8,256,128]{2,1,0:T(8,128)(2,1)} %get-tuple-element.38), channel_id=1, source_target_pairs={{0,8},{8,0},{16,24},{24,16},{32,40},{40,32},{48,56},{56,48},{64,72... | collective-permute-start | bytes 1572872 | tf_op jit(solution)/shard_map/ppermute | solution.py:454
  61.3 16.7 %collective-permute-start.3 = (bf16[8,256,128]{2,1,0:T(8,128)(2,1)S(1)}, bf16[8,256,128]{2,1,0:T(8,128)(2,1)S(1)}, u32[]{:S(2)}, u32[]{:S(2)}) collective-permute-start(bf16[8,256,128]{2,1,0:T(8,128)(2,1)S(1)} %add_convert_fusion.1), channel_id=1, source_target_pairs={{0,128},{8,136},{16,144},{24,152},{32,160},{40,168},{48,176},{56,1... | collective-permute-start | bytes 1572872 | tf_op jit(solution)/shard_map/ppermute | solution.py:457
  69.0 26.9 %copy-start.7 = (f32[256,128]{1,0:T(8,128)S(1)}, f32[256,128]{1,0:T(8,128)}, u32[]{:S(2)}) copy-start(f32[256,128]{1,0:T(8,128)} %get-tuple-element.47.x_ref) | copy-start | bytes 393220
  69.0 26.9 %copy-start.8 = (f32[256,128]{1,0:T(8,128)S(1)}, f32[256,128]{1,0:T(8,128)}, u32[]{:S(2)}) copy-start(f32[256,128]{1,0:T(8,128)} %get-tuple-element.48.w_ref) | copy-start | bytes 393220
  69.0 9.0 %collective-permute-start.2 = (bf16[8,256,128]{2,1,0:T(8,128)(2,1)}, bf16[8,256,128]{2,1,0:T(8,128)(2,1)S(1)}, u32[]{:S(2)}, u32[]{:S(2)}) collective-permute-start(bf16[8,256,128]{2,1,0:T(8,128)(2,1)} %get-tuple-element.43), channel_id=1, source_target_pairs={{0,8},{8,0},{16,24},{24,16},{32,40},{40,32},{48,56},{56,48},{64,72... | collective-permute-start | bytes 1572872 | tf_op jit(solution)/shard_map/ppermute | solution.py:460
  69.1 2.1 %collective-permute-start = (bf16[32,128]{1,0:T(8,128)(2,1)S(1)}, bf16[32,128]{1,0:T(8,128)(2,1)S(1)}, u32[]{:S(2)}, u32[]{:S(2)}) collective-permute-start(bf16[32,128]{1,0:T(8,128)(2,1)S(1)} %get-tuple-element.34), channel_id=1, source_target_pairs={{0,8},{8,0},{16,24},{24,16},{32,40},{40,32},{48,56},{56,48},{64,72... | collective-permute-start | bytes 24584 | tf_op jit(solution)/shard_map/ppermute | solution.py:455
  71.9 15.4 %all-to-all-start.2 = ((bf16[8,64,128]{2,1,0:T(8,128)(2,1)}), bf16[8,64,128]{2,1,0:T(8,128)(2,1)S(1)}, u32[]{:S(2)}, u32[]{:S(2)}) async-start(bf16[8,64,128]{2,1,0:T(8,128)(2,1)} %broadcast_in_dim.2), calls=%async_computation.2 | async-start | bytes 262144 | tf_op jit(solution)/shard_map/all_to_all | solution.py:428
  87.3 19.7 %all-to-all-start.3 = ((bf16[8,256,128]{2,1,0:T(8,128)(2,1)}), bf16[8,256,128]{2,1,0:T(8,128)(2,1)S(1)}, u32[]{:S(2)}, u32[]{:S(2)}) async-start(bf16[8,256,128]{2,1,0:T(8,128)(2,1)} %add_convert_fusion), calls=%async_computation.3 | async-start | bytes 1048576 | tf_op jit(solution)/shard_map/all_to_all | solution.py:428
  90.8 5.1 %collective-permute-start.4 = (bf16[8,64,128]{2,1,0:T(8,128)(2,1)S(1)}, bf16[8,64,128]{2,1,0:T(8,128)(2,1)S(1)}, u32[]{:S(2)}, u32[]{:S(2)}) collective-permute-start(bf16[8,64,128]{2,1,0:T(8,128)(2,1)S(1)} %all-to-all-done.2.near_ref), channel_id=1, source_target_pairs={{0,128},{8,136},{16,144},{24,152},{32,160},{40,168},{48,176},{56,1... | collective-permute-start | bytes 393224 | tf_op jit(solution)/shard_map/ppermute | solution.py:465
  97.1 6.7 %collective-permute-start.5 = (f32[256,128]{1,0:T(8,128)S(1)}, f32[256,128]{1,0:T(8,128)S(1)}, u32[]{:S(2)}, u32[]{:S(2)}) collective-permute-start(f32[256,128]{1,0:T(8,128)S(1)} %row_pass.1), channel_id=1, source_target_pairs={{0,4},{1,5},{2,6},{3,7},{4,0},{5,1},{6,2},{7,3},{8,12},{9,13},{10,... | collective-permute-start | bytes 393224 | tf_op jit(solution)/shard_map/ppermute | solution.py:432
  125.2 9.2 %collective-permute-start.9 = (bf16[8,256,128]{2,1,0:T(8,128)(2,1)S(1)}, bf16[8,256,128]{2,1,0:T(8,128)(2,1)S(1)}, u32[]{:S(2)}, u32[]{:S(2)}) collective-permute-start(bf16[8,256,128]{2,1,0:T(8,128)(2,1)S(1)} %all_to_all.25), channel_id=1, source_target_pairs={{0,128},{8,136},{16,144},{24,152},{32,160},{40,168},{48,176},{56,1... | collective-permute-start | bytes 1572872 | tf_op jit(solution)/shard_map/ppermute | solution.py:474
  126.1 16.5 %collective-permute-start.8 = (bf16[8,256,128]{2,1,0:T(8,128)(2,1)S(1)}, bf16[8,256,128]{2,1,0:T(8,128)(2,1)S(1)}, u32[]{:S(2)}, u32[]{:S(2)}) collective-permute-start(bf16[8,256,128]{2,1,0:T(8,128)(2,1)S(1)} %all_to_all.25), channel_id=1, source_target_pairs={{0,8},{8,0},{16,24},{24,16},{32,40},{40,32},{48,56},{56,48},{64,72... | collective-permute-start | bytes 1572872 | tf_op jit(solution)/shard_map/ppermute | solution.py:477
  126.1 8.3 %collective-permute-start.6 = (f32[256,128]{1,0:T(8,128)S(1)}, f32[256,128]{1,0:T(8,128)S(1)}, u32[]{:S(2)}, u32[]{:S(2)}) collective-permute-start(f32[256,128]{1,0:T(8,128)S(1)} %add.27), channel_id=1, source_target_pairs={{0,2},{1,3},{2,0},{3,1},{4,6},{5,7},{6,4},{7,5},{8,10},{9,11},{10,... | collective-permute-start | bytes 393224 | tf_op jit(solution)/shard_map/ppermute | solution.py:432
  134.4 8.4 %collective-permute-start.10 = (bf16[8,256,128]{2,1,0:T(8,128)(2,1)S(1)}, bf16[8,256,128]{2,1,0:T(8,128)(2,1)S(1)}, u32[]{:S(2)}, u32[]{:S(2)}) collective-permute-start(bf16[8,256,128]{2,1,0:T(8,128)(2,1)S(1)} %collective-permute-done.9), channel_id=1, source_target_pairs={{0,8},{8,0},{16,24},{24,16},{32,40},{40,32},{48,56},{56,48},{64,72... | collective-permute-start | bytes 1572872 | tf_op jit(solution)/shard_map/ppermute | solution.py:478
  134.5 7.5 %collective-permute-start.7 = (f32[256,128]{1,0:T(8,128)S(1)}, f32[256,128]{1,0:T(8,128)S(1)}, u32[]{:S(2)}, u32[]{:S(2)}) collective-permute-start(f32[256,128]{1,0:T(8,128)S(1)} %add.28), channel_id=1, source_target_pairs={{0,1},{1,0},{2,3},{3,2},{4,5},{5,4},{6,7},{7,6},{8,9},{9,8},{10,11... | collective-permute-start | bytes 393224 | tf_op jit(solution)/shard_map/ppermute | solution.py:432
  (2 other events, 1.5 us)

commit v4 on v3

--- a/solution.py
+++ b/solution.py
@@ -79,38 +79,7 @@
     )(q, codes, tan)
 
 
-def h_kernel(codes_ref, pert_ref, h_ref, acc):
-    step = pl.program_id(0)
-
-    @pl.when(step == 0)
-    def _():
-        acc[...] = jnp.zeros_like(acc)
-
-    acc[...] += jnp.dot(codes_ref[...], pert_ref[...], preferred_element_type=F32)
-
-    @pl.when(step == NCH - 1)
-    def _():
-        h_ref[...] = acc[...].astype(BF16)
-
-
-def h_pass(codes, pert):
-    return pl.pallas_call(
-        h_kernel,
-        grid=(NCH,),
-        in_specs=[
-            pl.BlockSpec((ROWS, CN), lambda c: (0, c)),
-            pl.BlockSpec((CN, D), lambda c: (c, 0)),
-        ],
-        out_specs=pl.BlockSpec((ROWS, D), lambda c: (0, 0)),
-        out_shape=jax.ShapeDtypeStruct((ROWS, D), BF16),
-        scratch_shapes=[pltpu.VMEM((ROWS, D), F32)],
-        cost_estimate=pl.CostEstimate(flops=2 * ROWS * LOCAL * D * 2, bytes_accessed=7 << 20, transcendentals=0),
-        compiler_params=pltpu.CompilerParams(vmem_limit_bytes=56 * MB),
-        name="h_pass",
-    )(codes, pert)
-
-
-def score_kernel(f_ref, tan_ref, a_ref, p_ref, e_ref, u_ref, cst_ref, st_ref, s_sc, t_sc, run):
+def score_kernel(f_ref, tan_ref, a_ref, p_ref, codes_ref, e_ref, u_ref, cst_ref, st_ref, h_ref, s_sc, t_sc, run, acc):
     step = pl.program_id(0)
     f = f_ref[...]
     s_sc[...] = lax.dot_general(f, a_ref[...], NT, preferred_element_type=F32)
@@ -123,7 +92,10 @@
         run[0] = jnp.full((ROWS, D), -jnp.inf, F32)
         run[1] = jnp.zeros((ROWS, D), F32)
         run[2] = jnp.zeros((ROWS, D), F32)
-
+        acc[...] = jnp.zeros_like(acc)
+
+    acc[...] += jnp.dot(codes_ref[...], p_ref[...], preferred_element_type=F32)
+    h_ref[...] = acc[...].astype(BF16)
     lane = lax.broadcasted_iota(jnp.int32, (RG, D), 1)
     for g in range(ROWS // RG):
         rows = slice(g * RG, (g + 1) * RG)
@@ -150,7 +122,7 @@
         st_ref[rows, :] = jnp.where(lane == 0, new, jnp.where(lane == 1, z_run, et_run))
 
 
-def score_pass(f, tan, a, p):
+def score_pass(f, tan, a, p, codes):
     return pl.pallas_call(
         score_kernel,
         grid=(NCH,),
@@ -159,11 +131,13 @@
             pl.BlockSpec((ROWS, D), lambda c: (0, 0)),
             pl.BlockSpec((CN, D), lambda c: (c, 0)),
             pl.BlockSpec((CN, D), lambda c: (c, 0)),
+            pl.BlockSpec((ROWS, CN), lambda c: (0, c)),
         ],
         out_specs=[
             pl.BlockSpec((ROWS, CN), lambda c: (0, c)),
             pl.BlockSpec((ROWS, CN), lambda c: (0, c)),
             pl.BlockSpec((1, ROWS, D), lambda c: (c, 0, 0)),
+            pl.BlockSpec((ROWS, D), lambda c: (0, 0)),
             pl.BlockSpec((ROWS, D), lambda c: (0, 0)),
         ],
         out_shape=[
@@ -171,16 +145,18 @@
             jax.ShapeDtypeStruct((ROWS, LOCAL), BF16),
             jax.ShapeDtypeStruct((NCH, ROWS, D), F32),
             jax.ShapeDtypeStruct((ROWS, D), F32),
+            jax.ShapeDtypeStruct((ROWS, D), BF16),
         ],
         scratch_shapes=[
             pltpu.VMEM((ROWS, CN), F32),
             pltpu.VMEM((ROWS, CN), F32),
             pltpu.VMEM((3, ROWS, D), F32),
+            pltpu.VMEM((ROWS, D), F32),
         ],
         cost_estimate=pl.CostEstimate(flops=10 * ROWS * LOCAL * D * 2, bytes_accessed=12 << 20, transcendentals=ROWS * LOCAL),
         compiler_params=pltpu.CompilerParams(vmem_limit_bytes=56 * MB),
         name="score_pass",
-    )(f, tan, a, p)
+    )(f, tan, a, p, codes)
 
 
 def embed_kernel(e_ref, u_ref, a_ref, p_ref, cst_ref, st_ref, x_ref, w_ref):
@@ -366,9 +342,6 @@
     )(scalars, f12, swt, u, e, codes)
 
 
-HR = 2 * SUB
-
-
 def final_kernel(pieces_ref, out_ref):
     total = pieces_ref[0].astype(F32)
     for i in range(1, 8):
@@ -389,26 +362,21 @@
     )(pieces)
 
 
-def row_kernel(s_ref, near_ref, far_ref, part_ref, x_ref, w_ref, st_ref, gst_ref, emb_ref):
+def row_kernel(s_ref, own_ref, other_ref, part_ref, x_ref, w_ref, st_ref, gst_ref, emb_ref):
     q = s_ref[0]
-    core = s_ref[1]
-    y = s_ref[2]
     partner = part_ref[...]
-    group = partner // ROWS
+    away = (partner // ROWS) ^ s_ref[1]
+    block = ((away >> 3) & 1) + 2 * ((away >> 2) & 1) + 4 * ((away >> 1) & 1) + 8 * ((away >> 4) & 1) + 16 * (away & 1)
     row = partner % ROWS
-    c_rel = jnp.where(group % 2 == core, 0, 1)
-    column = ((group // 2) % 8) * HR + c_rel * SUB + row % SUB
-    mine = (row // SUB) == q
-    h = jnp.zeros((ROWS, D), F32)
-    for table_ref, side in ((near_ref, y), (far_ref, 1 - y)):
-        col = jnp.where(jnp.logical_and(mine, group // 16 == side), column, -1)
-        hot = (lax.broadcasted_iota(jnp.int32, (ROWS, 8 * HR), 1) == col).astype(F32).astype(BF16)
-        h = h + jnp.dot(hot, table_ref[...].reshape(8 * HR, D), preferred_element_type=F32)
+    column = jnp.where((row // SUB) == q, block * SUB + row % SUB, -1)
+    hot = (lax.broadcasted_iota(jnp.int32, (ROWS, DP * SUB), 1) == column).astype(F32).astype(BF16)
+    table = jnp.concatenate([own_ref[...], other_ref[...]], axis=0)
+    h = jnp.dot(hot, table, preferred_element_type=F32)
     scale = gst_ref[:, 2:3] * jnp.exp(st_ref[:, 0:1] - gst_ref[:, 0:1])
     emb_ref[...] = scale * (x_ref[...] - gst_ref[:, 1:2] * w_ref[...]) - SCALE * h
 
 
-def row_pass(scalars, near, far, partner, x, w, st, gst):
+def row_pass(scalars, own, other, partner, x, w, st, gst):
     return pl.pallas_call(
         row_kernel,
         in_specs=[SMEM] + [VMEM] * 7,
@@ -416,7 +384,33 @@
         out_shape=jax.ShapeDtypeStruct((ROWS, D), F32),
         compiler_params=pltpu.CompilerParams(vmem_limit_bytes=8 * MB),
         name="row_pass",
-    )(scalars, near, far, partner, x, w, st, gst)
+    )(scalars, own, other, partner, x, w, st, gst)
+
+
+def place_kernel(s_ref, own_ref, other_ref, *refs):
+    out_ref, sems = refs[-2], refs[-1]
+    copies = [
+        pltpu.make_async_copy(own_ref, out_ref.at[s_ref[0], :, s_ref[1]], sems.at[0]),
+        pltpu.make_async_copy(other_ref, out_ref.at[s_ref[0], :, 1 - s_ref[1]], sems.at[1]),
+    ]
+    for copy in copies:
+        copy.start()
+    for copy in copies:
+        copy.wait()
+
+
+def place(scalars, own, other, whole):
+    rest = () if whole is None else (whole,)
+    return pl.pallas_call(
+        place_kernel,
+        in_specs=[SMEM, VMEM, VMEM] + [pl.BlockSpec(memory_space=pltpu.HBM)] * len(rest),
+        out_specs=pl.BlockSpec(memory_space=pltpu.HBM),
+        out_shape=jax.ShapeDtypeStruct((2, 8, 2, ROWS, D), BF16),
+        scratch_shapes=[pltpu.SemaphoreType.DMA((2,))],
+        input_output_aliases={3: 0} if rest else {},
+        compiler_params=pltpu.CompilerParams(vmem_limit_bytes=4 * MB),
+        name="place",
+    )(scalars, own, other, *rest)
 
 
 CORE_PERM = [(i, i ^ 1) for i in range(DP)]
@@ -426,6 +420,11 @@
 
 def exchange(x, axis, groups=None):
     return lax.all_to_all(x, axis, 0, 0, axis_index_groups=groups, tiled=True)
+
+
+def doubled(x, bit):
+    other = lax.ppermute(x, "dp", [(i, i ^ bit) for i in range(DP)])
+    return lax.optimization_barrier(jnp.concatenate([x, other], axis=0))
 
 
 def swap(x, bit):
@@ -442,8 +441,7 @@
 
     block = mass_pass(qs, codes, tangent_embed)
     table = exchange(block, "dp")
-    e, u, cst, st = score_pass(feature_matrix, tangent_embed, anchor_matrix, anchor_perturbation)
-    h_part = h_pass(codes, anchor_perturbation)
+    e, u, cst, st, h_part = score_pass(feature_matrix, tangent_embed, anchor_matrix, anchor_perturbation, codes)
 
     received = exchange(pick(qs, table, partner, st, h_part), "proto")
     x, w = embed_pass(e, u, anchor_matrix, anchor_perturbation, cst, st)
@@ -452,34 +450,34 @@
 
     mine_far, send_far = proto_pass(jnp.stack([core, 1 - y]), f12, swt, u, e, codes)
     got_far = lax.ppermute(send_far, "dp", CORE_PERM)
-    h_pair = jnp.concatenate([h_own, lax.ppermute(h_own, "dp", CORE_PERM)], axis=0)
     to_y = (mine_far + got_far.astype(F32)).astype(BF16)
     from_far = lax.ppermute(to_y, "dp", Y_PERM)
-    f12, swt, to_y = lax.optimization_barrier((f12, swt, to_y))
+    f12, swt, to_y, h_own = lax.optimization_barrier((f12, swt, to_y, h_own))
+    table = doubled(h_own, 8)
     mine_near, send_near = proto_pass(jnp.stack([core, y]), f12, swt, u, e, codes)
+    table = doubled(table, 4)
     got_near = lax.ppermute(send_near, "dp", CORE_PERM)
-    h_pair, mine_near = lax.optimization_barrier((h_pair, mine_near))
-    h_near = exchange(jnp.broadcast_to(h_pair[None], (8, HR, D)), "dp", Z_GROUPS)
+    table = doubled(table, 2)
     quarter = (mine_near + got_near.astype(F32) + from_far.astype(F32)).astype(BF16)
-    quarter, h_near = lax.optimization_barrier((quarter, h_near))
-    h_far = lax.ppermute(h_near, "dp", Y_PERM)
     pieces = exchange(quarter, "dp", Z_GROUPS)
-    embed = row_pass(jnp.stack([q, core, y]), h_near, h_far, partner, x, w, st, gst)
-    embed = embed + swap(embed, 4)
-    pieces, embed = lax.optimization_barrier((pieces, embed))
+    table = doubled(table, 16)
+    other = lax.ppermute(table, "dp", CORE_PERM)
+    embed = row_pass(jnp.stack([q, dp]), table, other, partner, x, w, st, gst)
     final = final_pass(pieces)
 
-    swapped = swap(embed, 2)
+    swapped = swap(embed, 4)
     along_z = exchange(final, "dp", Z_GROUPS)
     from_y = lax.ppermute(along_z, "dp", Y_PERM)
     embed = embed + swapped
-    embed = embed + swap(embed, 1)
+    swapped = swap(embed, 2)
+    embed = embed + swapped
+    swapped = swap(embed, 1)
+    hvp_embed = (embed + swapped).astype(BF16)
     own_core = lax.ppermute(along_z, "dp", CORE_PERM)
+    whole = place(jnp.stack([y, core]), along_z, own_core, None)
     far_core = lax.ppermute(from_y, "dp", CORE_PERM)
-    own = jnp.where(core == 0, jnp.stack([along_z, own_core], 1), jnp.stack([own_core, along_z], 1))
-    far = jnp.where(core == 0, jnp.stack([from_y, far_core], 1), jnp.stack([far_core, from_y], 1))
-    hvp_proto = jnp.where(y == 0, jnp.stack([own, far]), jnp.stack([far, own])).reshape(LOCAL, D)
-    return (embed.astype(BF16), hvp_proto)
+    whole = place(jnp.stack([1 - y, core]), from_y, far_core, whole)
+    return (hvp_embed, whole.reshape(LOCAL, D))
 
 
 def solution(mesh):

time: 147 us -> 167 us (1.14)
  waiting for transfers between devices: 40.7 us -> 59.2 us
  blocking collectives: 18.1 us -> 20.4 us
  starting transfers between devices: 33.7 us -> 35.8 us
    ppermute x2 -> x5, waiting for transfers between devices: 5.68 us -> 24.1 us  [the longest x4 22.9 us: doubled(): other = lax.ppermute(x, 'dp', [(i, i ^ bit) for i in range(DP)])]
    ppermute x1, waiting for transfers between devices: 0.01 us -> 12.5 us  [inner(): from_far = lax.ppermute(to_y, 'dp', Y_PERM)]
    ppermute x1, waiting for transfers between devices: 7.81 us -> 0.01 us  [inner(): from_y = lax.ppermute(along_z, 'dp', Y_PERM)]
    all_to_all x4 -> x3, waiting for transfers between devices: 14.1 us -> 6.83 us  [exchange(): return lax.all_to_all(x, axis, 0, 0, axis_index_groups=groups, tiled=True)]
    ppermute x2 -> x5, starting transfers between devices: 1.42 us -> 7.78 us  [the longest x4 7.69 us: doubled(): other = lax.ppermute(x, 'dp', [(i, i ^ bit) for i in range(DP)])]
    all_to_all x4 -> x3, starting transfers between devices: 25.7 us -> 19.6 us  [exchange(): return lax.all_to_all(x, axis, 0, 0, axis_index_groups=groups, tiled=True)]
    ppermute x3, waiting for transfers between devices: 11 us -> 13.7 us  [swap(): return lax.ppermute(x, 'proto', [(i, i ^ bit) for i in range(PR)])]
    all_to_all x1, blocking collectives: 18.1 us -> 20.4 us  [exchange(): return lax.all_to_all(x, axis, 0, 0, axis_index_groups=groups, tiled=True)]
  transfers between devices with their start and end apart: 15 -> 17, of which waited for: 10 -> 12; matrix products, arithmetic and copies ran while one was open for 3% -> 1% of each run, Pallas kernels for 20% -> 13%
where the time goes in v4:
time: 167 us; the launch traced here: 166 us
  waiting for transfers between devices  59.2 us (35%)
  Pallas kernels  41.6 us (25%)
  starting transfers between devices  35.8 us (21%)
  blocking collectives  20.4 us (12%)
  other arithmetic  4.27 us (3%)
  local copies, waits for them, and re-layouts  3.36 us (2%)
    ppermute x4, waiting for transfers between devices, doubled(): other = lax.ppermute(x, 'dp', [(i, i ^ bit) for i in range(DP)])  22.9 us
    all_to_all x1, blocking collectives, exchange(): return lax.all_to_all(x, axis, 0, 0, axis_index_groups=groups, tiled=True)  20.4 us
    all_to_all x3, starting transfers between devices, exchange(): return lax.all_to_all(x, axis, 0, 0, axis_index_groups=groups, tiled=True)  19.6 us
    ppermute x3, waiting for transfers between devices, swap(): return lax.ppermute(x, 'proto', [(i, i ^ bit) for i in range(PR)])  13.7 us
    ppermute x1, waiting for transfers between devices, inner(): from_far = lax.ppermute(to_y, 'dp', Y_PERM)  12.5 us
    pallas_call x2, Pallas kernels, proto_pass(): pl.pallas_call(proto_kernel, grid_spec=pltpu.PrefetchScalarGridSpec(num_s...  11.7 us
    pallas_call x1, Pallas kernels, score_pass(): pl.pallas_call(score_kernel, grid=(NCH,), in_specs=[pl.BlockSpec((ROWS, D...  10.2 us
    pallas_call x1, Pallas kernels, embed_pass(): pl.pallas_call(embed_kernel, grid=(NCH,), in_specs=[pl.BlockSpec((ROWS, C...  7.96 us
  transfers between devices with their start and end apart: 17, of which 12 were waited for; matrix products, arithmetic and copies ran while one was open for 1% of the time, Pallas kernels for 13%

profile of v4, /device:TPU:8, one launch (start us, length us, event | category | flops | bytes accessed | tf_op | source)
XLA Modules:
  0.0 165.7 jit_solution(10732479764737132020)
XLA Ops:
  0.6 4.0 %mass_pass.1 = bf16[32,48,128]{2,1,0:T(8,128)(2,1)} custom-call(s32[1]{0:T(128)} %bitcast.q_ref, bf16[256,8192]{1,0:T(8,128)(2,1)} %codes_ref.7, bf16[256,128]{1,0:T(8,128)(2,1)} %tan_ref.5), custom_call_target="tpu_custom_call" | custom-call | flops 2097152 | bytes 5242880 | tf_op jit(solution)/shard_map/mass_pass/pallas_call | solution.py:65
  4.7 10.1 %all-to-all-start = ((bf16[32,48,128]{2,1,0:T(8,128)(2,1)}), bf16[32,48,128]{2,1,0:T(8,128)(2,1)S(1)}, u32[]{:S(2)}, u32[]{:S(2)}) async-start(bf16[32,48,128]{2,1,0:T(8,128)(2,1)} %mass_pass.1), calls=%async_computation | async-start | bytes 786432 | tf_op jit(solution)/shard_map/all_to_all | solution.py:422
  14.9 10.2 %score_pass.1 = (bf16[256,8192]{1,0:T(8,128)(2,1)}, bf16[256,8192]{1,0:T(8,128)(2,1)}, f32[4,256,128]{2,1,0:T(8,128)}, f32[256,128]{1,0:T(8,128)}, bf16[256,128]{1,0:T(8,128)(2,1)}) custom-call(bf16[256,128]{1,0:T(8,128)(2,1)} %f_ref.3, bf16[256,128]{1,0:T(8,128)(2,1)} %tan_ref.5, bf16[8192,128]{1,0:T(8,128)(2,1)} %a_ref.3, bf16[8192,128]{1,0:T(8,128)(2,1)} %p_ref.3, ...), custom_call_target="tpu_custom_call" | custom-call | flops 5368709120 | bytes 12582912 | tf_op jit(solution)/shard_map/score_pass/pallas_call | solution.py:126
  25.2 4.1 %all-to-all-done.tab_ref = bf16[32,48,128]{2,1,0:T(8,128)(2,1)S(1)} async-done(((bf16[32,48,128]{2,1,0:T(8,128)(2,1)}), bf16[32,48,128]{2,1,0:T(8,128)(2,1)S(1)}, u32[]{:S(2)}, u32[]{:S(2)}) %all-to-all-start) | async-done | bytes 393248 | tf_op jit(solution)/shard_map/all_to_all | solution.py:422
  32.7 6.0 %all-to-all-start.1 = ((bf16[8,320,128]{2,1,0:T(8,128)(2,1)}), bf16[8,320,128]{2,1,0:T(8,128)(2,1)S(1)}, u32[]{:S(2)}, u32[]{:S(2)}) async-start(bf16[8,320,128]{2,1,0:T(8,128)(2,1)} %pick.1), calls=%async_computation.1 | async-start | bytes 1310720 | tf_op jit(solution)/shard_map/all_to_all | solution.py:422
  39.3 8.0 %embed_pass.1 = (f32[256,128]{1,0:T(8,128)}, f32[256,128]{1,0:T(8,128)}) custom-call(bf16[256,8192]{1,0:T(8,128)(2,1)} %get-tuple-element.25.e_ref, bf16[256,8192]{1,0:T(8,128)(2,1)} %get-tuple-element.26.u_ref, bf16[8192,128]{1,0:T(8,128)(2,1)} %a_ref.3, bf16[8192,128]{1,0:T(8,128)(2,1)} %p_ref.3, f32[4,256,128]{2,1,0:T(8,128)} %get-tuple-element.27.cst_ref, ...), custom_call_target="tpu_custom_call" | custom-call | flops 3221225472 | bytes 12582912 | tf_op jit(solution)/shard_map/embed_pass/pallas_call | solution.py:179
  47.3 2.7 %all-to-all-done.1.rec_ref = bf16[8,320,128]{2,1,0:T(8,128)(2,1)S(1)} async-done(((bf16[8,320,128]{2,1,0:T(8,128)(2,1)}), bf16[8,320,128]{2,1,0:T(8,128)(2,1)S(1)}, u32[]{:S(2)}, u32[]{:S(2)}) %all-to-all-start.1) | async-done | bytes 655392 | tf_op jit(solution)/shard_map/all_to_all | solution.py:422
  52.5 5.9 %proto_pass.2 = (f32[8,256,128]{2,1,0:T(8,128)}, bf16[8,256,128]{2,1,0:T(8,128)(2,1)}) custom-call(s32[2]{0:T(128)} %get-tuple-element.44.s_ref, bf16[4,256,256]{2,1,0:T(8,128)(2,1)} %copy-done.2, bf16[256,128]{1,0:T(8,128)(2,1)} %copy-done.4, bf16[256,8192]{1,0:T(8,128)(2,1)} %get-tuple-element.26.u_ref, bf16[256,8192]{1,0:T(8,128)(2,1)} %get-tuple-element.25.e_ref, ...), custom_call_target="tpu_custom_call" | custom-call | flops 1610612736 | bytes 9437184 | tf_op jit(solution)/shard_map/proto_pass/pallas_call | solution.py:318
  58.3 2.1 %collective-permute-done = bf16[8,256,128]{2,1,0:T(8,128)(2,1)S(1)} collective-permute-done((bf16[8,256,128]{2,1,0:T(8,128)(2,1)}, bf16[8,256,128]{2,1,0:T(8,128)(2,1)S(1)}, u32[]{:S(2)}, u32[]{:S(2)}) %collective-permute-start) | collective-permute-done | bytes 524320 | tf_op jit(solution)/shard_map/ppermute | solution.py:452
  61.8 5.9 %proto_pass.3 = (f32[8,256,128]{2,1,0:T(8,128)}, bf16[8,256,128]{2,1,0:T(8,128)(2,1)}) custom-call(s32[2]{0:T(128)} %get-tuple-element.45.s_ref, bf16[4,256,256]{2,1,0:T(8,128)(2,1)} %copy-done.2, bf16[256,128]{1,0:T(8,128)(2,1)} %copy-done.4, bf16[256,8192]{1,0:T(8,128)(2,1)} %get-tuple-element.26.u_ref, bf16[256,8192]{1,0:T(8,128)(2,1)} %get-tuple-element.25.e_ref, ...), custom_call_target="tpu_custom_call" | custom-call | flops 1610612736 | bytes 9437184 | tf_op jit(solution)/shard_map/proto_pass/pallas_call | solution.py:318
  67.8 2.0 %collective-permute-start.10 = (bf16[8,256,128]{2,1,0:T(8,128)(2,1)S(1)}, bf16[8,256,128]{2,1,0:T(8,128)(2,1)S(1)}, u32[]{:S(2)}, u32[]{:S(2)}) collective-permute-start(bf16[8,256,128]{2,1,0:T(8,128)(2,1)S(1)} %add_convert_fusion.1), channel_id=1, source_target_pairs={{0,128},{8,136},{16,144},{24,152},{32,160},{40,168},{48,176},{56,1... | collective-permute-start | bytes 1572872 | tf_op jit(solution)/shard_map/ppermute | solution.py:454
  69.8 12.5 %collective-permute-done.10 = bf16[8,256,128]{2,1,0:T(8,128)(2,1)S(1)} collective-permute-done((bf16[8,256,128]{2,1,0:T(8,128)(2,1)S(1)}, bf16[8,256,128]{2,1,0:T(8,128)(2,1)S(1)}, u32[]{:S(2)}, u32[]{:S(2)}) %collective-permute-start.10) | collective-permute-done | bytes 524320 | tf_op jit(solution)/shard_map/ppermute | solution.py:454
  83.7 20.4 %all_to_all.20.pieces_ref = bf16[8,256,128]{2,1,0:T(8,128)(2,1)S(1)} all-to-all(bf16[8,256,128]{2,1,0:T(8,128)(2,1)S(1)} %add_convert_fusion), channel_id=1, replica_groups={{0,16,32,48,64,80,96,112},{8,24,40,56,72,88,104,120},{128,144,160,176,1..., dimensions={0} | all-to-all | bytes 1048576 | tf_op jit(solution)/shard_map/all_to_all | solution.py:422
  105.0 3.5 %all-to-all-start.3 = ((bf16[8,256,128]{2,1,0:T(8,128)(2,1)}), bf16[8,256,128]{2,1,0:T(8,128)(2,1)S(1)}, u32[]{:S(2)}, u32[]{:S(2)}) async-start(bf16[8,256,128]{2,1,0:T(8,128)(2,1)} %final_pass.1), calls=%async_computation.3 | async-start | bytes 1048576 | tf_op jit(solution)/shard_map/all_to_all | solution.py:422
  108.5 5.8 %collective-permute-start.1 = (bf16[32,128]{1,0:T(8,128)(2,1)S(1)}, bf16[32,128]{1,0:T(8,128)(2,1)S(1)}, u32[]{:S(2)}, u32[]{:S(2)}) collective-permute-start(bf16[32,128]{1,0:T(8,128)(2,1)S(1)} %get-tuple-element.36), channel_id=1, source_target_pairs={{0,64},{8,72},{16,80},{24,88},{32,96},{40,104},{48,112},{56,120},{... | collective-permute-start | bytes 24584 | tf_op jit(solution)/shard_map/ppermute | solution.py:426
  114.3 10.2 %collective-permute-done.1 = bf16[32,128]{1,0:T(8,128)(2,1)S(1)} collective-permute-done((bf16[32,128]{1,0:T(8,128)(2,1)S(1)}, bf16[32,128]{1,0:T(8,128)(2,1)S(1)}, u32[]{:S(2)}, u32[]{:S(2)}) %collective-permute-start.1) | collective-permute-done | bytes 8224 | tf_op jit(solution)/shard_map/ppermute | solution.py:426
  124.5 4.8 %collective-permute-done.2 = bf16[64,128]{1,0:T(8,128)(2,1)S(1)} collective-permute-done((bf16[64,128]{1,0:T(8,128)(2,1)S(1)}, bf16[64,128]{1,0:T(8,128)(2,1)S(1)}, u32[]{:S(2)}, u32[]{:S(2)}) %collective-permute-start.2) | collective-permute-done | bytes 16416 | tf_op jit(solution)/shard_map/ppermute | solution.py:426
  131.2 2.1 %collective-permute-done.3 = bf16[128,128]{1,0:T(8,128)(2,1)S(1)} collective-permute-done((bf16[128,128]{1,0:T(8,128)(2,1)S(1)}, bf16[128,128]{1,0:T(8,128)(2,1)S(1)}, u32[]{:S(2)}, u32[]{:S(2)}) %collective-permute-start.3) | collective-permute-done | bytes 32800 | tf_op jit(solution)/shard_map/ppermute | solution.py:426
  134.6 5.8 %collective-permute-done.4 = bf16[256,128]{1,0:T(8,128)(2,1)S(1)} collective-permute-done((bf16[256,128]{1,0:T(8,128)(2,1)S(1)}, bf16[256,128]{1,0:T(8,128)(2,1)S(1)}, u32[]{:S(2)}, u32[]{:S(2)}) %collective-permute-start.4) | collective-permute-done | bytes 65568 | tf_op jit(solution)/shard_map/ppermute | solution.py:426
  143.0 1.9 %collective-permute-start.6 = (f32[256,128]{1,0:T(8,128)S(1)}, f32[256,128]{1,0:T(8,128)S(1)}, u32[]{:S(2)}, u32[]{:S(2)}) collective-permute-start(f32[256,128]{1,0:T(8,128)S(1)} %row_pass.1), channel_id=1, source_target_pairs={{0,4},{1,5},{2,6},{3,7},{4,0},{5,1},{6,2},{7,3},{8,12},{9,13},{10,... | collective-permute-start | bytes 393224 | tf_op jit(solution)/shard_map/ppermute | solution.py:431
  144.9 5.2 %collective-permute-done.6 = f32[256,128]{1,0:T(8,128)S(1)} collective-permute-done((f32[256,128]{1,0:T(8,128)S(1)}, f32[256,128]{1,0:T(8,128)S(1)}, u32[]{:S(2)}, u32[]{:S(2)}) %collective-permute-start.6) | collective-permute-done | bytes 131104 | tf_op jit(solution)/shard_map/ppermute | solution.py:431
  151.3 3.9 %collective-permute-done.7 = f32[256,128]{1,0:T(8,128)S(1)} collective-permute-done((f32[256,128]{1,0:T(8,128)S(1)}, f32[256,128]{1,0:T(8,128)S(1)}, u32[]{:S(2)}, u32[]{:S(2)}) %collective-permute-start.7) | collective-permute-done | bytes 131104 | tf_op jit(solution)/shard_map/ppermute | solution.py:431
  155.2 1.9 %collective-permute-start.8 = (f32[256,128]{1,0:T(8,128)S(1)}, f32[256,128]{1,0:T(8,128)S(1)}, u32[]{:S(2)}, u32[]{:S(2)}) collective-permute-start(f32[256,128]{1,0:T(8,128)S(1)} %add.26), channel_id=1, source_target_pairs={{0,1},{1,0},{2,3},{3,2},{4,5},{5,4},{6,7},{7,6},{8,9},{9,8},{10,11... | collective-permute-start | bytes 393224 | tf_op jit(solution)/shard_map/ppermute | solution.py:431
  157.2 4.5 %collective-permute-done.8 = f32[256,128]{1,0:T(8,128)S(1)} collective-permute-done((f32[256,128]{1,0:T(8,128)S(1)}, f32[256,128]{1,0:T(8,128)S(1)}, u32[]{:S(2)}, u32[]{:S(2)}) %collective-permute-start.8) | collective-permute-done | bytes 131104 | tf_op jit(solution)/shard_map/ppermute | solution.py:431
  (58 shorter events, 21.1 us)
Async XLA Ops:
  0.6 14.1 %copy-start.10 = (s32[256]{0:T(256)S(1)}, s32[256]{0:T(256)}, u32[]{:S(2)}) copy-start(s32[256]{0:T(256)} %param.11) | copy-start | bytes 3076
  4.7 24.6 %all-to-all-start = ((bf16[32,48,128]{2,1,0:T(8,128)(2,1)}), bf16[32,48,128]{2,1,0:T(8,128)(2,1)S(1)}, u32[]{:S(2)}, u32[]{:S(2)}) async-start(bf16[32,48,128]{2,1,0:T(8,128)(2,1)} %mass_pass.1), calls=%async_computation | async-start | bytes 786432 | tf_op jit(solution)/shard_map/all_to_all | solution.py:422
  32.7 17.3 %all-to-all-start.1 = ((bf16[8,320,128]{2,1,0:T(8,128)(2,1)}), bf16[8,320,128]{2,1,0:T(8,128)(2,1)S(1)}, u32[]{:S(2)}, u32[]{:S(2)}) async-start(bf16[8,320,128]{2,1,0:T(8,128)(2,1)} %pick.1), calls=%async_computation.1 | async-start | bytes 1310720 | tf_op jit(solution)/shard_map/all_to_all | solution.py:422
  39.3 10.7 %copy-start.1 = (f32[256,128]{1,0:T(8,128)S(1)}, f32[256,128]{1,0:T(8,128)}, u32[]{:S(2)}) copy-start(f32[256,128]{1,0:T(8,128)} %get-tuple-element.23.st_ref) | copy-start | bytes 393220
  39.3 10.7 %copy-start.3 = (f32[4,256,128]{2,1,0:T(8,128)S(1)}, f32[4,256,128]{2,1,0:T(8,128)}, u32[]{:S(2)}) copy-start(f32[4,256,128]{2,1,0:T(8,128)} %get-tuple-element.27.cst_ref) | copy-start | bytes 1572868
  39.3 10.7 %copy-start.5 = (bf16[256,128]{1,0:T(8,128)(2,1)S(1)}, bf16[256,128]{1,0:T(8,128)(2,1)}, u32[]{:S(2)}) copy-start(bf16[256,128]{1,0:T(8,128)(2,1)} %tan_ref.5) | copy-start | bytes 196612
  39.3 10.7 %copy-start.8 = (bf16[256,128]{1,0:T(8,128)(2,1)S(1)}, bf16[256,128]{1,0:T(8,128)(2,1)}, u32[]{:S(2)}) copy-start(bf16[256,128]{1,0:T(8,128)(2,1)} %f_ref.3) | copy-start | bytes 196612
  58.3 2.1 %collective-permute-start = (bf16[8,256,128]{2,1,0:T(8,128)(2,1)}, bf16[8,256,128]{2,1,0:T(8,128)(2,1)S(1)}, u32[]{:S(2)}, u32[]{:S(2)}) collective-permute-start(bf16[8,256,128]{2,1,0:T(8,128)(2,1)} %get-tuple-element.34), channel_id=1, source_target_pairs={{0,8},{8,0},{16,24},{24,16},{32,40},{40,32},{48,56},{56,48},{64,72... | collective-permute-start | bytes 1572872 | tf_op jit(solution)/shard_map/ppermute | solution.py:452
  67.6 2.2 %collective-permute-start.9 = (bf16[8,256,128]{2,1,0:T(8,128)(2,1)}, bf16[8,256,128]{2,1,0:T(8,128)(2,1)S(1)}, u32[]{:S(2)}, u32[]{:S(2)}) collective-permute-start(bf16[8,256,128]{2,1,0:T(8,128)(2,1)} %get-tuple-element.43), channel_id=1, source_target_pairs={{0,8},{8,0},{16,24},{24,16},{32,40},{40,32},{48,56},{56,48},{64,72... | collective-permute-start | bytes 1572872 | tf_op jit(solution)/shard_map/ppermute | solution.py:459
  67.8 14.5 %collective-permute-start.10 = (bf16[8,256,128]{2,1,0:T(8,128)(2,1)S(1)}, bf16[8,256,128]{2,1,0:T(8,128)(2,1)S(1)}, u32[]{:S(2)}, u32[]{:S(2)}) collective-permute-start(bf16[8,256,128]{2,1,0:T(8,128)(2,1)S(1)} %add_convert_fusion.1), channel_id=1, source_target_pairs={{0,128},{8,136},{16,144},{24,152},{32,160},{40,168},{48,176},{56,1... | collective-permute-start | bytes 1572872 | tf_op jit(solution)/shard_map/ppermute | solution.py:454
  83.7 58.2 %copy-start.6 = (f32[256,128]{1,0:T(8,128)S(1)}, f32[256,128]{1,0:T(8,128)}, u32[]{:S(2)}) copy-start(f32[256,128]{1,0:T(8,128)} %get-tuple-element.37.x_ref) | copy-start | bytes 393220
  83.7 58.2 %copy-start.7 = (f32[256,128]{1,0:T(8,128)S(1)}, f32[256,128]{1,0:T(8,128)}, u32[]{:S(2)}) copy-start(f32[256,128]{1,0:T(8,128)} %get-tuple-element.38.w_ref) | copy-start | bytes 393220
  105.0 24.9 %all-to-all-start.3 = ((bf16[8,256,128]{2,1,0:T(8,128)(2,1)}), bf16[8,256,128]{2,1,0:T(8,128)(2,1)S(1)}, u32[]{:S(2)}, u32[]{:S(2)}) async-start(bf16[8,256,128]{2,1,0:T(8,128)(2,1)} %final_pass.1), calls=%async_computation.3 | async-start | bytes 1048576 | tf_op jit(solution)/shard_map/all_to_all | solution.py:422
  108.5 16.0 %collective-permute-start.1 = (bf16[32,128]{1,0:T(8,128)(2,1)S(1)}, bf16[32,128]{1,0:T(8,128)(2,1)S(1)}, u32[]{:S(2)}, u32[]{:S(2)}) collective-permute-start(bf16[32,128]{1,0:T(8,128)(2,1)S(1)} %get-tuple-element.36), channel_id=1, source_target_pairs={{0,64},{8,72},{16,80},{24,88},{32,96},{40,104},{48,112},{56,120},{... | collective-permute-start | bytes 24584 | tf_op jit(solution)/shard_map/ppermute | solution.py:426
  124.5 4.8 %collective-permute-start.2 = (bf16[64,128]{1,0:T(8,128)(2,1)S(1)}, bf16[64,128]{1,0:T(8,128)(2,1)S(1)}, u32[]{:S(2)}, u32[]{:S(2)}) collective-permute-start(bf16[64,128]{1,0:T(8,128)(2,1)S(1)} %pad_maximum_fusion.3), channel_id=1, source_target_pairs={{0,32},{8,40},{16,48},{24,56},{32,0},{40,8},{48,16},{56,24},{64,96... | collective-permute-start | bytes 49160 | tf_op jit(solution)/shard_map/ppermute | solution.py:426
  129.4 3.9 %collective-permute-start.3 = (bf16[128,128]{1,0:T(8,128)(2,1)S(1)}, bf16[128,128]{1,0:T(8,128)(2,1)S(1)}, u32[]{:S(2)}, u32[]{:S(2)}) collective-permute-start(bf16[128,128]{1,0:T(8,128)(2,1)S(1)} %pad_maximum_fusion.2), channel_id=1, source_target_pairs={{0,16},{8,24},{16,0},{24,8},{32,48},{40,56},{48,32},{56,40},{64,80... | collective-permute-start | bytes 98312 | tf_op jit(solution)/shard_map/ppermute | solution.py:426
  129.9 20.9 %collective-permute-start.11 = (bf16[8,256,128]{2,1,0:T(8,128)(2,1)S(1)}, bf16[8,256,128]{2,1,0:T(8,128)(2,1)S(1)}, u32[]{:S(2)}, u32[]{:S(2)}) collective-permute-start(bf16[8,256,128]{2,1,0:T(8,128)(2,1)S(1)} %all-to-all-done.3.own_ref), channel_id=1, source_target_pairs={{0,128},{8,136},{16,144},{24,152},{32,160},{40,168},{48,176},{56,1... | collective-permute-start | bytes 1572872 | tf_op jit(solution)/shard_map/ppermute | solution.py:470
  133.3 7.1 %collective-permute-start.4 = (bf16[256,128]{1,0:T(8,128)(2,1)S(1)}, bf16[256,128]{1,0:T(8,128)(2,1)S(1)}, u32[]{:S(2)}, u32[]{:S(2)}) collective-permute-start(bf16[256,128]{1,0:T(8,128)(2,1)S(1)} %pad_maximum_fusion.1), channel_id=1, source_target_pairs={{0,128},{8,136},{16,144},{24,152},{32,160},{40,168},{48,176},{56,1... | collective-permute-start | bytes 196616 | tf_op jit(solution)/shard_map/ppermute | solution.py:426
  140.4 1.4 collective-permute-start.5
  143.0 7.1 %collective-permute-start.6 = (f32[256,128]{1,0:T(8,128)S(1)}, f32[256,128]{1,0:T(8,128)S(1)}, u32[]{:S(2)}, u32[]{:S(2)}) collective-permute-start(f32[256,128]{1,0:T(8,128)S(1)} %row_pass.1), channel_id=1, source_target_pairs={{0,4},{1,5},{2,6},{3,7},{4,0},{5,1},{6,2},{7,3},{8,12},{9,13},{10,... | collective-permute-start | bytes 393224 | tf_op jit(solution)/shard_map/ppermute | solution.py:431
  150.1 5.1 %collective-permute-start.7 = (f32[256,128]{1,0:T(8,128)S(1)}, f32[256,128]{1,0:T(8,128)S(1)}, u32[]{:S(2)}, u32[]{:S(2)}) collective-permute-start(f32[256,128]{1,0:T(8,128)S(1)} %add.25), channel_id=1, source_target_pairs={{0,2},{1,3},{2,0},{3,1},{4,6},{5,7},{6,4},{7,5},{8,10},{9,11},{10,... | collective-permute-start | bytes 393224 | tf_op jit(solution)/shard_map/ppermute | solution.py:431
  150.8 11.6 %collective-permute-start.13 = (bf16[8,256,128]{2,1,0:T(8,128)(2,1)S(1)}, bf16[8,256,128]{2,1,0:T(8,128)(2,1)S(1)}, u32[]{:S(2)}, u32[]{:S(2)}) collective-permute-start(bf16[8,256,128]{2,1,0:T(8,128)(2,1)S(1)} %all-to-all-done.3.own_ref), channel_id=1, source_target_pairs={{0,8},{8,0},{16,24},{24,16},{32,40},{40,32},{48,56},{56,48},{64,72... | collective-permute-start | bytes 1572872 | tf_op jit(solution)/shard_map/ppermute | solution.py:476
  150.8 13.2 %collective-permute-start.12 = (bf16[8,256,128]{2,1,0:T(8,128)(2,1)S(1)}, bf16[8,256,128]{2,1,0:T(8,128)(2,1)S(1)}, u32[]{:S(2)}, u32[]{:S(2)}) collective-permute-start(bf16[8,256,128]{2,1,0:T(8,128)(2,1)S(1)} %collective-permute-done.11.own_ref), channel_id=1, source_target_pairs={{0,8},{8,0},{16,24},{24,16},{32,40},{40,32},{48,56},{56,48},{64,72... | collective-permute-start | bytes 1572872 | tf_op jit(solution)/shard_map/ppermute | solution.py:478
  155.2 6.6 %collective-permute-start.8 = (f32[256,128]{1,0:T(8,128)S(1)}, f32[256,128]{1,0:T(8,128)S(1)}, u32[]{:S(2)}, u32[]{:S(2)}) collective-permute-start(f32[256,128]{1,0:T(8,128)S(1)} %add.26), channel_id=1, source_target_pairs={{0,1},{1,0},{2,3},{3,2},{4,5},{5,4},{6,7},{7,6},{8,9},{9,8},{10,11... | collective-permute-start | bytes 393224 | tf_op jit(solution)/shard_map/ppermute | solution.py:431
  (4 other events, 3.2 us)

commit v5 on v4

--- a/solution.py
+++ b/solution.py
@@ -1,3 +1,5 @@
+import functools
+
 import jax
 import jax.numpy as jnp
 from jax import lax
@@ -24,6 +26,7 @@
 LOG2E = 1.4426950408889634
 VMEM = pl.BlockSpec(memory_space=pltpu.VMEM)
 SMEM = pl.BlockSpec(memory_space=pltpu.SMEM)
+HBM = pl.BlockSpec(memory_space=pltpu.HBM)
 MB = 1024 * 1024
 
 
@@ -34,6 +37,9 @@
     return hi, mid, lo
 
 
+WIDE = 4096
+
+
 def mass_kernel(q_ref, codes_ref, tan_ref, blk_ref, acc):
     step = pl.program_id(0)
 
@@ -45,11 +51,11 @@
         rows = slice(g * RG, (g + 1) * RG)
         x = codes_ref[rows, :].astype(F32)
         total = x[:, :D]
-        for k in range(1, CN // D):
+        for k in range(1, WIDE // D):
             total = total + x[:, k * D : (k + 1) * D]
         acc[rows, :] += total
 
-    @pl.when(step == NCH - 1)
+    @pl.when(step == LOCAL // WIDE - 1)
     def _():
         mass = jnp.sum(jnp.transpose(acc[...]), axis=0, keepdims=True)
         hi, mid, lo = split3(mass)
@@ -64,10 +70,10 @@
 def mass_pass(q, codes, tan):
     return pl.pallas_call(
         mass_kernel,
-        grid=(NCH,),
+        grid=(LOCAL // WIDE,),
         in_specs=[
             SMEM,
-            pl.BlockSpec((ROWS, CN), lambda c: (0, c)),
+            pl.BlockSpec((ROWS, WIDE), lambda c: (0, c)),
             pl.BlockSpec((ROWS, D), lambda c: (0, 0)),
         ],
         out_specs=pl.BlockSpec((DP, SUB + 16, D), lambda c: (0, 0, 0)),
@@ -79,7 +85,7 @@
     )(q, codes, tan)
 
 
-def score_kernel(f_ref, tan_ref, a_ref, p_ref, codes_ref, e_ref, u_ref, cst_ref, st_ref, h_ref, s_sc, t_sc, run, acc):
+def score_kernel(f_ref, tan_ref, a_ref, p_ref, codes_ref, e_ref, u_ref, cst_ref, st_ref, s_sc, t_sc, run, acc):
     step = pl.program_id(0)
     f = f_ref[...]
     s_sc[...] = lax.dot_general(f, a_ref[...], NT, preferred_element_type=F32)
@@ -95,7 +101,7 @@
         acc[...] = jnp.zeros_like(acc)
 
     acc[...] += jnp.dot(codes_ref[...], p_ref[...], preferred_element_type=F32)
-    h_ref[...] = acc[...].astype(BF16)
+    st_ref[:, D:] = acc[...]
     lane = lax.broadcasted_iota(jnp.int32, (RG, D), 1)
     for g in range(ROWS // RG):
         rows = slice(g * RG, (g + 1) * RG)
@@ -119,7 +125,7 @@
         run[0, rows, :] = new
         run[1, rows, :] = z_run
         run[2, rows, :] = et_run
-        st_ref[rows, :] = jnp.where(lane == 0, new, jnp.where(lane == 1, z_run, et_run))
+        st_ref[rows, :D] = jnp.where(lane == 0, new, jnp.where(lane == 1, z_run, et_run))
 
 
 def score_pass(f, tan, a, p, codes):
@@ -137,15 +143,13 @@
             pl.BlockSpec((ROWS, CN), lambda c: (0, c)),
             pl.BlockSpec((ROWS, CN), lambda c: (0, c)),
             pl.BlockSpec((1, ROWS, D), lambda c: (c, 0, 0)),
-            pl.BlockSpec((ROWS, D), lambda c: (0, 0)),
-            pl.BlockSpec((ROWS, D), lambda c: (0, 0)),
+            pl.BlockSpec((ROWS, 2 * D), lambda c: (0, 0)),
         ],
         out_shape=[
             jax.ShapeDtypeStruct((ROWS, LOCAL), BF16),
             jax.ShapeDtypeStruct((ROWS, LOCAL), BF16),
             jax.ShapeDtypeStruct((NCH, ROWS, D), F32),
-            jax.ShapeDtypeStruct((ROWS, D), F32),
-            jax.ShapeDtypeStruct((ROWS, D), BF16),
+            jax.ShapeDtypeStruct((ROWS, 2 * D), F32),
         ],
         scratch_shapes=[
             pltpu.VMEM((ROWS, CN), F32),
@@ -202,7 +206,7 @@
 PAY = ROWS + 2 * STAT + SUB
 
 
-def pick_kernel(q_ref, tab_ref, part_ref, st_ref, h_ref, pay_ref):
+def pick_kernel(q_ref, tab_ref, part_ref, st_ref, pay_ref):
     q = q_ref[0]
     partner = part_ref[...]
     group = partner // ROWS
@@ -223,7 +227,7 @@
     mass = jnp.sum(jnp.where(here, mass, 0.0), axis=1, keepdims=True)
 
     lane = lax.broadcasted_iota(jnp.int32, (ROWS, D), 1)
-    stats = jnp.where(lane == 3, mass, st_ref[...])
+    stats = jnp.where(lane == 3, mass, st_ref[:, :D])
     flat = jnp.transpose(stats)[:4, :]
     hi, mid, lo = split3(flat)
     flat = jnp.concatenate([hi, mid, lo, jnp.zeros((STAT - 12, ROWS), F32)], axis=0)
@@ -231,21 +235,21 @@
     payload = jnp.concatenate([rows, flat], axis=0)
     for i in range(PR):
         pay_ref[i, : ROWS + 2 * STAT, :] = payload
-        pay_ref[i, ROWS + 2 * STAT :, :] = h_ref[i * SUB : (i + 1) * SUB, :]
-
-
-def pick(q, tab, partner, st, h):
+        pay_ref[i, ROWS + 2 * STAT :, :] = st_ref[i * SUB : (i + 1) * SUB, D:].astype(BF16)
+
+
+def pick(q, tab, partner, st):
     return pl.pallas_call(
         pick_kernel,
-        in_specs=[SMEM, VMEM, VMEM, VMEM, VMEM],
+        in_specs=[SMEM, VMEM, VMEM, VMEM],
         out_specs=VMEM,
         out_shape=jax.ShapeDtypeStruct((PR, PAY, D), BF16),
         compiler_params=pltpu.CompilerParams(vmem_limit_bytes=10 * MB),
         name="pick",
-    )(q, tab, partner, st, h)
-
-
-def stats_kernel(rec_ref, f_ref, tan_ref, st_ref, cst_ref, f12_ref, swt_ref, gst_ref, h_ref):
+    )(q, tab, partner, st)
+
+
+def stats_kernel(rec_ref, f_ref, tan_ref, cst_ref, f12_ref, gst_ref, h_ref):
     total = jnp.zeros((ROWS, D), F32)
     h = jnp.zeros((SUB, D), F32)
     flats = []
@@ -255,7 +259,7 @@
         flat = jnp.concatenate([flat[:STAT], flat[STAT:]], axis=1)
         flats.append((flat[0:4] + flat[4:8]) + flat[8:12])
         h = h + rec_ref[i, ROWS + 2 * STAT :, :].astype(F32)
-    swt_ref[...] = (total * SCALE).astype(BF16)
+    f12_ref[2 * NCH] = (total * SCALE).astype(BF16)
     h_ref[...] = h.astype(BF16)
     top = flats[0][0:1]
     for i in range(1, PR):
@@ -278,31 +282,29 @@
     tan = tan_ref[...].astype(F32)
     for c in range(NCH):
         scale = weight * jnp.exp(cst_ref[c, :, 0:1] - top)
-        f12_ref[c, :, :D] = (INV * scale * f).astype(BF16)
-        f12_ref[c, :, D:] = (scale * ((cst_ref[c, :, 1:2] - mean) * f + tan)).astype(BF16)
-
-
-def stats_pass(rec, f, tan, st, cst):
+        f12_ref[2 * c] = (INV * scale * f).astype(BF16)
+        f12_ref[2 * c + 1] = (scale * ((cst_ref[c, :, 1:2] - mean) * f + tan)).astype(BF16)
+
+
+def stats_pass(rec, f, tan, cst):
     return pl.pallas_call(
         stats_kernel,
-        in_specs=[VMEM] * 5,
-        out_specs=[VMEM] * 4,
+        in_specs=[VMEM] * 4,
+        out_specs=[VMEM] * 3,
         out_shape=[
-            jax.ShapeDtypeStruct((NCH, ROWS, 2 * D), BF16),
-            jax.ShapeDtypeStruct((ROWS, D), BF16),
+            jax.ShapeDtypeStruct((2 * NCH + 1, ROWS, D), BF16),
             jax.ShapeDtypeStruct((ROWS, D), F32),
             jax.ShapeDtypeStruct((SUB, D), BF16),
         ],
         compiler_params=pltpu.CompilerParams(vmem_limit_bytes=10 * MB),
         name="stats_pass",
-    )(rec, f, tan, st, cst)
+    )(rec, f, tan, cst)
 
 
 def proto_kernel(s_ref, f12_ref, swt_ref, u_ref, e_ref, codes_ref, mine_ref, send_ref):
-    f12 = f12_ref[0]
-    res = lax.dot_general(u_ref[...], f12[:, :D], TN, preferred_element_type=F32)
-    res = res + lax.dot_general(e_ref[...], f12[:, D:], TN, preferred_element_type=F32)
-    res = res - lax.dot_general(codes_ref[...], swt_ref[...], TN, preferred_element_type=F32)
+    res = lax.dot_general(u_ref[...], f12_ref[0], TN, preferred_element_type=F32)
+    res = res + lax.dot_general(e_ref[...], f12_ref[1], TN, preferred_element_type=F32)
+    res = res - lax.dot_general(codes_ref[...], swt_ref[0], TN, preferred_element_type=F32)
     first = s_ref[0] == 0
     for b in range(CN // (2 * ROWS)):
         even = res[2 * b * ROWS : (2 * b + 1) * ROWS]
@@ -311,7 +313,7 @@
         send_ref[b] = jnp.where(first, odd, even).astype(BF16)
 
 
-def proto_pass(scalars, f12, swt, u, e, codes):
+def proto_pass(scalars, f12, u, e, codes):
     nb = CN // (2 * ROWS)
     steps = NCH // 2
     wide = pl.BlockSpec((ROWS, CN), lambda c, s: (0, s[1] * steps + c))
@@ -321,8 +323,8 @@
             num_scalar_prefetch=1,
             grid=(steps,),
             in_specs=[
-                pl.BlockSpec((1, ROWS, 2 * D), lambda c, s: (s[1] * steps + c, 0, 0)),
-                pl.BlockSpec((ROWS, D), lambda c, s: (0, 0)),
+                pl.BlockSpec((2, ROWS, D), lambda c, s: (s[1] * steps + c, 0, 0)),
+                pl.BlockSpec((1, ROWS, D), lambda c, s: (2 * NCH, 0, 0)),
                 wide,
                 wide,
                 wide,
@@ -339,7 +341,7 @@
         cost_estimate=pl.CostEstimate(flops=3 * ROWS * LOCAL * D * 2, bytes_accessed=9 << 20, transcendentals=0),
         compiler_params=pltpu.CompilerParams(vmem_limit_bytes=56 * MB),
         name="proto_pass",
-    )(scalars, f12, swt, u, e, codes)
+    )(scalars, f12, f12, u, e, codes)
 
 
 def final_kernel(pieces_ref, out_ref):
@@ -366,7 +368,7 @@
     q = s_ref[0]
     partner = part_ref[...]
     away = (partner // ROWS) ^ s_ref[1]
-    block = ((away >> 3) & 1) + 2 * ((away >> 2) & 1) + 4 * ((away >> 1) & 1) + 8 * ((away >> 4) & 1) + 16 * (away & 1)
+    block = (away & 1) + 2 * ((away >> 3) & 1) + 4 * ((away >> 2) & 1) + 8 * ((away >> 1) & 1) + 16 * ((away >> 4) & 1)
     row = partner % ROWS
     column = jnp.where((row // SUB) == q, block * SUB + row % SUB, -1)
     hot = (lax.broadcasted_iota(jnp.int32, (ROWS, DP * SUB), 1) == column).astype(F32).astype(BF16)
@@ -387,30 +389,34 @@
     )(scalars, own, other, partner, x, w, st, gst)
 
 
-def place_kernel(s_ref, own_ref, other_ref, *refs):
+def place_kernel(count, s_ref, *refs):
     out_ref, sems = refs[-2], refs[-1]
-    copies = [
-        pltpu.make_async_copy(own_ref, out_ref.at[s_ref[0], :, s_ref[1]], sems.at[0]),
-        pltpu.make_async_copy(other_ref, out_ref.at[s_ref[0], :, 1 - s_ref[1]], sems.at[1]),
-    ]
+    copies = []
+    for i in range(count):
+        for part in range(4):
+            copies.append(pltpu.make_async_copy(
+                refs[i].at[2 * part : 2 * part + 2],
+                out_ref.at[s_ref[0], 2 * part : 2 * part + 2, s_ref[1 + i]],
+                sems.at[4 * i + part],
+            ))
     for copy in copies:
         copy.start()
     for copy in copies:
         copy.wait()
 
 
-def place(scalars, own, other, whole):
+def place(scalars, blocks, whole):
     rest = () if whole is None else (whole,)
     return pl.pallas_call(
-        place_kernel,
-        in_specs=[SMEM, VMEM, VMEM] + [pl.BlockSpec(memory_space=pltpu.HBM)] * len(rest),
-        out_specs=pl.BlockSpec(memory_space=pltpu.HBM),
+        functools.partial(place_kernel, len(blocks)),
+        in_specs=[SMEM] + [VMEM] * len(blocks) + [HBM] * len(rest),
+        out_specs=HBM,
         out_shape=jax.ShapeDtypeStruct((2, 8, 2, ROWS, D), BF16),
-        scratch_shapes=[pltpu.SemaphoreType.DMA((2,))],
-        input_output_aliases={3: 0} if rest else {},
+        scratch_shapes=[pltpu.SemaphoreType.DMA((8,))],
+        input_output_aliases={1 + len(blocks): 0} if rest else {},
         compiler_params=pltpu.CompilerParams(vmem_limit_bytes=4 * MB),
         name="place",
-    )(scalars, own, other, *rest)
+    )(scalars, *blocks, *rest)
 
 
 CORE_PERM = [(i, i ^ 1) for i in range(DP)]
@@ -441,42 +447,43 @@
 
     block = mass_pass(qs, codes, tangent_embed)
     table = exchange(block, "dp")
-    e, u, cst, st, h_part = score_pass(feature_matrix, tangent_embed, anchor_matrix, anchor_perturbation, codes)
-
-    received = exchange(pick(qs, table, partner, st, h_part), "proto")
+    e, u, cst, st = score_pass(feature_matrix, tangent_embed, anchor_matrix, anchor_perturbation, codes)
+
+    received = exchange(pick(qs, table, partner, st), "proto")
     x, w = embed_pass(e, u, anchor_matrix, anchor_perturbation, cst, st)
     received, x, w = lax.optimization_barrier((received, x, w))
-    f12, swt, gst, h_own = stats_pass(received, feature_matrix, tangent_embed, st, cst)
-
-    mine_far, send_far = proto_pass(jnp.stack([core, 1 - y]), f12, swt, u, e, codes)
+    f12, gst, h_own = stats_pass(received, feature_matrix, tangent_embed, cst)
+
+    table = doubled(h_own, 1)
+    mine_far, send_far = proto_pass(jnp.stack([core, 1 - y]), f12, u, e, codes)
+    table = doubled(table, 8)
     got_far = lax.ppermute(send_far, "dp", CORE_PERM)
     to_y = (mine_far + got_far.astype(F32)).astype(BF16)
     from_far = lax.ppermute(to_y, "dp", Y_PERM)
-    f12, swt, to_y, h_own = lax.optimization_barrier((f12, swt, to_y, h_own))
-    table = doubled(h_own, 8)
-    mine_near, send_near = proto_pass(jnp.stack([core, y]), f12, swt, u, e, codes)
+    f12, to_y = lax.optimization_barrier((f12, to_y))
     table = doubled(table, 4)
+    mine_near, send_near = proto_pass(jnp.stack([core, y]), f12, u, e, codes)
     got_near = lax.ppermute(send_near, "dp", CORE_PERM)
     table = doubled(table, 2)
     quarter = (mine_near + got_near.astype(F32) + from_far.astype(F32)).astype(BF16)
     pieces = exchange(quarter, "dp", Z_GROUPS)
-    table = doubled(table, 16)
-    other = lax.ppermute(table, "dp", CORE_PERM)
+    other = lax.ppermute(table, "dp", Y_PERM)
     embed = row_pass(jnp.stack([q, dp]), table, other, partner, x, w, st, gst)
     final = final_pass(pieces)
 
-    swapped = swap(embed, 4)
+    swapped = swap(embed, 1)
     along_z = exchange(final, "dp", Z_GROUPS)
     from_y = lax.ppermute(along_z, "dp", Y_PERM)
     embed = embed + swapped
+    swapped = swap(embed, 4)
+    embed = embed + swapped
     swapped = swap(embed, 2)
-    embed = embed + swapped
-    swapped = swap(embed, 1)
     hvp_embed = (embed + swapped).astype(BF16)
     own_core = lax.ppermute(along_z, "dp", CORE_PERM)
-    whole = place(jnp.stack([y, core]), along_z, own_core, None)
+    whole = place(jnp.stack([y, core, 1 - core]), (along_z, own_core), None)
     far_core = lax.ppermute(from_y, "dp", CORE_PERM)
-    whole = place(jnp.stack([1 - y, core]), from_y, far_core, whole)
+    whole = place(jnp.stack([1 - y, core]), (from_y,), whole)
+    whole = place(jnp.stack([1 - y, 1 - core]), (far_core,), whole)
     return (hvp_embed, whole.reshape(LOCAL, D))
 
 

time: 167 us -> 163 us (0.976)
  waiting for transfers between devices: 59.2 us -> 56.8 us
    ppermute x4, waiting for transfers between devices: 22.9 us -> 18.2 us  [doubled(): other = lax.ppermute(x, 'dp', [(i, i ^ bit) for i in range(DP)])]
    ppermute x1, waiting for transfers between devices: 1.26 us -> 3.6 us  [inner(): other = lax.ppermute(table, 'dp', Y_PERM)]
    pallas_call x5 -> x6, Pallas kernels: 9.69 us -> 10.4 us  [the longest x3 4.37 us: place(): pl.pallas_call(functools.partial(place_kernel, len(blocks)), in_specs=[SM...]
  transfers between devices with their start and end apart: 17 -> 17, of which waited for: 12 -> 12; matrix products, arithmetic and copies ran while one was open for 1% -> 1% of each run, Pallas kernels for 13% -> 14%
where the time goes in v5:
time: 163 us; the launch traced here: 162 us
  waiting for transfers between devices  56.8 us (35%)
  Pallas kernels  41.6 us (26%)
  starting transfers between devices  36.1 us (22%)
  blocking collectives  20.5 us (13%)
  other arithmetic  4.26 us (3%)
  local copies, waits for them, and re-layouts  1.97 us (1%)
    all_to_all x1, blocking collectives, exchange(): return lax.all_to_all(x, axis, 0, 0, axis_index_groups=groups, tiled=True)  20.5 us
    all_to_all x3, starting transfers between devices, exchange(): return lax.all_to_all(x, axis, 0, 0, axis_index_groups=groups, tiled=True)  19.6 us
    ppermute x4, waiting for transfers between devices, doubled(): other = lax.ppermute(x, 'dp', [(i, i ^ bit) for i in range(DP)])  18.2 us
    ppermute x3, waiting for transfers between devices, swap(): return lax.ppermute(x, 'proto', [(i, i ^ bit) for i in range(PR)])  13.3 us
    ppermute x1, waiting for transfers between devices, inner(): from_far = lax.ppermute(to_y, 'dp', Y_PERM)  12.5 us
    pallas_call x2, Pallas kernels, proto_pass(): pl.pallas_call(proto_kernel, grid_spec=pltpu.PrefetchScalarGridSpec(num_s...  11.3 us
    pallas_call x1, Pallas kernels, score_pass(): pl.pallas_call(score_kernel, grid=(NCH,), in_specs=[pl.BlockSpec((ROWS, D...  10.3 us
    pallas_call x1, Pallas kernels, embed_pass(): pl.pallas_call(embed_kernel, grid=(NCH,), in_specs=[pl.BlockSpec((ROWS, C...  7.61 us
  transfers between devices with their start and end apart: 17, of which 12 were waited for; matrix products, arithmetic and copies ran while one was open for 1% of the time, Pallas kernels for 14%

profile of v5, /device:TPU:8, one launch (start us, length us, event | category | flops | bytes accessed | tf_op | source)
XLA Modules:
  0.0 162.2 jit_solution(9869990880884718013)
XLA Ops:
  0.6 3.4 %mass_pass.1 = bf16[32,48,128]{2,1,0:T(8,128)(2,1)} custom-call(s32[1]{0:T(128)} %bitcast.q_ref, bf16[256,8192]{1,0:T(8,128)(2,1)} %codes_ref.7, bf16[256,128]{1,0:T(8,128)(2,1)} %tan_ref.5), custom_call_target="tpu_custom_call" | custom-call | flops 2097152 | bytes 5242880 | tf_op jit(solution)/shard_map/mass_pass/pallas_call | solution.py:71
  4.1 10.1 %all-to-all-start = ((bf16[32,48,128]{2,1,0:T(8,128)(2,1)}), bf16[32,48,128]{2,1,0:T(8,128)(2,1)S(1)}, u32[]{:S(2)}, u32[]{:S(2)}) async-start(bf16[32,48,128]{2,1,0:T(8,128)(2,1)} %mass_pass.1), calls=%async_computation | async-start | bytes 786432 | tf_op jit(solution)/shard_map/all_to_all | solution.py:428
  14.3 10.3 %score_pass.1 = (bf16[256,8192]{1,0:T(8,128)(2,1)}, bf16[256,8192]{1,0:T(8,128)(2,1)}, f32[4,256,128]{2,1,0:T(8,128)}, f32[256,256]{1,0:T(8,128)}) custom-call(bf16[256,128]{1,0:T(8,128)(2,1)} %f_ref.3, bf16[256,128]{1,0:T(8,128)(2,1)} %tan_ref.5, bf16[8192,128]{1,0:T(8,128)(2,1)} %a_ref.3, bf16[8192,128]{1,0:T(8,128)(2,1)} %p_ref.3, bf16[256,8192]{1,0:T(8,128)(2,1)} %codes_ref.7), custom_call_target="tpu_custom_call" | custom-call | flops 5368709120 | bytes 12582912 | tf_op jit(solution)/shard_map/score_pass/pallas_call | solution.py:132
  24.6 4.1 %all-to-all-done.tab_ref = bf16[32,48,128]{2,1,0:T(8,128)(2,1)S(1)} async-done(((bf16[32,48,128]{2,1,0:T(8,128)(2,1)}), bf16[32,48,128]{2,1,0:T(8,128)(2,1)S(1)}, u32[]{:S(2)}, u32[]{:S(2)}) %all-to-all-start) | async-done | bytes 393248 | tf_op jit(solution)/shard_map/all_to_all | solution.py:428
  31.2 6.0 %all-to-all-start.1 = ((bf16[8,320,128]{2,1,0:T(8,128)(2,1)}), bf16[8,320,128]{2,1,0:T(8,128)(2,1)S(1)}, u32[]{:S(2)}, u32[]{:S(2)}) async-start(bf16[8,320,128]{2,1,0:T(8,128)(2,1)} %pick.1), calls=%async_computation.1 | async-start | bytes 1310720 | tf_op jit(solution)/shard_map/all_to_all | solution.py:428
  37.9 7.6 %embed_pass.1 = (f32[256,128]{1,0:T(8,128)}, f32[256,128]{1,0:T(8,128)}) custom-call(bf16[256,8192]{1,0:T(8,128)(2,1)} %get-tuple-element.20.e_ref, bf16[256,8192]{1,0:T(8,128)(2,1)} %get-tuple-element.21.u_ref, bf16[8192,128]{1,0:T(8,128)(2,1)} %a_ref.3, bf16[8192,128]{1,0:T(8,128)(2,1)} %p_ref.3, f32[4,256,128]{2,1,0:T(8,128)} %get-tuple-element.22.cst_ref, ...), custom_call_target="tpu_custom_call" | custom-call | flops 3221225472 | bytes 12582912 | tf_op jit(solution)/shard_map/embed_pass/pallas_call | solution.py:183
  45.5 3.1 %all-to-all-done.1.rec_ref = bf16[8,320,128]{2,1,0:T(8,128)(2,1)S(1)} async-done(((bf16[8,320,128]{2,1,0:T(8,128)(2,1)}), bf16[8,320,128]{2,1,0:T(8,128)(2,1)S(1)}, u32[]{:S(2)}, u32[]{:S(2)}) %all-to-all-start.1) | async-done | bytes 655392 | tf_op jit(solution)/shard_map/all_to_all | solution.py:428
  50.4 5.7 %proto_pass.2 = (f32[8,256,128]{2,1,0:T(8,128)}, bf16[8,256,128]{2,1,0:T(8,128)(2,1)}) custom-call(s32[2]{0:T(128)} %get-tuple-element.39.s_ref, bf16[9,256,128]{2,1,0:T(8,128)(2,1)} %copy-done, bf16[9,256,128]{2,1,0:T(8,128)(2,1)} %copy-done, bf16[256,8192]{1,0:T(8,128)(2,1)} %get-tuple-element.21.u_ref, bf16[256,8192]{1,0:T(8,128)(2,1)} %get-tuple-element.20.e_ref, ...), custom_call_target="tpu_custom_call" | custom-call | flops 1610612736 | bytes 9437184 | tf_op jit(solution)/shard_map/proto_pass/pallas_call | solution.py:320
  56.1 2.1 %collective-permute-done.8 = bf16[8,256,128]{2,1,0:T(8,128)(2,1)S(1)} collective-permute-done((bf16[8,256,128]{2,1,0:T(8,128)(2,1)}, bf16[8,256,128]{2,1,0:T(8,128)(2,1)S(1)}, u32[]{:S(2)}, u32[]{:S(2)}) %collective-permute-start.8) | collective-permute-done | bytes 524320 | tf_op jit(solution)/shard_map/ppermute | solution.py:460
  59.6 5.7 %proto_pass.3 = (f32[8,256,128]{2,1,0:T(8,128)}, bf16[8,256,128]{2,1,0:T(8,128)(2,1)}) custom-call(s32[2]{0:T(128)} %get-tuple-element.38.s_ref, bf16[9,256,128]{2,1,0:T(8,128)(2,1)} %copy-done, bf16[9,256,128]{2,1,0:T(8,128)(2,1)} %copy-done, bf16[256,8192]{1,0:T(8,128)(2,1)} %get-tuple-element.21.u_ref, bf16[256,8192]{1,0:T(8,128)(2,1)} %get-tuple-element.20.e_ref, ...), custom_call_target="tpu_custom_call" | custom-call | flops 1610612736 | bytes 9437184 | tf_op jit(solution)/shard_map/proto_pass/pallas_call | solution.py:320
  65.4 2.0 %collective-permute-start.10 = (bf16[8,256,128]{2,1,0:T(8,128)(2,1)S(1)}, bf16[8,256,128]{2,1,0:T(8,128)(2,1)S(1)}, u32[]{:S(2)}, u32[]{:S(2)}) collective-permute-start(bf16[8,256,128]{2,1,0:T(8,128)(2,1)S(1)} %add_convert_fusion.1), channel_id=1, source_target_pairs={{0,128},{8,136},{16,144},{24,152},{32,160},{40,168},{48,176},{56,1... | collective-permute-start | bytes 1572872 | tf_op jit(solution)/shard_map/ppermute | solution.py:462
  67.4 12.5 %collective-permute-done.10 = bf16[8,256,128]{2,1,0:T(8,128)(2,1)S(1)} collective-permute-done((bf16[8,256,128]{2,1,0:T(8,128)(2,1)S(1)}, bf16[8,256,128]{2,1,0:T(8,128)(2,1)S(1)}, u32[]{:S(2)}, u32[]{:S(2)}) %collective-permute-start.10) | collective-permute-done | bytes 524320 | tf_op jit(solution)/shard_map/ppermute | solution.py:462
  81.3 20.5 %all_to_all.20.pieces_ref = bf16[8,256,128]{2,1,0:T(8,128)(2,1)S(1)} all-to-all(bf16[8,256,128]{2,1,0:T(8,128)(2,1)S(1)} %add_convert_fusion), channel_id=1, replica_groups={{0,16,32,48,64,80,96,112},{8,24,40,56,72,88,104,120},{128,144,160,176,1..., dimensions={0} | all-to-all | bytes 1048576 | tf_op jit(solution)/shard_map/all_to_all | solution.py:428
  102.6 3.5 %all-to-all-start.3 = ((bf16[8,256,128]{2,1,0:T(8,128)(2,1)}), bf16[8,256,128]{2,1,0:T(8,128)(2,1)S(1)}, u32[]{:S(2)}, u32[]{:S(2)}) async-start(bf16[8,256,128]{2,1,0:T(8,128)(2,1)} %final_pass.1), calls=%async_computation.3 | async-start | bytes 1048576 | tf_op jit(solution)/shard_map/all_to_all | solution.py:428
  107.4 5.8 %collective-permute-start.1 = (bf16[64,128]{1,0:T(8,128)(2,1)S(1)}, bf16[64,128]{1,0:T(8,128)(2,1)S(1)}, u32[]{:S(2)}, u32[]{:S(2)}) collective-permute-start(bf16[64,128]{1,0:T(8,128)(2,1)S(1)} %pad_maximum_fusion.3), channel_id=1, source_target_pairs={{0,64},{8,72},{16,80},{24,88},{32,96},{40,104},{48,112},{56,120},{... | collective-permute-start | bytes 49160 | tf_op jit(solution)/shard_map/ppermute | solution.py:432
  113.2 9.5 %collective-permute-done.1 = bf16[64,128]{1,0:T(8,128)(2,1)S(1)} collective-permute-done((bf16[64,128]{1,0:T(8,128)(2,1)S(1)}, bf16[64,128]{1,0:T(8,128)(2,1)S(1)}, u32[]{:S(2)}, u32[]{:S(2)}) %collective-permute-start.1) | collective-permute-done | bytes 16416 | tf_op jit(solution)/shard_map/ppermute | solution.py:432
  124.2 3.5 %collective-permute-done.2 = bf16[128,128]{1,0:T(8,128)(2,1)S(1)} collective-permute-done((bf16[128,128]{1,0:T(8,128)(2,1)S(1)}, bf16[128,128]{1,0:T(8,128)(2,1)S(1)}, u32[]{:S(2)}, u32[]{:S(2)}) %collective-permute-start.2) | collective-permute-done | bytes 32800 | tf_op jit(solution)/shard_map/ppermute | solution.py:432
  128.0 4.0 %collective-permute-done.3 = bf16[256,128]{1,0:T(8,128)(2,1)S(1)} collective-permute-done((bf16[256,128]{1,0:T(8,128)(2,1)S(1)}, bf16[256,128]{1,0:T(8,128)(2,1)S(1)}, u32[]{:S(2)}, u32[]{:S(2)}) %collective-permute-start.3) | collective-permute-done | bytes 65568 | tf_op jit(solution)/shard_map/ppermute | solution.py:432
  133.5 3.6 %collective-permute-done.4.other_ref = bf16[512,128]{1,0:T(8,128)(2,1)S(1)} collective-permute-done((bf16[512,128]{1,0:T(8,128)(2,1)S(1)}, bf16[512,128]{1,0:T(8,128)(2,1)S(1)}, u32[]{:S(2)}, u32[]{:S(2)}) %collective-permute-start.4) | collective-permute-done | bytes 131104 | tf_op jit(solution)/shard_map/ppermute | solution.py:470
  138.2 2.0 %collective-permute-start.5 = (f32[256,128]{1,0:T(8,128)S(1)}, f32[256,128]{1,0:T(8,128)S(1)}, u32[]{:S(2)}, u32[]{:S(2)}) collective-permute-start(f32[256,128]{1,0:T(8,128)S(1)} %row_pass.1), channel_id=1, source_target_pairs={{0,1},{1,0},{2,3},{3,2},{4,5},{5,4},{6,7},{7,6},{8,9},{9,8},{10,11... | collective-permute-start | bytes 393224 | tf_op jit(solution)/shard_map/ppermute | solution.py:437
  140.2 4.5 %collective-permute-done.5 = f32[256,128]{1,0:T(8,128)S(1)} collective-permute-done((f32[256,128]{1,0:T(8,128)S(1)}, f32[256,128]{1,0:T(8,128)S(1)}, u32[]{:S(2)}, u32[]{:S(2)}) %collective-permute-start.5) | collective-permute-done | bytes 131104 | tf_op jit(solution)/shard_map/ppermute | solution.py:437
  144.8 1.9 %collective-permute-start.6 = (f32[256,128]{1,0:T(8,128)S(1)}, f32[256,128]{1,0:T(8,128)S(1)}, u32[]{:S(2)}, u32[]{:S(2)}) collective-permute-start(f32[256,128]{1,0:T(8,128)S(1)} %add.23), channel_id=1, source_target_pairs={{0,4},{1,5},{2,6},{3,7},{4,0},{5,1},{6,2},{7,3},{8,12},{9,13},{10,... | collective-permute-start | bytes 393224 | tf_op jit(solution)/shard_map/ppermute | solution.py:437
  147.1 4.8 %collective-permute-done.6 = f32[256,128]{1,0:T(8,128)S(1)} collective-permute-done((f32[256,128]{1,0:T(8,128)S(1)}, f32[256,128]{1,0:T(8,128)S(1)}, u32[]{:S(2)}, u32[]{:S(2)}) %collective-permute-start.6) | collective-permute-done | bytes 131104 | tf_op jit(solution)/shard_map/ppermute | solution.py:437
  153.0 4.0 %collective-permute-done.7 = f32[256,128]{1,0:T(8,128)S(1)} collective-permute-done((f32[256,128]{1,0:T(8,128)S(1)}, f32[256,128]{1,0:T(8,128)S(1)}, u32[]{:S(2)}, u32[]{:S(2)}) %collective-permute-start.7) | collective-permute-done | bytes 131104 | tf_op jit(solution)/shard_map/ppermute | solution.py:437
  (55 shorter events, 21.2 us)
Async XLA Ops:
  0.6 13.5 %copy-start.8 = (s32[256]{0:T(256)S(1)}, s32[256]{0:T(256)}, u32[]{:S(2)}) copy-start(s32[256]{0:T(256)} %param.11) | copy-start | bytes 3076
  4.1 24.6 %all-to-all-start = ((bf16[32,48,128]{2,1,0:T(8,128)(2,1)}), bf16[32,48,128]{2,1,0:T(8,128)(2,1)S(1)}, u32[]{:S(2)}, u32[]{:S(2)}) async-start(bf16[32,48,128]{2,1,0:T(8,128)(2,1)} %mass_pass.1), calls=%async_computation | async-start | bytes 786432 | tf_op jit(solution)/shard_map/all_to_all | solution.py:428
  31.2 17.3 %all-to-all-start.1 = ((bf16[8,320,128]{2,1,0:T(8,128)(2,1)}), bf16[8,320,128]{2,1,0:T(8,128)(2,1)S(1)}, u32[]{:S(2)}, u32[]{:S(2)}) async-start(bf16[8,320,128]{2,1,0:T(8,128)(2,1)} %pick.1), calls=%async_computation.1 | async-start | bytes 1310720 | tf_op jit(solution)/shard_map/all_to_all | solution.py:428
  37.9 10.7 %copy-start.3 = (f32[4,256,128]{2,1,0:T(8,128)S(1)}, f32[4,256,128]{2,1,0:T(8,128)}, u32[]{:S(2)}) copy-start(f32[4,256,128]{2,1,0:T(8,128)} %get-tuple-element.22.cst_ref) | copy-start | bytes 1572868
  37.9 10.7 %copy-start.4 = (bf16[256,128]{1,0:T(8,128)(2,1)S(1)}, bf16[256,128]{1,0:T(8,128)(2,1)}, u32[]{:S(2)}) copy-start(bf16[256,128]{1,0:T(8,128)(2,1)} %tan_ref.5) | copy-start | bytes 196612
  37.9 10.7 %copy-start.7 = (bf16[256,128]{1,0:T(8,128)(2,1)S(1)}, bf16[256,128]{1,0:T(8,128)(2,1)}, u32[]{:S(2)}) copy-start(bf16[256,128]{1,0:T(8,128)(2,1)} %f_ref.3) | copy-start | bytes 196612
  56.1 2.1 %collective-permute-start.8 = (bf16[8,256,128]{2,1,0:T(8,128)(2,1)}, bf16[8,256,128]{2,1,0:T(8,128)(2,1)S(1)}, u32[]{:S(2)}, u32[]{:S(2)}) collective-permute-start(bf16[8,256,128]{2,1,0:T(8,128)(2,1)} %get-tuple-element.32), channel_id=1, source_target_pairs={{0,8},{8,0},{16,24},{24,16},{32,40},{40,32},{48,56},{56,48},{64,72... | collective-permute-start | bytes 1572872 | tf_op jit(solution)/shard_map/ppermute | solution.py:460
  65.2 2.2 %collective-permute-start.9 = (bf16[8,256,128]{2,1,0:T(8,128)(2,1)}, bf16[8,256,128]{2,1,0:T(8,128)(2,1)S(1)}, u32[]{:S(2)}, u32[]{:S(2)}) collective-permute-start(bf16[8,256,128]{2,1,0:T(8,128)(2,1)} %get-tuple-element.35), channel_id=1, source_target_pairs={{0,8},{8,0},{16,24},{24,16},{32,40},{40,32},{48,56},{56,48},{64,72... | collective-permute-start | bytes 1572872 | tf_op jit(solution)/shard_map/ppermute | solution.py:466
  65.4 14.5 %collective-permute-start.10 = (bf16[8,256,128]{2,1,0:T(8,128)(2,1)S(1)}, bf16[8,256,128]{2,1,0:T(8,128)(2,1)S(1)}, u32[]{:S(2)}, u32[]{:S(2)}) collective-permute-start(bf16[8,256,128]{2,1,0:T(8,128)(2,1)S(1)} %add_convert_fusion.1), channel_id=1, source_target_pairs={{0,128},{8,136},{16,144},{24,152},{32,160},{40,168},{48,176},{56,1... | collective-permute-start | bytes 1572872 | tf_op jit(solution)/shard_map/ppermute | solution.py:462
  81.2 55.8 %copy-start.2 = (f32[256,256]{1,0:T(8,128)S(1)}, f32[256,256]{1,0:T(8,128)}, u32[]{:S(2)}) copy-start(f32[256,256]{1,0:T(8,128)} %get-tuple-element.19.st_ref) | copy-start | bytes 786436
  81.3 55.8 %copy-start.5 = (f32[256,128]{1,0:T(8,128)S(1)}, f32[256,128]{1,0:T(8,128)}, u32[]{:S(2)}) copy-start(f32[256,128]{1,0:T(8,128)} %get-tuple-element.27.x_ref) | copy-start | bytes 393220
  81.3 55.8 %copy-start.6 = (f32[256,128]{1,0:T(8,128)S(1)}, f32[256,128]{1,0:T(8,128)}, u32[]{:S(2)}) copy-start(f32[256,128]{1,0:T(8,128)} %get-tuple-element.28.w_ref) | copy-start | bytes 393220
  102.6 20.0 %all-to-all-start.3 = ((bf16[8,256,128]{2,1,0:T(8,128)(2,1)}), bf16[8,256,128]{2,1,0:T(8,128)(2,1)S(1)}, u32[]{:S(2)}, u32[]{:S(2)}) async-start(bf16[8,256,128]{2,1,0:T(8,128)(2,1)} %final_pass.1), calls=%async_computation.3 | async-start | bytes 1048576 | tf_op jit(solution)/shard_map/all_to_all | solution.py:428
  106.1 1.3 collective-permute-start
  107.4 15.2 %collective-permute-start.1 = (bf16[64,128]{1,0:T(8,128)(2,1)S(1)}, bf16[64,128]{1,0:T(8,128)(2,1)S(1)}, u32[]{:S(2)}, u32[]{:S(2)}) collective-permute-start(bf16[64,128]{1,0:T(8,128)(2,1)S(1)} %pad_maximum_fusion.3), channel_id=1, source_target_pairs={{0,64},{8,72},{16,80},{24,88},{32,96},{40,104},{48,112},{56,120},{... | collective-permute-start | bytes 49160 | tf_op jit(solution)/shard_map/ppermute | solution.py:432
  122.6 5.1 %collective-permute-start.2 = (bf16[128,128]{1,0:T(8,128)(2,1)S(1)}, bf16[128,128]{1,0:T(8,128)(2,1)S(1)}, u32[]{:S(2)}, u32[]{:S(2)}) collective-permute-start(bf16[128,128]{1,0:T(8,128)(2,1)S(1)} %pad_maximum_fusion.2), channel_id=1, source_target_pairs={{0,32},{8,40},{16,48},{24,56},{32,0},{40,8},{48,16},{56,24},{64,96... | collective-permute-start | bytes 98312 | tf_op jit(solution)/shard_map/ppermute | solution.py:432
  122.6 24.0 %collective-permute-start.11 = (bf16[8,256,128]{2,1,0:T(8,128)(2,1)S(1)}, bf16[8,256,128]{2,1,0:T(8,128)(2,1)S(1)}, u32[]{:S(2)}, u32[]{:S(2)}) collective-permute-start(bf16[8,256,128]{2,1,0:T(8,128)(2,1)S(1)} %all-to-all-done.3.refs_0_), channel_id=1, source_target_pairs={{0,128},{8,136},{16,144},{24,152},{32,160},{40,168},{48,176},{56,1... | collective-permute-start | bytes 1572872 | tf_op jit(solution)/shard_map/ppermute | solution.py:476
  127.7 4.3 %collective-permute-start.3 = (bf16[256,128]{1,0:T(8,128)(2,1)S(1)}, bf16[256,128]{1,0:T(8,128)(2,1)S(1)}, u32[]{:S(2)}, u32[]{:S(2)}) collective-permute-start(bf16[256,128]{1,0:T(8,128)(2,1)S(1)} %pad_maximum_fusion.1), channel_id=1, source_target_pairs={{0,16},{8,24},{16,0},{24,8},{32,48},{40,56},{48,32},{56,40},{64,80... | collective-permute-start | bytes 196616 | tf_op jit(solution)/shard_map/ppermute | solution.py:432
  132.0 5.1 %collective-permute-start.4 = (bf16[512,128]{1,0:T(8,128)(2,1)S(1)}, bf16[512,128]{1,0:T(8,128)(2,1)S(1)}, u32[]{:S(2)}, u32[]{:S(2)}) collective-permute-start(bf16[512,128]{1,0:T(8,128)(2,1)S(1)} %pad_maximum_fusion.own_ref), channel_id=1, source_target_pairs={{0,128},{8,136},{16,144},{24,152},{32,160},{40,168},{48,176},{56,1... | collective-permute-start | bytes 393224 | tf_op jit(solution)/shard_map/ppermute | solution.py:470
  138.2 6.6 %collective-permute-start.5 = (f32[256,128]{1,0:T(8,128)S(1)}, f32[256,128]{1,0:T(8,128)S(1)}, u32[]{:S(2)}, u32[]{:S(2)}) collective-permute-start(f32[256,128]{1,0:T(8,128)S(1)} %row_pass.1), channel_id=1, source_target_pairs={{0,1},{1,0},{2,3},{3,2},{4,5},{5,4},{6,7},{7,6},{8,9},{9,8},{10,11... | collective-permute-start | bytes 393224 | tf_op jit(solution)/shard_map/ppermute | solution.py:437
  144.8 7.2 %collective-permute-start.6 = (f32[256,128]{1,0:T(8,128)S(1)}, f32[256,128]{1,0:T(8,128)S(1)}, u32[]{:S(2)}, u32[]{:S(2)}) collective-permute-start(f32[256,128]{1,0:T(8,128)S(1)} %add.23), channel_id=1, source_target_pairs={{0,4},{1,5},{2,6},{3,7},{4,0},{5,1},{6,2},{7,3},{8,12},{9,13},{10,... | collective-permute-start | bytes 393224 | tf_op jit(solution)/shard_map/ppermute | solution.py:437
  146.6 11.0 %collective-permute-start.13 = (bf16[8,256,128]{2,1,0:T(8,128)(2,1)S(1)}, bf16[8,256,128]{2,1,0:T(8,128)(2,1)S(1)}, u32[]{:S(2)}, u32[]{:S(2)}) collective-permute-start(bf16[8,256,128]{2,1,0:T(8,128)(2,1)S(1)} %all-to-all-done.3.refs_0_), channel_id=1, source_target_pairs={{0,8},{8,0},{16,24},{24,16},{32,40},{40,32},{48,56},{56,48},{64,72... | collective-permute-start | bytes 1572872 | tf_op jit(solution)/shard_map/ppermute | solution.py:482
  146.6 14.0 %collective-permute-start.12 = (bf16[8,256,128]{2,1,0:T(8,128)(2,1)S(1)}, bf16[8,256,128]{2,1,0:T(8,128)(2,1)S(1)}, u32[]{:S(2)}, u32[]{:S(2)}) collective-permute-start(bf16[8,256,128]{2,1,0:T(8,128)(2,1)S(1)} %collective-permute-done.11.refs_0_), channel_id=1, source_target_pairs={{0,8},{8,0},{16,24},{24,16},{32,40},{40,32},{48,56},{56,48},{64,72... | collective-permute-start | bytes 1572872 | tf_op jit(solution)/shard_map/ppermute | solution.py:484
  151.9 5.1 %collective-permute-start.7 = (f32[256,128]{1,0:T(8,128)S(1)}, f32[256,128]{1,0:T(8,128)S(1)}, u32[]{:S(2)}, u32[]{:S(2)}) collective-permute-start(f32[256,128]{1,0:T(8,128)S(1)} %add.24), channel_id=1, source_target_pairs={{0,2},{1,3},{2,0},{3,1},{4,6},{5,7},{6,4},{7,5},{8,10},{9,11},{10,... | collective-permute-start | bytes 393224 | tf_op jit(solution)/shard_map/ppermute | solution.py:437
  (2 other events, 1.8 us)

commit v6 on v5

--- a/solution.py
+++ b/solution.py
@@ -348,9 +348,7 @@
     total = pieces_ref[0].astype(F32)
     for i in range(1, 8):
         total = total + pieces_ref[i].astype(F32)
-    total = total.astype(BF16)
-    for i in range(8):
-        out_ref[i] = total
+    out_ref[...] = total.astype(BF16)
 
 
 def final_pass(pieces):
@@ -358,7 +356,7 @@
         final_kernel,
         in_specs=[VMEM],
         out_specs=VMEM,
-        out_shape=jax.ShapeDtypeStruct((8, ROWS, D), BF16),
+        out_shape=jax.ShapeDtypeStruct((ROWS, D), BF16),
         compiler_params=pltpu.CompilerParams(vmem_limit_bytes=8 * MB),
         name="final_pass",
     )(pieces)
@@ -389,15 +387,15 @@
     )(scalars, own, other, partner, x, w, st, gst)
 
 
-def place_kernel(count, s_ref, *refs):
+def place_kernel(pieces, s_ref, *refs):
     out_ref, sems = refs[-2], refs[-1]
     copies = []
-    for i in range(count):
-        for part in range(4):
+    for ref, (far, other, shifts) in zip(refs, pieces):
+        for i, shift in enumerate(shifts):
             copies.append(pltpu.make_async_copy(
-                refs[i].at[2 * part : 2 * part + 2],
-                out_ref.at[s_ref[0], 2 * part : 2 * part + 2, s_ref[1 + i]],
-                sems.at[4 * i + part],
+                ref.at[i],
+                out_ref.at[s_ref[0] ^ far, (s_ref[1] + (8 - shift)) & 7, s_ref[2] ^ other],
+                sems.at[len(copies)],
             ))
     for copy in copies:
         copy.start()
@@ -405,14 +403,15 @@
         copy.wait()
 
 
-def place(scalars, blocks, whole):
+def place(scalars, pieces, blocks, whole):
     rest = () if whole is None else (whole,)
-    return pl.pallas_call(
-        functools.partial(place_kernel, len(blocks)),
+    count = sum(len(piece[2]) for piece in pieces)
+    return pl.pallas_call(
+        functools.partial(place_kernel, pieces),
         in_specs=[SMEM] + [VMEM] * len(blocks) + [HBM] * len(rest),
         out_specs=HBM,
         out_shape=jax.ShapeDtypeStruct((2, 8, 2, ROWS, D), BF16),
-        scratch_shapes=[pltpu.SemaphoreType.DMA((8,))],
+        scratch_shapes=[pltpu.SemaphoreType.DMA((count,))],
         input_output_aliases={1 + len(blocks): 0} if rest else {},
         compiler_params=pltpu.CompilerParams(vmem_limit_bytes=4 * MB),
         name="place",
@@ -421,6 +420,8 @@
 
 CORE_PERM = [(i, i ^ 1) for i in range(DP)]
 Y_PERM = [(i, i ^ 16) for i in range(DP)]
+Z_PERMS = {k: [(i, (i & 17) | (((i >> 1) + k) % 8) << 1) for i in range(DP)] for k in range(1, 8)}
+SHIFTS = ((0,), (4, 3, 5), (2, 6), (1, 7))
 Z_GROUPS = [[y * 16 + z * 2 + c for z in range(8)] for y in range(2) for c in range(2)]
 
 
@@ -431,6 +432,10 @@
 def doubled(x, bit):
     other = lax.ppermute(x, "dp", [(i, i ^ bit) for i in range(DP)])
     return lax.optimization_barrier(jnp.concatenate([x, other], axis=0))
+
+
+def along(x, perm):
+    return lax.ppermute(x, "dp", perm)
 
 
 def swap(x, bit):
@@ -471,19 +476,27 @@
     embed = row_pass(jnp.stack([q, dp]), table, other, partner, x, w, st, gst)
     final = final_pass(pieces)
 
-    swapped = swap(embed, 1)
-    along_z = exchange(final, "dp", Z_GROUPS)
-    from_y = lax.ppermute(along_z, "dp", Y_PERM)
-    embed = embed + swapped
-    swapped = swap(embed, 4)
-    embed = embed + swapped
-    swapped = swap(embed, 2)
-    hvp_embed = (embed + swapped).astype(BF16)
-    own_core = lax.ppermute(along_z, "dp", CORE_PERM)
-    whole = place(jnp.stack([y, core, 1 - core]), (along_z, own_core), None)
-    far_core = lax.ppermute(from_y, "dp", CORE_PERM)
-    whole = place(jnp.stack([1 - y, core]), (from_y,), whole)
-    whole = place(jnp.stack([1 - y, 1 - core]), (far_core,), whole)
+    first = swap(embed, 1)
+    groups = [final[None]]
+    for shifts in SHIFTS[1:]:
+        group = [along(final, Z_PERMS[k]) for k in shifts]
+        groups.append(lax.optimization_barrier(jnp.stack(group)))
+    across = [along(group, Y_PERM) for group in groups]
+    embed = embed + first
+    second = swap(embed, 4)
+    embed = embed + second
+    third = swap(embed, 2)
+    hvp_embed = (embed + third).astype(BF16)
+    own_core = [along(group, CORE_PERM) for group in groups]
+    far_core = [along(group, CORE_PERM) for group in across]
+    pieces, blocks = [], []
+    for i, shifts in enumerate(SHIFTS):
+        pieces += [(0, 0, shifts), (0, 1, shifts), (1, 0, shifts), (1, 1, shifts)]
+        blocks += [groups[i], own_core[i], across[i], far_core[i]]
+    where = jnp.stack([y, (dp // 2) % 8, core])
+    early = 14
+    whole = place(where, pieces[:early], blocks[:early], None)
+    whole = place(where, pieces[early:], blocks[early:], whole)
     return (hvp_embed, whole.reshape(LOCAL, D))
 
 

time: 163 us -> 168 us (1.031)
  blocking collectives: 20.5 us -> 0 us
  starting transfers between devices: 36.1 us -> 50.3 us
  waiting for transfers between devices: 56.8 us -> 67.7 us
  Pallas kernels: 41.6 us -> 39.7 us
    all_to_all x1 -> x0, blocking collectives: 20.5 us -> none  [exchange(): return lax.all_to_all(x, axis, 0, 0, axis_index_groups=groups, tiled=True)]
    ppermute x3 -> x19, starting transfers between devices: 2.07 us -> 17.7 us  [along(): return lax.ppermute(x, 'dp', perm)]
    ppermute x3 -> x19, waiting for transfers between devices: 0.01 us -> 14.7 us  [along(): return lax.ppermute(x, 'dp', perm)]
    ppermute x3, waiting for transfers between devices: 13.3 us -> 6.26 us  [swap(): return lax.ppermute(x, 'proto', [(i, i ^ bit) for i in range(PR)])]
    ppermute x4, waiting for transfers between devices: 18.2 us -> 21.7 us  [doubled(): other = lax.ppermute(x, 'dp', [(i, i ^ bit) for i in range(DP)])]
    pallas_call x3 -> x2, Pallas kernels: 4.37 us -> 3.27 us  [place(): pl.pallas_call(functools.partial(place_kernel, pieces), in_specs=[SMEM] +...]
  transfers between devices with their start and end apart: 17 -> 33, of which waited for: 12 -> 21; matrix products, arithmetic and copies ran while one was open for 1% -> 1% of each run, Pallas kernels for 14% -> 13%
where the time goes in v6:
time: 168 us; the launch traced here: 166 us
  waiting for transfers between devices  67.7 us (40%)
  starting transfers between devices  50.3 us (30%)
  Pallas kernels  39.7 us (24%)
  other arithmetic  5.09 us (3%)
  local copies, waits for them, and re-layouts  1.94 us (1%)
    ppermute x4, waiting for transfers between devices, doubled(): other = lax.ppermute(x, 'dp', [(i, i ^ bit) for i in range(DP)])  21.7 us
    all_to_all x3, starting transfers between devices, exchange(): return lax.all_to_all(x, axis, 0, 0, axis_index_groups=groups, tiled=True)  19.6 us
    ppermute x19, starting transfers between devices, along(): return lax.ppermute(x, 'dp', perm)  17.7 us
    ppermute x19, waiting for transfers between devices, along(): return lax.ppermute(x, 'dp', perm)  14.7 us
    ppermute x1, waiting for transfers between devices, inner(): from_far = lax.ppermute(to_y, 'dp', Y_PERM)  12.5 us
    pallas_call x2, Pallas kernels, proto_pass(): pl.pallas_call(proto_kernel, grid_spec=pltpu.PrefetchScalarGridSpec(num_s...  11.3 us
    pallas_call x1, Pallas kernels, score_pass(): pl.pallas_call(score_kernel, grid=(NCH,), in_specs=[pl.BlockSpec((ROWS, D...  10.3 us
    pallas_call x1, Pallas kernels, embed_pass(): pl.pallas_call(embed_kernel, grid=(NCH,), in_specs=[pl.BlockSpec((ROWS, C...  7.61 us
  transfers between devices with their start and end apart: 33, of which 21 were waited for; matrix products, arithmetic and copies ran while one was open for 1% of the time, Pallas kernels for 13%

profile of v6, /device:TPU:8, one launch (start us, length us, event | category | flops | bytes accessed | tf_op | source)
XLA Modules:
  0.0 165.8 jit_solution(12827100469935460912)
XLA Ops:
  0.6 3.4 %mass_pass.1 = bf16[32,48,128]{2,1,0:T(8,128)(2,1)} custom-call(s32[1]{0:T(128)} %bitcast.q_ref, bf16[256,8192]{1,0:T(8,128)(2,1)} %codes_ref.7, bf16[256,128]{1,0:T(8,128)(2,1)} %tan_ref.5), custom_call_target="tpu_custom_call" | custom-call | flops 2097152 | bytes 5242880 | tf_op jit(solution)/shard_map/mass_pass/pallas_call | solution.py:71
  4.1 10.1 %all-to-all-start = ((bf16[32,48,128]{2,1,0:T(8,128)(2,1)}), bf16[32,48,128]{2,1,0:T(8,128)(2,1)S(1)}, u32[]{:S(2)}, u32[]{:S(2)}) async-start(bf16[32,48,128]{2,1,0:T(8,128)(2,1)} %mass_pass.1), calls=%async_computation | async-start | bytes 786432 | tf_op jit(solution)/shard_map/all_to_all | solution.py:429
  14.3 10.3 %score_pass.1 = (bf16[256,8192]{1,0:T(8,128)(2,1)}, bf16[256,8192]{1,0:T(8,128)(2,1)}, f32[4,256,128]{2,1,0:T(8,128)}, f32[256,256]{1,0:T(8,128)}) custom-call(bf16[256,128]{1,0:T(8,128)(2,1)} %f_ref.3, bf16[256,128]{1,0:T(8,128)(2,1)} %tan_ref.5, bf16[8192,128]{1,0:T(8,128)(2,1)} %a_ref.3, bf16[8192,128]{1,0:T(8,128)(2,1)} %p_ref.3, bf16[256,8192]{1,0:T(8,128)(2,1)} %codes_ref.7), custom_call_target="tpu_custom_call" | custom-call | flops 5368709120 | bytes 12582912 | tf_op jit(solution)/shard_map/score_pass/pallas_call | solution.py:132
  24.6 4.1 %all-to-all-done.tab_ref = bf16[32,48,128]{2,1,0:T(8,128)(2,1)S(1)} async-done(((bf16[32,48,128]{2,1,0:T(8,128)(2,1)}), bf16[32,48,128]{2,1,0:T(8,128)(2,1)S(1)}, u32[]{:S(2)}, u32[]{:S(2)}) %all-to-all-start) | async-done | bytes 393248 | tf_op jit(solution)/shard_map/all_to_all | solution.py:429
  31.2 6.0 %all-to-all-start.1 = ((bf16[8,320,128]{2,1,0:T(8,128)(2,1)}), bf16[8,320,128]{2,1,0:T(8,128)(2,1)S(1)}, u32[]{:S(2)}, u32[]{:S(2)}) async-start(bf16[8,320,128]{2,1,0:T(8,128)(2,1)} %pick.1), calls=%async_computation.1 | async-start | bytes 1310720 | tf_op jit(solution)/shard_map/all_to_all | solution.py:429
  37.9 7.6 %embed_pass.1 = (f32[256,128]{1,0:T(8,128)}, f32[256,128]{1,0:T(8,128)}) custom-call(bf16[256,8192]{1,0:T(8,128)(2,1)} %get-tuple-element.20.e_ref, bf16[256,8192]{1,0:T(8,128)(2,1)} %get-tuple-element.21.u_ref, bf16[8192,128]{1,0:T(8,128)(2,1)} %a_ref.3, bf16[8192,128]{1,0:T(8,128)(2,1)} %p_ref.3, f32[4,256,128]{2,1,0:T(8,128)} %get-tuple-element.22.cst_ref, ...), custom_call_target="tpu_custom_call" | custom-call | flops 3221225472 | bytes 12582912 | tf_op jit(solution)/shard_map/embed_pass/pallas_call | solution.py:183
  45.5 3.0 %all-to-all-done.1.rec_ref = bf16[8,320,128]{2,1,0:T(8,128)(2,1)S(1)} async-done(((bf16[8,320,128]{2,1,0:T(8,128)(2,1)}), bf16[8,320,128]{2,1,0:T(8,128)(2,1)S(1)}, u32[]{:S(2)}, u32[]{:S(2)}) %all-to-all-start.1) | async-done | bytes 655392 | tf_op jit(solution)/shard_map/all_to_all | solution.py:429
  50.4 5.7 %proto_pass.2 = (f32[8,256,128]{2,1,0:T(8,128)}, bf16[8,256,128]{2,1,0:T(8,128)(2,1)}) custom-call(s32[2]{0:T(128)} %get-tuple-element.37.s_ref, bf16[9,256,128]{2,1,0:T(8,128)(2,1)} %copy-done, bf16[9,256,128]{2,1,0:T(8,128)(2,1)} %copy-done, bf16[256,8192]{1,0:T(8,128)(2,1)} %get-tuple-element.21.u_ref, bf16[256,8192]{1,0:T(8,128)(2,1)} %get-tuple-element.20.e_ref, ...), custom_call_target="tpu_custom_call" | custom-call | flops 1610612736 | bytes 9437184 | tf_op jit(solution)/shard_map/proto_pass/pallas_call | solution.py:320
  59.5 5.7 %proto_pass.3 = (f32[8,256,128]{2,1,0:T(8,128)}, bf16[8,256,128]{2,1,0:T(8,128)(2,1)}) custom-call(s32[2]{0:T(128)} %get-tuple-element.36.s_ref, bf16[9,256,128]{2,1,0:T(8,128)(2,1)} %copy-done, bf16[9,256,128]{2,1,0:T(8,128)(2,1)} %copy-done, bf16[256,8192]{1,0:T(8,128)(2,1)} %get-tuple-element.21.u_ref, bf16[256,8192]{1,0:T(8,128)(2,1)} %get-tuple-element.20.e_ref, ...), custom_call_target="tpu_custom_call" | custom-call | flops 1610612736 | bytes 9437184 | tf_op jit(solution)/shard_map/proto_pass/pallas_call | solution.py:320
  67.4 12.5 %collective-permute-done.10 = bf16[8,256,128]{2,1,0:T(8,128)(2,1)S(1)} collective-permute-done((bf16[8,256,128]{2,1,0:T(8,128)(2,1)S(1)}, bf16[8,256,128]{2,1,0:T(8,128)(2,1)S(1)}, u32[]{:S(2)}, u32[]{:S(2)}) %collective-permute-start.10) | collective-permute-done | bytes 524320 | tf_op jit(solution)/shard_map/ppermute | solution.py:467
  79.9 2.2 %add_convert_fusion = bf16[8,256,128]{2,1,0:T(8,128)(2,1)} fusion(bf16[8,256,128]{2,1,0:T(8,128)(2,1)S(1)} %collective-permute-done.10, f32[8,256,128]{2,1,0:T(8,128)} %get-tuple-element.34, bf16[8,256,128]{2,1,0:T(8,128)(2,1)S(1)} %collective-permute-done.9), kind=kLoop, calls=%fused_computation | loop fusion | flops 1310720 | bytes 2621440 | tf_op jit(solution)/shard_map/convert_element_type | solution.py:473
  82.1 3.5 %all-to-all-start.2 = ((bf16[8,256,128]{2,1,0:T(8,128)(2,1)}), bf16[8,256,128]{2,1,0:T(8,128)(2,1)S(1)}, u32[]{:S(2)}, u32[]{:S(2)}) async-start(bf16[8,256,128]{2,1,0:T(8,128)(2,1)} %add_convert_fusion), calls=%async_computation.2 | async-start | bytes 1048576 | tf_op jit(solution)/shard_map/all_to_all | solution.py:429
  86.9 5.8 %collective-permute-start.1 = (bf16[64,128]{1,0:T(8,128)(2,1)S(1)}, bf16[64,128]{1,0:T(8,128)(2,1)S(1)}, u32[]{:S(2)}, u32[]{:S(2)}) collective-permute-start(bf16[64,128]{1,0:T(8,128)(2,1)S(1)} %pad_maximum_fusion.6), channel_id=1, source_target_pairs={{0,64},{8,72},{16,80},{24,88},{32,96},{40,104},{48,112},{56,120},{... | collective-permute-start | bytes 49160 | tf_op jit(solution)/shard_map/ppermute | solution.py:433
  92.6 11.3 %collective-permute-done.1 = bf16[64,128]{1,0:T(8,128)(2,1)S(1)} collective-permute-done((bf16[64,128]{1,0:T(8,128)(2,1)S(1)}, bf16[64,128]{1,0:T(8,128)(2,1)S(1)}, u32[]{:S(2)}, u32[]{:S(2)}) %collective-permute-start.1) | collective-permute-done | bytes 16416 | tf_op jit(solution)/shard_map/ppermute | solution.py:433
  104.0 5.1 %collective-permute-done.2 = bf16[128,128]{1,0:T(8,128)(2,1)S(1)} collective-permute-done((bf16[128,128]{1,0:T(8,128)(2,1)S(1)}, bf16[128,128]{1,0:T(8,128)(2,1)S(1)}, u32[]{:S(2)}, u32[]{:S(2)}) %collective-permute-start.2) | collective-permute-done | bytes 32800 | tf_op jit(solution)/shard_map/ppermute | solution.py:433
  109.4 4.0 %collective-permute-done.3 = bf16[256,128]{1,0:T(8,128)(2,1)S(1)} collective-permute-done((bf16[256,128]{1,0:T(8,128)(2,1)S(1)}, bf16[256,128]{1,0:T(8,128)(2,1)S(1)}, u32[]{:S(2)}, u32[]{:S(2)}) %collective-permute-start.3) | collective-permute-done | bytes 65568 | tf_op jit(solution)/shard_map/ppermute | solution.py:433
  115.0 3.4 %collective-permute-done.4.other_ref = bf16[512,128]{1,0:T(8,128)(2,1)S(1)} collective-permute-done((bf16[512,128]{1,0:T(8,128)(2,1)S(1)}, bf16[512,128]{1,0:T(8,128)(2,1)S(1)}, u32[]{:S(2)}, u32[]{:S(2)}) %collective-permute-start.4) | collective-permute-done | bytes 131104 | tf_op jit(solution)/shard_map/ppermute | solution.py:475
  121.0 5.2 %collective-permute-done.5 = f32[256,128]{1,0:T(8,128)S(1)} collective-permute-done((f32[256,128]{1,0:T(8,128)S(1)}, f32[256,128]{1,0:T(8,128)S(1)}, u32[]{:S(2)}, u32[]{:S(2)}) %collective-permute-start.5) | collective-permute-done | bytes 131104 | tf_op jit(solution)/shard_map/ppermute | solution.py:442
  127.8 3.8 %collective-permute-start.19 = (bf16[256,128]{1,0:T(8,128)(2,1)S(1)}, bf16[256,128]{1,0:T(8,128)(2,1)S(1)}, u32[]{:S(2)}, u32[]{:S(2)}) collective-permute-start(bf16[256,128]{1,0:T(8,128)(2,1)S(1)} %final_pass.1), channel_id=1, source_target_pairs={{0,48},{8,56},{16,64},{24,72},{32,80},{40,88},{48,96},{56,104},{64... | collective-permute-start | bytes 196616 | tf_op jit(solution)/shard_map/ppermute | solution.py:438
  136.1 2.3 %collective-permute-start.25 = (bf16[256,128]{1,0:T(8,128)(2,1)S(1)}, bf16[256,128]{1,0:T(8,128)(2,1)S(1)}, u32[]{:S(2)}, u32[]{:S(2)}) collective-permute-start(bf16[256,128]{1,0:T(8,128)(2,1)S(1)} %final_pass.1), channel_id=1, source_target_pairs={{0,96},{8,104},{16,112},{24,120},{32,0},{40,8},{48,16},{56,24},{64... | collective-permute-start | bytes 196616 | tf_op jit(solution)/shard_map/ppermute | solution.py:438
  140.7 2.7 %collective-permute-done.25 = bf16[256,128]{1,0:T(8,128)(2,1)S(1)} collective-permute-done((bf16[256,128]{1,0:T(8,128)(2,1)S(1)}, bf16[256,128]{1,0:T(8,128)(2,1)S(1)}, u32[]{:S(2)}, u32[]{:S(2)}) %collective-permute-start.25) | collective-permute-done | bytes 65568 | tf_op jit(solution)/shard_map/ppermute | solution.py:438
  146.4 2.2 %collective-permute-start.11 = (bf16[256,128]{1,0:T(8,128)(2,1)S(1)}, bf16[256,128]{1,0:T(8,128)(2,1)S(1)}, u32[]{:S(2)}, u32[]{:S(2)}) collective-permute-start(bf16[256,128]{1,0:T(8,128)(2,1)S(1)} %final_pass.1), channel_id=1, source_target_pairs={{0,16},{8,24},{16,32},{24,40},{32,48},{40,56},{48,64},{56,72},{64,... | collective-permute-start | bytes 196616 | tf_op jit(solution)/shard_map/ppermute | solution.py:438
  155.9 2.6 %collective-permute-done.13.refs_0_ = bf16[2,256,128]{2,1,0:T(8,128)(2,1)S(1)} collective-permute-done((bf16[2,256,128]{2,1,0:T(8,128)(2,1)S(1)}, bf16[2,256,128]{2,1,0:T(8,128)(2,1)S(1)}, u32[]{:S(2)}, u32[]{:S(2)}) %collective-permute-start.13) | collective-permute-done | bytes 131104 | tf_op jit(solution)/shard_map/ppermute | solution.py:438
  158.5 2.2 %collective-permute-done.27.refs_10_ = bf16[2,256,128]{2,1,0:T(8,128)(2,1)S(1)} collective-permute-done((bf16[2,256,128]{2,1,0:T(8,128)(2,1)S(1)}, bf16[2,256,128]{2,1,0:T(8,128)(2,1)S(1)}, u32[]{:S(2)}, u32[]{:S(2)}) %collective-permute-start.27) | collective-permute-done | bytes 131104 | tf_op jit(solution)/shard_map/ppermute | solution.py:438
  (87 shorter events, 40.1 us)
Async XLA Ops:
  4.1 24.6 %all-to-all-start = ((bf16[32,48,128]{2,1,0:T(8,128)(2,1)}), bf16[32,48,128]{2,1,0:T(8,128)(2,1)S(1)}, u32[]{:S(2)}, u32[]{:S(2)}) async-start(bf16[32,48,128]{2,1,0:T(8,128)(2,1)} %mass_pass.1), calls=%async_computation | async-start | bytes 786432 | tf_op jit(solution)/shard_map/all_to_all | solution.py:429
  31.2 17.3 %all-to-all-start.1 = ((bf16[8,320,128]{2,1,0:T(8,128)(2,1)}), bf16[8,320,128]{2,1,0:T(8,128)(2,1)S(1)}, u32[]{:S(2)}, u32[]{:S(2)}) async-start(bf16[8,320,128]{2,1,0:T(8,128)(2,1)} %pick.1), calls=%async_computation.1 | async-start | bytes 1310720 | tf_op jit(solution)/shard_map/all_to_all | solution.py:429
  65.4 14.5 %collective-permute-start.10 = (bf16[8,256,128]{2,1,0:T(8,128)(2,1)S(1)}, bf16[8,256,128]{2,1,0:T(8,128)(2,1)S(1)}, u32[]{:S(2)}, u32[]{:S(2)}) collective-permute-start(bf16[8,256,128]{2,1,0:T(8,128)(2,1)S(1)} %add_convert_fusion.1), channel_id=1, source_target_pairs={{0,128},{8,136},{16,144},{24,152},{32,160},{40,168},{48,176},{56,1... | collective-permute-start | bytes 1572872 | tf_op jit(solution)/shard_map/ppermute | solution.py:467
  82.1 45.5 %all-to-all-start.2 = ((bf16[8,256,128]{2,1,0:T(8,128)(2,1)}), bf16[8,256,128]{2,1,0:T(8,128)(2,1)S(1)}, u32[]{:S(2)}, u32[]{:S(2)}) async-start(bf16[8,256,128]{2,1,0:T(8,128)(2,1)} %add_convert_fusion), calls=%async_computation.2 | async-start | bytes 1048576 | tf_op jit(solution)/shard_map/all_to_all | solution.py:429
  86.9 17.1 %collective-permute-start.1 = (bf16[64,128]{1,0:T(8,128)(2,1)S(1)}, bf16[64,128]{1,0:T(8,128)(2,1)S(1)}, u32[]{:S(2)}, u32[]{:S(2)}) collective-permute-start(bf16[64,128]{1,0:T(8,128)(2,1)S(1)} %pad_maximum_fusion.6), channel_id=1, source_target_pairs={{0,64},{8,72},{16,80},{24,88},{32,96},{40,104},{48,112},{56,120},{... | collective-permute-start | bytes 49160 | tf_op jit(solution)/shard_map/ppermute | solution.py:433
  104.0 5.1 %collective-permute-start.2 = (bf16[128,128]{1,0:T(8,128)(2,1)S(1)}, bf16[128,128]{1,0:T(8,128)(2,1)S(1)}, u32[]{:S(2)}, u32[]{:S(2)}) collective-permute-start(bf16[128,128]{1,0:T(8,128)(2,1)S(1)} %pad_maximum_fusion.5), channel_id=1, source_target_pairs={{0,32},{8,40},{16,48},{24,56},{32,0},{40,8},{48,16},{56,24},{64,96... | collective-permute-start | bytes 98312 | tf_op jit(solution)/shard_map/ppermute | solution.py:433
  119.6 6.6 %collective-permute-start.5 = (f32[256,128]{1,0:T(8,128)S(1)}, f32[256,128]{1,0:T(8,128)S(1)}, u32[]{:S(2)}, u32[]{:S(2)}) collective-permute-start(f32[256,128]{1,0:T(8,128)S(1)} %row_pass.1), channel_id=1, source_target_pairs={{0,1},{1,0},{2,3},{3,2},{4,5},{5,4},{6,7},{7,6},{8,9},{9,8},{10,11... | collective-permute-start | bytes 393224 | tf_op jit(solution)/shard_map/ppermute | solution.py:442
  126.2 7.4 %collective-permute-start.6 = (f32[256,128]{1,0:T(8,128)S(1)}, f32[256,128]{1,0:T(8,128)S(1)}, u32[]{:S(2)}, u32[]{:S(2)}) collective-permute-start(f32[256,128]{1,0:T(8,128)S(1)} %add.27), channel_id=1, source_target_pairs={{0,4},{1,5},{2,6},{3,7},{4,0},{5,1},{6,2},{7,3},{8,12},{9,13},{10,... | collective-permute-start | bytes 393224 | tf_op jit(solution)/shard_map/ppermute | solution.py:442
  127.7 8.0 %collective-permute-start.20 = (bf16[256,128]{1,0:T(8,128)(2,1)S(1)}, bf16[256,128]{1,0:T(8,128)(2,1)S(1)}, u32[]{:S(2)}, u32[]{:S(2)}) collective-permute-start(bf16[256,128]{1,0:T(8,128)(2,1)S(1)} %final_pass.1), channel_id=1, source_target_pairs={{0,80},{8,88},{16,96},{24,104},{32,112},{40,120},{48,0},{56,8},{64... | collective-permute-start | bytes 196616 | tf_op jit(solution)/shard_map/ppermute | solution.py:438
  127.8 8.3 %collective-permute-start.19 = (bf16[256,128]{1,0:T(8,128)(2,1)S(1)}, bf16[256,128]{1,0:T(8,128)(2,1)S(1)}, u32[]{:S(2)}, u32[]{:S(2)}) collective-permute-start(bf16[256,128]{1,0:T(8,128)(2,1)S(1)} %final_pass.1), channel_id=1, source_target_pairs={{0,48},{8,56},{16,64},{24,72},{32,80},{40,88},{48,96},{56,104},{64... | collective-permute-start | bytes 196616 | tf_op jit(solution)/shard_map/ppermute | solution.py:438
  131.6 8.2 %collective-permute-start.18 = (bf16[256,128]{1,0:T(8,128)(2,1)S(1)}, bf16[256,128]{1,0:T(8,128)(2,1)S(1)}, u32[]{:S(2)}, u32[]{:S(2)}) collective-permute-start(bf16[256,128]{1,0:T(8,128)(2,1)S(1)} %final_pass.1), channel_id=1, source_target_pairs={{0,64},{8,72},{16,80},{24,88},{32,96},{40,104},{48,112},{56,120},{... | collective-permute-start | bytes 196616 | tf_op jit(solution)/shard_map/ppermute | solution.py:438
  133.6 18.4 %collective-permute-start.7 = (f32[256,128]{1,0:T(8,128)S(1)}, f32[256,128]{1,0:T(8,128)S(1)}, u32[]{:S(2)}, u32[]{:S(2)}) collective-permute-start(f32[256,128]{1,0:T(8,128)S(1)} %add.28), channel_id=1, source_target_pairs={{0,2},{1,3},{2,0},{3,1},{4,6},{5,7},{6,4},{7,5},{8,10},{9,11},{10,... | collective-permute-start | bytes 393224 | tf_op jit(solution)/shard_map/ppermute | solution.py:442
  133.9 19.4 %collective-permute-start.16 = (bf16[1,256,128]{2,1,0:T(8,128)(2,1)S(1)}, bf16[1,256,128]{2,1,0:T(8,128)(2,1)S(1)}, u32[]{:S(2)}, u32[]{:S(2)}) collective-permute-start(bf16[1,256,128]{2,1,0:T(8,128)(2,1)S(1)} %bitcast.16), channel_id=1, source_target_pairs={{0,128},{8,136},{16,144},{24,152},{32,160},{40,168},{48,176},{56,1... | collective-permute-start | bytes 196616 | tf_op jit(solution)/shard_map/ppermute | solution.py:438
  135.6 18.5 %collective-permute-start.15 = (bf16[1,256,128]{2,1,0:T(8,128)(2,1)S(1)}, bf16[1,256,128]{2,1,0:T(8,128)(2,1)S(1)}, u32[]{:S(2)}, u32[]{:S(2)}) collective-permute-start(bf16[1,256,128]{2,1,0:T(8,128)(2,1)S(1)} %bitcast.17), channel_id=1, source_target_pairs={{0,8},{8,0},{16,24},{24,16},{32,40},{40,32},{48,56},{56,48},{64,72... | collective-permute-start | bytes 196616 | tf_op jit(solution)/shard_map/ppermute | solution.py:438
  136.1 7.4 %collective-permute-start.25 = (bf16[256,128]{1,0:T(8,128)(2,1)S(1)}, bf16[256,128]{1,0:T(8,128)(2,1)S(1)}, u32[]{:S(2)}, u32[]{:S(2)}) collective-permute-start(bf16[256,128]{1,0:T(8,128)(2,1)S(1)} %final_pass.1), channel_id=1, source_target_pairs={{0,96},{8,104},{16,112},{24,120},{32,0},{40,8},{48,16},{56,24},{64... | collective-permute-start | bytes 196616 | tf_op jit(solution)/shard_map/ppermute | solution.py:438
  139.7 6.7 %collective-permute-start.24 = (bf16[256,128]{1,0:T(8,128)(2,1)S(1)}, bf16[256,128]{1,0:T(8,128)(2,1)S(1)}, u32[]{:S(2)}, u32[]{:S(2)}) collective-permute-start(bf16[256,128]{1,0:T(8,128)(2,1)S(1)} %final_pass.1), channel_id=1, source_target_pairs={{0,32},{8,40},{16,48},{24,56},{32,64},{40,72},{48,80},{56,88},{64,... | collective-permute-start | bytes 196616 | tf_op jit(solution)/shard_map/ppermute | solution.py:438
  143.5 5.1 %collective-permute-start.12 = (bf16[256,128]{1,0:T(8,128)(2,1)S(1)}, bf16[256,128]{1,0:T(8,128)(2,1)S(1)}, u32[]{:S(2)}, u32[]{:S(2)}) collective-permute-start(bf16[256,128]{1,0:T(8,128)(2,1)S(1)} %final_pass.1), channel_id=1, source_target_pairs={{0,112},{8,120},{16,0},{24,8},{32,16},{40,24},{48,32},{56,40},{64,... | collective-permute-start | bytes 196616 | tf_op jit(solution)/shard_map/ppermute | solution.py:438
  146.4 5.5 %collective-permute-start.11 = (bf16[256,128]{1,0:T(8,128)(2,1)S(1)}, bf16[256,128]{1,0:T(8,128)(2,1)S(1)}, u32[]{:S(2)}, u32[]{:S(2)}) collective-permute-start(bf16[256,128]{1,0:T(8,128)(2,1)S(1)} %final_pass.1), channel_id=1, source_target_pairs={{0,16},{8,24},{16,32},{24,40},{32,48},{40,56},{48,64},{56,72},{64,... | collective-permute-start | bytes 196616 | tf_op jit(solution)/shard_map/ppermute | solution.py:438
  148.6 12.1 %collective-permute-start.22 = (bf16[3,256,128]{2,1,0:T(8,128)(2,1)S(1)}, bf16[3,256,128]{2,1,0:T(8,128)(2,1)S(1)}, u32[]{:S(2)}, u32[]{:S(2)}) collective-permute-start(bf16[3,256,128]{2,1,0:T(8,128)(2,1)S(1)} %pad_maximum_fusion.refs_4_), channel_id=1, source_target_pairs={{0,128},{8,136},{16,144},{24,152},{32,160},{40,168},{48,176},{56,1... | collective-permute-start | bytes 589832 | tf_op jit(solution)/shard_map/ppermute | solution.py:438
  152.0 6.5 %collective-permute-start.13 = (bf16[2,256,128]{2,1,0:T(8,128)(2,1)S(1)}, bf16[2,256,128]{2,1,0:T(8,128)(2,1)S(1)}, u32[]{:S(2)}, u32[]{:S(2)}) collective-permute-start(bf16[2,256,128]{2,1,0:T(8,128)(2,1)S(1)} %pad_maximum_fusion.2.refs_12_), channel_id=1, source_target_pairs={{0,128},{8,136},{16,144},{24,152},{32,160},{40,168},{48,176},{56,1... | collective-permute-start | bytes 393224 | tf_op jit(solution)/shard_map/ppermute | solution.py:438
  153.3 7.4 %collective-permute-start.27 = (bf16[2,256,128]{2,1,0:T(8,128)(2,1)S(1)}, bf16[2,256,128]{2,1,0:T(8,128)(2,1)S(1)}, u32[]{:S(2)}, u32[]{:S(2)}) collective-permute-start(bf16[2,256,128]{2,1,0:T(8,128)(2,1)S(1)} %pad_maximum_fusion.3.refs_8_), channel_id=1, source_target_pairs={{0,128},{8,136},{16,144},{24,152},{32,160},{40,168},{48,176},{56,1... | collective-permute-start | bytes 393224 | tf_op jit(solution)/shard_map/ppermute | solution.py:438
  155.4 6.5 %collective-permute-start.26 = (bf16[2,256,128]{2,1,0:T(8,128)(2,1)S(1)}, bf16[2,256,128]{2,1,0:T(8,128)(2,1)S(1)}, u32[]{:S(2)}, u32[]{:S(2)}) collective-permute-start(bf16[2,256,128]{2,1,0:T(8,128)(2,1)S(1)} %pad_maximum_fusion.3.refs_8_), channel_id=1, source_target_pairs={{0,8},{8,0},{16,24},{24,16},{32,40},{40,32},{48,56},{56,48},{64,72... | collective-permute-start | bytes 393224 | tf_op jit(solution)/shard_map/ppermute | solution.py:438
  155.6 6.3 %collective-permute-start.21 = (bf16[3,256,128]{2,1,0:T(8,128)(2,1)S(1)}, bf16[3,256,128]{2,1,0:T(8,128)(2,1)S(1)}, u32[]{:S(2)}, u32[]{:S(2)}) collective-permute-start(bf16[3,256,128]{2,1,0:T(8,128)(2,1)S(1)} %pad_maximum_fusion.refs_4_), channel_id=1, source_target_pairs={{0,8},{8,0},{16,24},{24,16},{32,40},{40,32},{48,56},{56,48},{64,72... | collective-permute-start | bytes 589832 | tf_op jit(solution)/shard_map/ppermute | solution.py:438
  158.5 5.9 %collective-permute-start.14 = (bf16[2,256,128]{2,1,0:T(8,128)(2,1)S(1)}, bf16[2,256,128]{2,1,0:T(8,128)(2,1)S(1)}, u32[]{:S(2)}, u32[]{:S(2)}) collective-permute-start(bf16[2,256,128]{2,1,0:T(8,128)(2,1)S(1)} %collective-permute-done.13.refs_0_), channel_id=1, source_target_pairs={{0,8},{8,0},{16,24},{24,16},{32,40},{40,32},{48,56},{56,48},{64,72... | collective-permute-start | bytes 393224 | tf_op jit(solution)/shard_map/ppermute | solution.py:438
  (18 other events, 229.8 us)

commit v7 on v5

--- a/solution.py
+++ b/solution.py
@@ -389,15 +389,15 @@
     )(scalars, own, other, partner, x, w, st, gst)
 
 
-def place_kernel(count, s_ref, *refs):
+def place_kernel(pieces, s_ref, *refs):
     out_ref, sems = refs[-2], refs[-1]
     copies = []
-    for i in range(count):
-        for part in range(4):
+    for ref, (far, other, first) in zip(refs, pieces):
+        for i in range(0, ref.shape[0], 2):
             copies.append(pltpu.make_async_copy(
-                refs[i].at[2 * part : 2 * part + 2],
-                out_ref.at[s_ref[0], 2 * part : 2 * part + 2, s_ref[1 + i]],
-                sems.at[4 * i + part],
+                ref.at[i : i + 2],
+                out_ref.at[s_ref[0] ^ far, first + i : first + i + 2, s_ref[1] ^ other],
+                sems.at[len(copies)],
             ))
     for copy in copies:
         copy.start()
@@ -405,14 +405,15 @@
         copy.wait()
 
 
-def place(scalars, blocks, whole):
+def place(scalars, pieces, blocks, whole):
     rest = () if whole is None else (whole,)
-    return pl.pallas_call(
-        functools.partial(place_kernel, len(blocks)),
+    count = sum(block.shape[0] // 2 for block in blocks)
+    return pl.pallas_call(
+        functools.partial(place_kernel, pieces),
         in_specs=[SMEM] + [VMEM] * len(blocks) + [HBM] * len(rest),
         out_specs=HBM,
         out_shape=jax.ShapeDtypeStruct((2, 8, 2, ROWS, D), BF16),
-        scratch_shapes=[pltpu.SemaphoreType.DMA((8,))],
+        scratch_shapes=[pltpu.SemaphoreType.DMA((count,))],
         input_output_aliases={1 + len(blocks): 0} if rest else {},
         compiler_params=pltpu.CompilerParams(vmem_limit_bytes=4 * MB),
         name="place",
@@ -465,7 +466,8 @@
     mine_near, send_near = proto_pass(jnp.stack([core, y]), f12, u, e, codes)
     got_near = lax.ppermute(send_near, "dp", CORE_PERM)
     table = doubled(table, 2)
-    quarter = (mine_near + got_near.astype(F32) + from_far.astype(F32)).astype(BF16)
+    near = lax.optimization_barrier(mine_near + got_near.astype(F32))
+    quarter = (near + from_far.astype(F32)).astype(BF16)
     pieces = exchange(quarter, "dp", Z_GROUPS)
     other = lax.ppermute(table, "dp", Y_PERM)
     embed = row_pass(jnp.stack([q, dp]), table, other, partner, x, w, st, gst)
@@ -473,17 +475,20 @@
 
     swapped = swap(embed, 1)
     along_z = exchange(final, "dp", Z_GROUPS)
-    from_y = lax.ppermute(along_z, "dp", Y_PERM)
+    far_a = lax.ppermute(along_z[:4], "dp", Y_PERM)
+    far_b = lax.ppermute(along_z[4:], "dp", Y_PERM)
     embed = embed + swapped
     swapped = swap(embed, 4)
     embed = embed + swapped
     swapped = swap(embed, 2)
     hvp_embed = (embed + swapped).astype(BF16)
     own_core = lax.ppermute(along_z, "dp", CORE_PERM)
-    whole = place(jnp.stack([y, core, 1 - core]), (along_z, own_core), None)
-    far_core = lax.ppermute(from_y, "dp", CORE_PERM)
-    whole = place(jnp.stack([1 - y, core]), (from_y,), whole)
-    whole = place(jnp.stack([1 - y, 1 - core]), (far_core,), whole)
+    core_a = lax.ppermute(far_a, "dp", CORE_PERM)
+    core_b = lax.ppermute(far_b, "dp", CORE_PERM)
+    where = jnp.stack([y, core])
+    whole = place(where, ((0, 0, 0), (0, 1, 0)), (along_z, own_core), None)
+    whole = place(where, ((1, 0, 0), (1, 1, 0)), (far_a, core_a), whole)
+    whole = place(where, ((1, 0, 4), (1, 1, 4)), (far_b, core_b), whole)
     return (hvp_embed, whole.reshape(LOCAL, D))
 
 

time: 163 us -> 162 us (level)
    ppermute x3, waiting for transfers between devices: 13.3 us -> 10.8 us  [swap(): return lax.ppermute(x, 'proto', [(i, i ^ bit) for i in range(PR)])]
  transfers between devices with their start and end apart: 17 -> 19, of which waited for: 12 -> 12; matrix products, arithmetic and copies ran while one was open for 1% -> 2% of each run, Pallas kernels for 14% -> 14%
where the time goes in v7:
time: 162 us
  waiting for transfers between devices  56 us (35%)
  Pallas kernels  41.5 us (26%)
  starting transfers between devices  36.4 us (22%)
  blocking collectives  20.5 us (13%)
  other arithmetic  4.22 us (3%)
  local copies, waits for them, and re-layouts  2.01 us (1%)
    all_to_all x1, blocking collectives, exchange(): return lax.all_to_all(x, axis, 0, 0, axis_index_groups=groups, tiled=True)  20.5 us
    ppermute x4, waiting for transfers between devices, doubled(): other = lax.ppermute(x, 'dp', [(i, i ^ bit) for i in range(DP)])  19.7 us
    all_to_all x3, starting transfers between devices, exchange(): return lax.all_to_all(x, axis, 0, 0, axis_index_groups=groups, tiled=True)  19.6 us
    pallas_call x2, Pallas kernels, proto_pass(): pl.pallas_call(proto_kernel, grid_spec=pltpu.PrefetchScalarGridSpec(num_s...  11.3 us
    ppermute x1, waiting for transfers between devices, inner(): from_far = lax.ppermute(to_y, 'dp', Y_PERM)  11.1 us
    ppermute x3, waiting for transfers between devices, swap(): return lax.ppermute(x, 'proto', [(i, i ^ bit) for i in range(PR)])  10.8 us
    pallas_call x1, Pallas kernels, score_pass(): pl.pallas_call(score_kernel, grid=(NCH,), in_specs=[pl.BlockSpec((ROWS, D...  10.3 us
    pallas_call x1, Pallas kernels, embed_pass(): pl.pallas_call(embed_kernel, grid=(NCH,), in_specs=[pl.BlockSpec((ROWS, C...  7.62 us
  transfers between devices with their start and end apart: 19, of which 12 were waited for; matrix products, arithmetic and copies ran while one was open for 2% of the time, Pallas kernels for 14%

profile of v7, /device:TPU:8, one launch (start us, length us, event | category | flops | bytes accessed | tf_op | source)
XLA Modules:
  0.0 161.7 jit_solution(6270588418228625568)
XLA Ops:
  0.6 3.4 %mass_pass.1 = bf16[32,48,128]{2,1,0:T(8,128)(2,1)} custom-call(s32[1]{0:T(128)} %bitcast.q_ref, bf16[256,8192]{1,0:T(8,128)(2,1)} %codes_ref.7, bf16[256,128]{1,0:T(8,128)(2,1)} %tan_ref.5), custom_call_target="tpu_custom_call" | custom-call | flops 2097152 | bytes 5242880 | tf_op jit(solution)/shard_map/mass_pass/pallas_call | solution.py:71
  4.1 10.1 %all-to-all-start = ((bf16[32,48,128]{2,1,0:T(8,128)(2,1)}), bf16[32,48,128]{2,1,0:T(8,128)(2,1)S(1)}, u32[]{:S(2)}, u32[]{:S(2)}) async-start(bf16[32,48,128]{2,1,0:T(8,128)(2,1)} %mass_pass.1), calls=%async_computation | async-start | bytes 786432 | tf_op jit(solution)/shard_map/all_to_all | solution.py:429
  14.3 10.3 %score_pass.1 = (bf16[256,8192]{1,0:T(8,128)(2,1)}, bf16[256,8192]{1,0:T(8,128)(2,1)}, f32[4,256,128]{2,1,0:T(8,128)}, f32[256,256]{1,0:T(8,128)}) custom-call(bf16[256,128]{1,0:T(8,128)(2,1)} %f_ref.3, bf16[256,128]{1,0:T(8,128)(2,1)} %tan_ref.5, bf16[8192,128]{1,0:T(8,128)(2,1)} %a_ref.3, bf16[8192,128]{1,0:T(8,128)(2,1)} %p_ref.3, bf16[256,8192]{1,0:T(8,128)(2,1)} %codes_ref.7), custom_call_target="tpu_custom_call" | custom-call | flops 5368709120 | bytes 12582912 | tf_op jit(solution)/shard_map/score_pass/pallas_call | solution.py:132
  24.6 4.1 %all-to-all-done.tab_ref = bf16[32,48,128]{2,1,0:T(8,128)(2,1)S(1)} async-done(((bf16[32,48,128]{2,1,0:T(8,128)(2,1)}), bf16[32,48,128]{2,1,0:T(8,128)(2,1)S(1)}, u32[]{:S(2)}, u32[]{:S(2)}) %all-to-all-start) | async-done | bytes 393248 | tf_op jit(solution)/shard_map/all_to_all | solution.py:429
  31.2 6.0 %all-to-all-start.1 = ((bf16[8,320,128]{2,1,0:T(8,128)(2,1)}), bf16[8,320,128]{2,1,0:T(8,128)(2,1)S(1)}, u32[]{:S(2)}, u32[]{:S(2)}) async-start(bf16[8,320,128]{2,1,0:T(8,128)(2,1)} %pick.1), calls=%async_computation.1 | async-start | bytes 1310720 | tf_op jit(solution)/shard_map/all_to_all | solution.py:429
  37.9 7.6 %embed_pass.1 = (f32[256,128]{1,0:T(8,128)}, f32[256,128]{1,0:T(8,128)}) custom-call(bf16[256,8192]{1,0:T(8,128)(2,1)} %get-tuple-element.20.e_ref, bf16[256,8192]{1,0:T(8,128)(2,1)} %get-tuple-element.21.u_ref, bf16[8192,128]{1,0:T(8,128)(2,1)} %a_ref.3, bf16[8192,128]{1,0:T(8,128)(2,1)} %p_ref.3, f32[4,256,128]{2,1,0:T(8,128)} %get-tuple-element.22.cst_ref, ...), custom_call_target="tpu_custom_call" | custom-call | flops 3221225472 | bytes 12582912 | tf_op jit(solution)/shard_map/embed_pass/pallas_call | solution.py:183
  45.5 3.1 %all-to-all-done.1.rec_ref = bf16[8,320,128]{2,1,0:T(8,128)(2,1)S(1)} async-done(((bf16[8,320,128]{2,1,0:T(8,128)(2,1)}), bf16[8,320,128]{2,1,0:T(8,128)(2,1)S(1)}, u32[]{:S(2)}, u32[]{:S(2)}) %all-to-all-start.1) | async-done | bytes 655392 | tf_op jit(solution)/shard_map/all_to_all | solution.py:429
  50.4 5.7 %proto_pass.2 = (f32[8,256,128]{2,1,0:T(8,128)}, bf16[8,256,128]{2,1,0:T(8,128)(2,1)}) custom-call(s32[2]{0:T(128)} %get-tuple-element.39.s_ref, bf16[9,256,128]{2,1,0:T(8,128)(2,1)} %copy-done, bf16[9,256,128]{2,1,0:T(8,128)(2,1)} %copy-done, bf16[256,8192]{1,0:T(8,128)(2,1)} %get-tuple-element.21.u_ref, bf16[256,8192]{1,0:T(8,128)(2,1)} %get-tuple-element.20.e_ref, ...), custom_call_target="tpu_custom_call" | custom-call | flops 1610612736 | bytes 9437184 | tf_op jit(solution)/shard_map/proto_pass/pallas_call | solution.py:320
  56.1 2.1 %collective-permute-done.8 = bf16[8,256,128]{2,1,0:T(8,128)(2,1)S(1)} collective-permute-done((bf16[8,256,128]{2,1,0:T(8,128)(2,1)}, bf16[8,256,128]{2,1,0:T(8,128)(2,1)S(1)}, u32[]{:S(2)}, u32[]{:S(2)}) %collective-permute-start.8) | collective-permute-done | bytes 524320 | tf_op jit(solution)/shard_map/ppermute | solution.py:461
  59.6 5.7 %proto_pass.3 = (f32[8,256,128]{2,1,0:T(8,128)}, bf16[8,256,128]{2,1,0:T(8,128)(2,1)}) custom-call(s32[2]{0:T(128)} %get-tuple-element.38.s_ref, bf16[9,256,128]{2,1,0:T(8,128)(2,1)} %copy-done, bf16[9,256,128]{2,1,0:T(8,128)(2,1)} %copy-done, bf16[256,8192]{1,0:T(8,128)(2,1)} %get-tuple-element.21.u_ref, bf16[256,8192]{1,0:T(8,128)(2,1)} %get-tuple-element.20.e_ref, ...), custom_call_target="tpu_custom_call" | custom-call | flops 1610612736 | bytes 9437184 | tf_op jit(solution)/shard_map/proto_pass/pallas_call | solution.py:320
  65.4 2.0 %collective-permute-start.10 = (bf16[8,256,128]{2,1,0:T(8,128)(2,1)S(1)}, bf16[8,256,128]{2,1,0:T(8,128)(2,1)S(1)}, u32[]{:S(2)}, u32[]{:S(2)}) collective-permute-start(bf16[8,256,128]{2,1,0:T(8,128)(2,1)S(1)} %add_convert_fusion.1), channel_id=1, source_target_pairs={{0,128},{8,136},{16,144},{24,152},{32,160},{40,168},{48,176},{56,1... | collective-permute-start | bytes 1572872 | tf_op jit(solution)/shard_map/ppermute | solution.py:463
  68.7 11.1 %collective-permute-done.10 = bf16[8,256,128]{2,1,0:T(8,128)(2,1)S(1)} collective-permute-done((bf16[8,256,128]{2,1,0:T(8,128)(2,1)S(1)}, bf16[8,256,128]{2,1,0:T(8,128)(2,1)S(1)}, u32[]{:S(2)}, u32[]{:S(2)}) %collective-permute-start.10) | collective-permute-done | bytes 524320 | tf_op jit(solution)/shard_map/ppermute | solution.py:463
  80.0 20.5 %all_to_all.20.pieces_ref = bf16[8,256,128]{2,1,0:T(8,128)(2,1)S(1)} all-to-all(bf16[8,256,128]{2,1,0:T(8,128)(2,1)S(1)} %add_convert_fusion), channel_id=1, replica_groups={{0,16,32,48,64,80,96,112},{8,24,40,56,72,88,104,120},{128,144,160,176,1..., dimensions={0} | all-to-all | bytes 1048576 | tf_op jit(solution)/shard_map/all_to_all | solution.py:429
  101.4 3.5 %all-to-all-start.3 = ((bf16[8,256,128]{2,1,0:T(8,128)(2,1)}), bf16[8,256,128]{2,1,0:T(8,128)(2,1)S(1)}, u32[]{:S(2)}, u32[]{:S(2)}) async-start(bf16[8,256,128]{2,1,0:T(8,128)(2,1)} %final_pass.1), calls=%async_computation.3 | async-start | bytes 1048576 | tf_op jit(solution)/shard_map/all_to_all | solution.py:429
  106.1 5.8 %collective-permute-start.1 = (bf16[64,128]{1,0:T(8,128)(2,1)S(1)}, bf16[64,128]{1,0:T(8,128)(2,1)S(1)}, u32[]{:S(2)}, u32[]{:S(2)}) collective-permute-start(bf16[64,128]{1,0:T(8,128)(2,1)S(1)} %pad_maximum_fusion.3), channel_id=1, source_target_pairs={{0,64},{8,72},{16,80},{24,88},{32,96},{40,104},{48,112},{56,120},{... | collective-permute-start | bytes 49160 | tf_op jit(solution)/shard_map/ppermute | solution.py:433
  111.9 9.5 %collective-permute-done.1 = bf16[64,128]{1,0:T(8,128)(2,1)S(1)} collective-permute-done((bf16[64,128]{1,0:T(8,128)(2,1)S(1)}, bf16[64,128]{1,0:T(8,128)(2,1)S(1)}, u32[]{:S(2)}, u32[]{:S(2)}) %collective-permute-start.1) | collective-permute-done | bytes 16416 | tf_op jit(solution)/shard_map/ppermute | solution.py:433
  121.4 5.1 %collective-permute-done.2 = bf16[128,128]{1,0:T(8,128)(2,1)S(1)} collective-permute-done((bf16[128,128]{1,0:T(8,128)(2,1)S(1)}, bf16[128,128]{1,0:T(8,128)(2,1)S(1)}, u32[]{:S(2)}, u32[]{:S(2)}) %collective-permute-start.2) | collective-permute-done | bytes 32800 | tf_op jit(solution)/shard_map/ppermute | solution.py:433
  126.7 4.0 %collective-permute-done.3 = bf16[256,128]{1,0:T(8,128)(2,1)S(1)} collective-permute-done((bf16[256,128]{1,0:T(8,128)(2,1)S(1)}, bf16[256,128]{1,0:T(8,128)(2,1)S(1)}, u32[]{:S(2)}, u32[]{:S(2)}) %collective-permute-start.3) | collective-permute-done | bytes 65568 | tf_op jit(solution)/shard_map/ppermute | solution.py:433
  132.1 5.1 %collective-permute-done.4.other_ref = bf16[512,128]{1,0:T(8,128)(2,1)S(1)} collective-permute-done((bf16[512,128]{1,0:T(8,128)(2,1)S(1)}, bf16[512,128]{1,0:T(8,128)(2,1)S(1)}, u32[]{:S(2)}, u32[]{:S(2)}) %collective-permute-start.4) | collective-permute-done | bytes 131104 | tf_op jit(solution)/shard_map/ppermute | solution.py:472
  138.3 1.9 %collective-permute-start.5 = (f32[256,128]{1,0:T(8,128)S(1)}, f32[256,128]{1,0:T(8,128)S(1)}, u32[]{:S(2)}, u32[]{:S(2)}) collective-permute-start(f32[256,128]{1,0:T(8,128)S(1)} %row_pass.1), channel_id=1, source_target_pairs={{0,1},{1,0},{2,3},{3,2},{4,5},{5,4},{6,7},{7,6},{8,9},{9,8},{10,11... | collective-permute-start | bytes 393224 | tf_op jit(solution)/shard_map/ppermute | solution.py:438
  142.4 2.5 %collective-permute-done.5 = f32[256,128]{1,0:T(8,128)S(1)} collective-permute-done((f32[256,128]{1,0:T(8,128)S(1)}, f32[256,128]{1,0:T(8,128)S(1)}, u32[]{:S(2)}, u32[]{:S(2)}) %collective-permute-start.5) | collective-permute-done | bytes 131104 | tf_op jit(solution)/shard_map/ppermute | solution.py:438
  144.9 1.9 %collective-permute-start.6 = (f32[256,128]{1,0:T(8,128)S(1)}, f32[256,128]{1,0:T(8,128)S(1)}, u32[]{:S(2)}, u32[]{:S(2)}) collective-permute-start(f32[256,128]{1,0:T(8,128)S(1)} %add.23), channel_id=1, source_target_pairs={{0,4},{1,5},{2,6},{3,7},{4,0},{5,1},{6,2},{7,3},{8,12},{9,13},{10,... | collective-permute-start | bytes 393224 | tf_op jit(solution)/shard_map/ppermute | solution.py:438
  146.8 4.7 %collective-permute-done.6 = f32[256,128]{1,0:T(8,128)S(1)} collective-permute-done((f32[256,128]{1,0:T(8,128)S(1)}, f32[256,128]{1,0:T(8,128)S(1)}, u32[]{:S(2)}, u32[]{:S(2)}) %collective-permute-start.6) | collective-permute-done | bytes 131104 | tf_op jit(solution)/shard_map/ppermute | solution.py:438
  152.9 3.6 %collective-permute-done.7 = f32[256,128]{1,0:T(8,128)S(1)} collective-permute-done((f32[256,128]{1,0:T(8,128)S(1)}, f32[256,128]{1,0:T(8,128)S(1)}, u32[]{:S(2)}, u32[]{:S(2)}) %collective-permute-start.7) | collective-permute-done | bytes 131104 | tf_op jit(solution)/shard_map/ppermute | solution.py:438
  (60 shorter events, 21.6 us)
Async XLA Ops:
  0.6 13.5 %copy-start.8 = (s32[256]{0:T(256)S(1)}, s32[256]{0:T(256)}, u32[]{:S(2)}) copy-start(s32[256]{0:T(256)} %param.11) | copy-start | bytes 3076
  4.1 24.6 %all-to-all-start = ((bf16[32,48,128]{2,1,0:T(8,128)(2,1)}), bf16[32,48,128]{2,1,0:T(8,128)(2,1)S(1)}, u32[]{:S(2)}, u32[]{:S(2)}) async-start(bf16[32,48,128]{2,1,0:T(8,128)(2,1)} %mass_pass.1), calls=%async_computation | async-start | bytes 786432 | tf_op jit(solution)/shard_map/all_to_all | solution.py:429
  31.2 17.3 %all-to-all-start.1 = ((bf16[8,320,128]{2,1,0:T(8,128)(2,1)}), bf16[8,320,128]{2,1,0:T(8,128)(2,1)S(1)}, u32[]{:S(2)}, u32[]{:S(2)}) async-start(bf16[8,320,128]{2,1,0:T(8,128)(2,1)} %pick.1), calls=%async_computation.1 | async-start | bytes 1310720 | tf_op jit(solution)/shard_map/all_to_all | solution.py:429
  37.9 10.7 %copy-start.7 = (bf16[256,128]{1,0:T(8,128)(2,1)S(1)}, bf16[256,128]{1,0:T(8,128)(2,1)}, u32[]{:S(2)}) copy-start(bf16[256,128]{1,0:T(8,128)(2,1)} %f_ref.3) | copy-start | bytes 196612
  56.1 2.1 %collective-permute-start.8 = (bf16[8,256,128]{2,1,0:T(8,128)(2,1)}, bf16[8,256,128]{2,1,0:T(8,128)(2,1)S(1)}, u32[]{:S(2)}, u32[]{:S(2)}) collective-permute-start(bf16[8,256,128]{2,1,0:T(8,128)(2,1)} %get-tuple-element.32), channel_id=1, source_target_pairs={{0,8},{8,0},{16,24},{24,16},{32,40},{40,32},{48,56},{56,48},{64,72... | collective-permute-start | bytes 1572872 | tf_op jit(solution)/shard_map/ppermute | solution.py:461
  65.2 2.2 %collective-permute-start.9 = (bf16[8,256,128]{2,1,0:T(8,128)(2,1)}, bf16[8,256,128]{2,1,0:T(8,128)(2,1)S(1)}, u32[]{:S(2)}, u32[]{:S(2)}) collective-permute-start(bf16[8,256,128]{2,1,0:T(8,128)(2,1)} %get-tuple-element.35), channel_id=1, source_target_pairs={{0,8},{8,0},{16,24},{24,16},{32,40},{40,32},{48,56},{56,48},{64,72... | collective-permute-start | bytes 1572872 | tf_op jit(solution)/shard_map/ppermute | solution.py:467
  65.4 14.5 %collective-permute-start.10 = (bf16[8,256,128]{2,1,0:T(8,128)(2,1)S(1)}, bf16[8,256,128]{2,1,0:T(8,128)(2,1)S(1)}, u32[]{:S(2)}, u32[]{:S(2)}) collective-permute-start(bf16[8,256,128]{2,1,0:T(8,128)(2,1)S(1)} %add_convert_fusion.1), channel_id=1, source_target_pairs={{0,128},{8,136},{16,144},{24,152},{32,160},{40,168},{48,176},{56,1... | collective-permute-start | bytes 1572872 | tf_op jit(solution)/shard_map/ppermute | solution.py:463
  79.9 57.2 %copy-start.2 = (f32[256,256]{1,0:T(8,128)S(1)}, f32[256,256]{1,0:T(8,128)}, u32[]{:S(2)}) copy-start(f32[256,256]{1,0:T(8,128)} %get-tuple-element.19.st_ref) | copy-start | bytes 786436
  80.0 57.2 %copy-start.5 = (f32[256,128]{1,0:T(8,128)S(1)}, f32[256,128]{1,0:T(8,128)}, u32[]{:S(2)}) copy-start(f32[256,128]{1,0:T(8,128)} %get-tuple-element.27.x_ref) | copy-start | bytes 393220
  80.0 57.2 %copy-start.6 = (f32[256,128]{1,0:T(8,128)S(1)}, f32[256,128]{1,0:T(8,128)}, u32[]{:S(2)}) copy-start(f32[256,128]{1,0:T(8,128)} %get-tuple-element.28.w_ref) | copy-start | bytes 393220
  101.4 38.8 %all-to-all-start.3 = ((bf16[8,256,128]{2,1,0:T(8,128)(2,1)}), bf16[8,256,128]{2,1,0:T(8,128)(2,1)S(1)}, u32[]{:S(2)}, u32[]{:S(2)}) async-start(bf16[8,256,128]{2,1,0:T(8,128)(2,1)} %final_pass.1), calls=%async_computation.3 | async-start | bytes 1048576 | tf_op jit(solution)/shard_map/all_to_all | solution.py:429
  104.9 1.3 collective-permute-start
  106.1 15.2 %collective-permute-start.1 = (bf16[64,128]{1,0:T(8,128)(2,1)S(1)}, bf16[64,128]{1,0:T(8,128)(2,1)S(1)}, u32[]{:S(2)}, u32[]{:S(2)}) collective-permute-start(bf16[64,128]{1,0:T(8,128)(2,1)S(1)} %pad_maximum_fusion.3), channel_id=1, source_target_pairs={{0,64},{8,72},{16,80},{24,88},{32,96},{40,104},{48,112},{56,120},{... | collective-permute-start | bytes 49160 | tf_op jit(solution)/shard_map/ppermute | solution.py:433
  121.4 5.1 %collective-permute-start.2 = (bf16[128,128]{1,0:T(8,128)(2,1)S(1)}, bf16[128,128]{1,0:T(8,128)(2,1)S(1)}, u32[]{:S(2)}, u32[]{:S(2)}) collective-permute-start(bf16[128,128]{1,0:T(8,128)(2,1)S(1)} %pad_maximum_fusion.2), channel_id=1, source_target_pairs={{0,32},{8,40},{16,48},{24,56},{32,0},{40,8},{48,16},{56,24},{64,96... | collective-permute-start | bytes 98312 | tf_op jit(solution)/shard_map/ppermute | solution.py:433
  126.5 4.3 %collective-permute-start.3 = (bf16[256,128]{1,0:T(8,128)(2,1)S(1)}, bf16[256,128]{1,0:T(8,128)(2,1)S(1)}, u32[]{:S(2)}, u32[]{:S(2)}) collective-permute-start(bf16[256,128]{1,0:T(8,128)(2,1)S(1)} %pad_maximum_fusion.1), channel_id=1, source_target_pairs={{0,16},{8,24},{16,0},{24,8},{32,48},{40,56},{48,32},{56,40},{64,80... | collective-permute-start | bytes 196616 | tf_op jit(solution)/shard_map/ppermute | solution.py:433
  130.7 6.5 %collective-permute-start.4 = (bf16[512,128]{1,0:T(8,128)(2,1)S(1)}, bf16[512,128]{1,0:T(8,128)(2,1)S(1)}, u32[]{:S(2)}, u32[]{:S(2)}) collective-permute-start(bf16[512,128]{1,0:T(8,128)(2,1)S(1)} %pad_maximum_fusion.own_ref), channel_id=1, source_target_pairs={{0,128},{8,136},{16,144},{24,152},{32,160},{40,168},{48,176},{56,1... | collective-permute-start | bytes 393224 | tf_op jit(solution)/shard_map/ppermute | solution.py:472
  138.3 6.6 %collective-permute-start.5 = (f32[256,128]{1,0:T(8,128)S(1)}, f32[256,128]{1,0:T(8,128)S(1)}, u32[]{:S(2)}, u32[]{:S(2)}) collective-permute-start(f32[256,128]{1,0:T(8,128)S(1)} %row_pass.1), channel_id=1, source_target_pairs={{0,1},{1,0},{2,3},{3,2},{4,5},{5,4},{6,7},{7,6},{8,9},{9,8},{10,11... | collective-permute-start | bytes 393224 | tf_op jit(solution)/shard_map/ppermute | solution.py:438
  140.2 12.1 %collective-permute-start.13 = (bf16[4,256,128]{2,1,0:T(8,128)(2,1)S(1)}, bf16[4,256,128]{2,1,0:T(8,128)(2,1)S(1)}, u32[]{:S(2)}, u32[]{:S(2)}) collective-permute-start(bf16[4,256,128]{2,1,0:T(8,128)(2,1)S(1)} %get-tuple-element.36), channel_id=1, source_target_pairs={{0,128},{8,136},{16,144},{24,152},{32,160},{40,168},{48,176},{56,1... | collective-permute-start | bytes 786440 | tf_op jit(solution)/shard_map/ppermute | solution.py:478
  141.6 10.8 %collective-permute-start.11 = (bf16[4,256,128]{2,1,0:T(8,128)(2,1)S(1)}, bf16[4,256,128]{2,1,0:T(8,128)(2,1)S(1)}, u32[]{:S(2)}, u32[]{:S(2)}) collective-permute-start(bf16[4,256,128]{2,1,0:T(8,128)(2,1)S(1)} %get-tuple-element.37), channel_id=1, source_target_pairs={{0,128},{8,136},{16,144},{24,152},{32,160},{40,168},{48,176},{56,1... | collective-permute-start | bytes 786440 | tf_op jit(solution)/shard_map/ppermute | solution.py:479
  142.4 14.8 %collective-permute-start.15 = (bf16[8,256,128]{2,1,0:T(8,128)(2,1)S(1)}, bf16[8,256,128]{2,1,0:T(8,128)(2,1)S(1)}, u32[]{:S(2)}, u32[]{:S(2)}) collective-permute-start(bf16[8,256,128]{2,1,0:T(8,128)(2,1)S(1)} %all-to-all-done.3.refs_0_), channel_id=1, source_target_pairs={{0,8},{8,0},{16,24},{24,16},{32,40},{40,32},{48,56},{56,48},{64,72... | collective-permute-start | bytes 1572872 | tf_op jit(solution)/shard_map/ppermute | solution.py:485
  144.9 6.6 %collective-permute-start.6 = (f32[256,128]{1,0:T(8,128)S(1)}, f32[256,128]{1,0:T(8,128)S(1)}, u32[]{:S(2)}, u32[]{:S(2)}) collective-permute-start(f32[256,128]{1,0:T(8,128)S(1)} %add.23), channel_id=1, source_target_pairs={{0,4},{1,5},{2,6},{3,7},{4,0},{5,1},{6,2},{7,3},{8,12},{9,13},{10,... | collective-permute-start | bytes 393224 | tf_op jit(solution)/shard_map/ppermute | solution.py:438
  151.5 5.1 %collective-permute-start.7 = (f32[256,128]{1,0:T(8,128)S(1)}, f32[256,128]{1,0:T(8,128)S(1)}, u32[]{:S(2)}, u32[]{:S(2)}) collective-permute-start(f32[256,128]{1,0:T(8,128)S(1)} %add.24), channel_id=1, source_target_pairs={{0,2},{1,3},{2,0},{3,1},{4,6},{5,7},{6,4},{7,5},{8,10},{9,11},{10,... | collective-permute-start | bytes 393224 | tf_op jit(solution)/shard_map/ppermute | solution.py:438
  152.4 6.4 %collective-permute-start.14 = (bf16[4,256,128]{2,1,0:T(8,128)(2,1)S(1)}, bf16[4,256,128]{2,1,0:T(8,128)(2,1)S(1)}, u32[]{:S(2)}, u32[]{:S(2)}) collective-permute-start(bf16[4,256,128]{2,1,0:T(8,128)(2,1)S(1)} %collective-permute-done.13.refs_0_), channel_id=1, source_target_pairs={{0,8},{8,0},{16,24},{24,16},{32,40},{40,32},{48,56},{56,48},{64,72... | collective-permute-start | bytes 786440 | tf_op jit(solution)/shard_map/ppermute | solution.py:486
  152.4 7.8 %collective-permute-start.12 = (bf16[4,256,128]{2,1,0:T(8,128)(2,1)S(1)}, bf16[4,256,128]{2,1,0:T(8,128)(2,1)S(1)}, u32[]{:S(2)}, u32[]{:S(2)}) collective-permute-start(bf16[4,256,128]{2,1,0:T(8,128)(2,1)S(1)} %collective-permute-done.11.refs_0_), channel_id=1, source_target_pairs={{0,8},{8,0},{16,24},{24,16},{32,40},{40,32},{48,56},{56,48},{64,72... | collective-permute-start | bytes 786440 | tf_op jit(solution)/shard_map/ppermute | solution.py:487
  (4 other events, 23.2 us)

commit v8 on v7

--- a/solution.py
+++ b/solution.py
@@ -158,7 +158,7 @@
             pltpu.VMEM((ROWS, D), F32),
         ],
         cost_estimate=pl.CostEstimate(flops=10 * ROWS * LOCAL * D * 2, bytes_accessed=12 << 20, transcendentals=ROWS * LOCAL),
-        compiler_params=pltpu.CompilerParams(vmem_limit_bytes=56 * MB),
+        compiler_params=pltpu.CompilerParams(vmem_limit_bytes=51 * MB),
         name="score_pass",
     )(f, tan, a, p, codes)
 
@@ -197,7 +197,7 @@
         ],
         out_shape=[jax.ShapeDtypeStruct((ROWS, D), F32)] * 2,
         cost_estimate=pl.CostEstimate(flops=6 * ROWS * LOCAL * D * 2, bytes_accessed=12 << 20, transcendentals=0),
-        compiler_params=pltpu.CompilerParams(vmem_limit_bytes=56 * MB),
+        compiler_params=pltpu.CompilerParams(vmem_limit_bytes=51 * MB),
         name="embed_pass",
     )(e, u, a, p, cst, st)
 
@@ -339,7 +339,7 @@
             jax.ShapeDtypeStruct((8, ROWS, D), BF16),
         ],
         cost_estimate=pl.CostEstimate(flops=3 * ROWS * LOCAL * D * 2, bytes_accessed=9 << 20, transcendentals=0),
-        compiler_params=pltpu.CompilerParams(vmem_limit_bytes=56 * MB),
+        compiler_params=pltpu.CompilerParams(vmem_limit_bytes=51 * MB),
         name="proto_pass",
     )(scalars, f12, f12, u, e, codes)
 

time: 162 us -> 158 us (0.975)
  Pallas kernels: 41.5 us -> 38.3 us
  other arithmetic: 4.22 us -> 1.23 us
  waiting for transfers between devices: 56 us -> 58.3 us
  local copies, waits for them, and re-layouts: 2.01 us -> 0.21 us
    pallas_call x2, Pallas kernels: 11.3 us -> 9.15 us  [proto_pass(): pl.pallas_call(proto_kernel, grid_spec=pltpu.PrefetchScalarGridSpec(num_s...]
    unnamed x18 -> x16, local copies, waits for them, and re-layouts: 1.84 us -> 0.04 us
    all_to_all x3, waiting for transfers between devices: 7.13 us -> 8.8 us  [exchange(): return lax.all_to_all(x, axis, 0, 0, axis_index_groups=groups, tiled=True)]
  transfers between devices with their start and end apart: 19 -> 19, of which waited for: 12 -> 12; matrix products, arithmetic and copies ran while one was open for 2% -> 1% of each run, Pallas kernels for 14% -> 13%
where the time goes in v8:
time: 158 us; the launch traced here: 157 us
  waiting for transfers between devices  58.3 us (37%)
  Pallas kernels  38.3 us (24%)
  starting transfers between devices  37 us (23%)
  blocking collectives  20.6 us (13%)
    all_to_all x1, blocking collectives, exchange(): return lax.all_to_all(x, axis, 0, 0, axis_index_groups=groups, tiled=True)  20.6 us
    ppermute x4, waiting for transfers between devices, doubled(): other = lax.ppermute(x, 'dp', [(i, i ^ bit) for i in range(DP)])  19.7 us
    all_to_all x3, starting transfers between devices, exchange(): return lax.all_to_all(x, axis, 0, 0, axis_index_groups=groups, tiled=True)  19.6 us
    ppermute x1, waiting for transfers between devices, inner(): from_far = lax.ppermute(to_y, 'dp', Y_PERM)  12.4 us
    pallas_call x1, Pallas kernels, score_pass(): pl.pallas_call(score_kernel, grid=(NCH,), in_specs=[pl.BlockSpec((ROWS, D...  10.4 us
    ppermute x3, waiting for transfers between devices, swap(): return lax.ppermute(x, 'proto', [(i, i ^ bit) for i in range(PR)])  10.3 us
    pallas_call x2, Pallas kernels, proto_pass(): pl.pallas_call(proto_kernel, grid_spec=pltpu.PrefetchScalarGridSpec(num_s...  9.15 us
    all_to_all x3, waiting for transfers between devices, exchange(): return lax.all_to_all(x, axis, 0, 0, axis_index_groups=groups, tiled=True)  8.8 us
  transfers between devices with their start and end apart: 19, of which 12 were waited for; matrix products, arithmetic and copies ran while one was open for 1% of the time, Pallas kernels for 13%

profile of v8, /device:TPU:8, one launch (start us, length us, event | category | flops | bytes accessed | tf_op | source)
XLA Modules:
  0.0 156.7 jit_solution(17793026149859678861)
XLA Ops:
  0.7 3.6 %mass_pass.1 = bf16[32,48,128]{2,1,0:T(8,128)(2,1)} custom-call(s32[1]{0:T(128)} %bitcast.q_ref, bf16[256,8192]{1,0:T(8,128)(2,1)} %codes_ref.7, bf16[256,128]{1,0:T(8,128)(2,1)} %tan_ref.5), custom_call_target="tpu_custom_call" | custom-call | flops 2097152 | bytes 5242880 | tf_op jit(solution)/shard_map/mass_pass/pallas_call | solution.py:71
  4.2 10.1 %all-to-all-start = ((bf16[32,48,128]{2,1,0:T(8,128)(2,1)}), bf16[32,48,128]{2,1,0:T(8,128)(2,1)S(1)}, u32[]{:S(2)}, u32[]{:S(2)}) async-start(bf16[32,48,128]{2,1,0:T(8,128)(2,1)} %mass_pass.1), calls=%async_computation | async-start | bytes 786432 | tf_op jit(solution)/shard_map/all_to_all | solution.py:429
  14.5 10.4 %score_pass.1 = (bf16[256,8192]{1,0:T(8,128)(2,1)}, bf16[256,8192]{1,0:T(8,128)(2,1)}, f32[4,256,128]{2,1,0:T(8,128)S(1)}, f32[256,256]{1,0:T(8,128)S(1)}) custom-call(bf16[256,128]{1,0:T(8,128)(2,1)S(1)} %copy-done.5, bf16[256,128]{1,0:T(8,128)(2,1)S(1)} %copy-done.3, bf16[8192,128]{1,0:T(8,128)(2,1)S(1)} %copy-done, bf16[8192,128]{1,0:T(8,128)(2,1)} %p_ref.3, ...), custom_call_target="tpu_custom_call" | custom-call | flops 5368709120 | bytes 12582912 | tf_op jit(solution)/shard_map/score_pass/pallas_call | solution.py:132
  24.9 4.0 %all-to-all-done.tab_ref = bf16[32,48,128]{2,1,0:T(8,128)(2,1)S(1)} async-done(((bf16[32,48,128]{2,1,0:T(8,128)(2,1)}), bf16[32,48,128]{2,1,0:T(8,128)(2,1)S(1)}, u32[]{:S(2)}, u32[]{:S(2)}) %all-to-all-start) | async-done | bytes 393248 | tf_op jit(solution)/shard_map/all_to_all | solution.py:429
  30.5 6.0 %all-to-all-start.1 = ((bf16[8,320,128]{2,1,0:T(8,128)(2,1)}), bf16[8,320,128]{2,1,0:T(8,128)(2,1)S(1)}, u32[]{:S(2)}, u32[]{:S(2)}) async-start(bf16[8,320,128]{2,1,0:T(8,128)(2,1)} %pick.1), calls=%async_computation.1 | async-start | bytes 1310720 | tf_op jit(solution)/shard_map/all_to_all | solution.py:429
  36.6 6.4 %embed_pass.1 = (f32[256,128]{1,0:T(8,128)S(1)}, f32[256,128]{1,0:T(8,128)S(1)}) custom-call(bf16[256,8192]{1,0:T(8,128)(2,1)} %get-tuple-element.20.e_ref, bf16[256,8192]{1,0:T(8,128)(2,1)} %get-tuple-element.21.u_ref, bf16[8192,128]{1,0:T(8,128)(2,1)} %a_ref.3, bf16[8192,128]{1,0:T(8,128)(2,1)} %p_ref.3, f32[4,256,128]{2,1,0:T(8,128)S(1)} %get-tuple-element.22.cst_ref, ...), custom_call_target="tpu_custom_call" | custom-call | flops 3221225472 | bytes 12582912 | tf_op jit(solution)/shard_map/embed_pass/pallas_call | solution.py:183
  43.0 4.8 %all-to-all-done.1.rec_ref = bf16[8,320,128]{2,1,0:T(8,128)(2,1)S(1)} async-done(((bf16[8,320,128]{2,1,0:T(8,128)(2,1)}), bf16[8,320,128]{2,1,0:T(8,128)(2,1)S(1)}, u32[]{:S(2)}, u32[]{:S(2)}) %all-to-all-start.1) | async-done | bytes 655392 | tf_op jit(solution)/shard_map/all_to_all | solution.py:429
  48.8 4.6 %proto_pass.2 = (f32[8,256,128]{2,1,0:T(8,128)S(1)}, bf16[8,256,128]{2,1,0:T(8,128)(2,1)S(1)}) custom-call(s32[2]{0:T(128)S(1)} %get-tuple-element.39.s_ref, bf16[9,256,128]{2,1,0:T(8,128)(2,1)S(1)} %get-tuple-element.33.f12_ref.swt_ref, bf16[9,256,128]{2,1,0:T(8,128)(2,1)S(1)} %get-tuple-element.33.f12_ref.swt_ref, ...), custom_call_target="tpu_custom_call" | custom-call | flops 1610612736 | bytes 9437184 | tf_op jit(solution)/shard_map/proto_pass/pallas_call | solution.py:320
  53.5 1.9 %collective-permute-done.8 = bf16[8,256,128]{2,1,0:T(8,128)(2,1)S(1)} collective-permute-done((bf16[8,256,128]{2,1,0:T(8,128)(2,1)S(1)}, bf16[8,256,128]{2,1,0:T(8,128)(2,1)S(1)}, u32[]{:S(2)}, u32[]{:S(2)}) %collective-permute-start.8) | collective-permute-done | bytes 524320 | tf_op jit(solution)/shard_map/ppermute | solution.py:461
  55.5 4.6 %proto_pass.3 = (f32[8,256,128]{2,1,0:T(8,128)S(1)}, bf16[8,256,128]{2,1,0:T(8,128)(2,1)S(1)}) custom-call(s32[2]{0:T(128)S(1)} %get-tuple-element.38.s_ref, bf16[9,256,128]{2,1,0:T(8,128)(2,1)S(1)} %get-tuple-element.33.f12_ref.swt_ref, bf16[9,256,128]{2,1,0:T(8,128)(2,1)S(1)} %get-tuple-element.33.f12_ref.swt_ref, ...), custom_call_target="tpu_custom_call" | custom-call | flops 1610612736 | bytes 9437184 | tf_op jit(solution)/shard_map/proto_pass/pallas_call | solution.py:320
  60.3 2.0 %collective-permute-start.10 = (bf16[8,256,128]{2,1,0:T(8,128)(2,1)S(1)}, bf16[8,256,128]{2,1,0:T(8,128)(2,1)S(1)}, u32[]{:S(2)}, u32[]{:S(2)}) collective-permute-start(bf16[8,256,128]{2,1,0:T(8,128)(2,1)S(1)} %add_convert_fusion.1), channel_id=1, source_target_pairs={{0,128},{8,136},{16,144},{24,152},{32,160},{40,168},{48,176},{56,1... | collective-permute-start | bytes 1572872 | tf_op jit(solution)/shard_map/ppermute | solution.py:463
  62.4 12.4 %collective-permute-done.10 = bf16[8,256,128]{2,1,0:T(8,128)(2,1)S(1)} collective-permute-done((bf16[8,256,128]{2,1,0:T(8,128)(2,1)S(1)}, bf16[8,256,128]{2,1,0:T(8,128)(2,1)S(1)}, u32[]{:S(2)}, u32[]{:S(2)}) %collective-permute-start.10) | collective-permute-done | bytes 524320 | tf_op jit(solution)/shard_map/ppermute | solution.py:463
  74.9 20.6 %all_to_all.20.pieces_ref = bf16[8,256,128]{2,1,0:T(8,128)(2,1)S(1)} all-to-all(bf16[8,256,128]{2,1,0:T(8,128)(2,1)S(1)} %add_convert_fusion), channel_id=1, replica_groups={{0,16,32,48,64,80,96,112},{8,24,40,56,72,88,104,120},{128,144,160,176,1..., dimensions={0} | all-to-all | bytes 1048576 | tf_op jit(solution)/shard_map/all_to_all | solution.py:429
  96.3 3.5 %all-to-all-start.3 = ((bf16[8,256,128]{2,1,0:T(8,128)(2,1)}), bf16[8,256,128]{2,1,0:T(8,128)(2,1)S(1)}, u32[]{:S(2)}, u32[]{:S(2)}) async-start(bf16[8,256,128]{2,1,0:T(8,128)(2,1)} %final_pass.1), calls=%async_computation.3 | async-start | bytes 1048576 | tf_op jit(solution)/shard_map/all_to_all | solution.py:429
  101.1 5.8 %collective-permute-start.1 = (bf16[64,128]{1,0:T(8,128)(2,1)S(1)}, bf16[64,128]{1,0:T(8,128)(2,1)S(1)}, u32[]{:S(2)}, u32[]{:S(2)}) collective-permute-start(bf16[64,128]{1,0:T(8,128)(2,1)S(1)} %pad_maximum_fusion.3), channel_id=1, source_target_pairs={{0,64},{8,72},{16,80},{24,88},{32,96},{40,104},{48,112},{56,120},{... | collective-permute-start | bytes 49160 | tf_op jit(solution)/shard_map/ppermute | solution.py:433
  106.9 9.5 %collective-permute-done.1 = bf16[64,128]{1,0:T(8,128)(2,1)S(1)} collective-permute-done((bf16[64,128]{1,0:T(8,128)(2,1)S(1)}, bf16[64,128]{1,0:T(8,128)(2,1)S(1)}, u32[]{:S(2)}, u32[]{:S(2)}) %collective-permute-start.1) | collective-permute-done | bytes 16416 | tf_op jit(solution)/shard_map/ppermute | solution.py:433
  116.3 5.1 %collective-permute-done.2 = bf16[128,128]{1,0:T(8,128)(2,1)S(1)} collective-permute-done((bf16[128,128]{1,0:T(8,128)(2,1)S(1)}, bf16[128,128]{1,0:T(8,128)(2,1)S(1)}, u32[]{:S(2)}, u32[]{:S(2)}) %collective-permute-start.2) | collective-permute-done | bytes 32800 | tf_op jit(solution)/shard_map/ppermute | solution.py:433
  121.7 4.0 %collective-permute-done.3 = bf16[256,128]{1,0:T(8,128)(2,1)S(1)} collective-permute-done((bf16[256,128]{1,0:T(8,128)(2,1)S(1)}, bf16[256,128]{1,0:T(8,128)(2,1)S(1)}, u32[]{:S(2)}, u32[]{:S(2)}) %collective-permute-start.3) | collective-permute-done | bytes 65568 | tf_op jit(solution)/shard_map/ppermute | solution.py:433
  127.0 5.2 %collective-permute-done.4.other_ref = bf16[512,128]{1,0:T(8,128)(2,1)S(1)} collective-permute-done((bf16[512,128]{1,0:T(8,128)(2,1)S(1)}, bf16[512,128]{1,0:T(8,128)(2,1)S(1)}, u32[]{:S(2)}, u32[]{:S(2)}) %collective-permute-start.4) | collective-permute-done | bytes 131104 | tf_op jit(solution)/shard_map/ppermute | solution.py:472
  133.3 1.9 %collective-permute-start.5 = (f32[256,128]{1,0:T(8,128)S(1)}, f32[256,128]{1,0:T(8,128)S(1)}, u32[]{:S(2)}, u32[]{:S(2)}) collective-permute-start(f32[256,128]{1,0:T(8,128)S(1)} %row_pass.1), channel_id=1, source_target_pairs={{0,1},{1,0},{2,3},{3,2},{4,5},{5,4},{6,7},{7,6},{8,9},{9,8},{10,11... | collective-permute-start | bytes 393224 | tf_op jit(solution)/shard_map/ppermute | solution.py:438
  137.3 2.5 %collective-permute-done.5 = f32[256,128]{1,0:T(8,128)S(1)} collective-permute-done((f32[256,128]{1,0:T(8,128)S(1)}, f32[256,128]{1,0:T(8,128)S(1)}, u32[]{:S(2)}, u32[]{:S(2)}) %collective-permute-start.5) | collective-permute-done | bytes 131104 | tf_op jit(solution)/shard_map/ppermute | solution.py:438
  139.9 1.9 %collective-permute-start.6 = (f32[256,128]{1,0:T(8,128)S(1)}, f32[256,128]{1,0:T(8,128)S(1)}, u32[]{:S(2)}, u32[]{:S(2)}) collective-permute-start(f32[256,128]{1,0:T(8,128)S(1)} %add.23), channel_id=1, source_target_pairs={{0,4},{1,5},{2,6},{3,7},{4,0},{5,1},{6,2},{7,3},{8,12},{9,13},{10,... | collective-permute-start | bytes 393224 | tf_op jit(solution)/shard_map/ppermute | solution.py:438
  141.7 4.7 %collective-permute-done.6 = f32[256,128]{1,0:T(8,128)S(1)} collective-permute-done((f32[256,128]{1,0:T(8,128)S(1)}, f32[256,128]{1,0:T(8,128)S(1)}, u32[]{:S(2)}, u32[]{:S(2)}) %collective-permute-start.6) | collective-permute-done | bytes 131104 | tf_op jit(solution)/shard_map/ppermute | solution.py:438
  148.4 3.1 %collective-permute-done.7 = f32[256,128]{1,0:T(8,128)S(1)} collective-permute-done((f32[256,128]{1,0:T(8,128)S(1)}, f32[256,128]{1,0:T(8,128)S(1)}, u32[]{:S(2)}, u32[]{:S(2)}) %collective-permute-start.7) | collective-permute-done | bytes 131104 | tf_op jit(solution)/shard_map/ppermute | solution.py:438
  (58 shorter events, 17.3 us)
Async XLA Ops:
  0.6 13.8 %copy-start = (bf16[8192,128]{1,0:T(8,128)(2,1)S(1)}, bf16[8192,128]{1,0:T(8,128)(2,1)}, u32[]{:S(2)}) copy-start(bf16[8192,128]{1,0:T(8,128)(2,1)} %a_ref.3) | copy-start | bytes 6291460
  0.7 13.8 %copy-start.3 = (bf16[256,128]{1,0:T(8,128)(2,1)S(1)}, bf16[256,128]{1,0:T(8,128)(2,1)}, u32[]{:S(2)}) copy-start(bf16[256,128]{1,0:T(8,128)(2,1)} %tan_ref.5) | copy-start | bytes 196612
  0.7 13.8 %copy-start.5 = (bf16[256,128]{1,0:T(8,128)(2,1)S(1)}, bf16[256,128]{1,0:T(8,128)(2,1)}, u32[]{:S(2)}) copy-start(bf16[256,128]{1,0:T(8,128)(2,1)} %f_ref.3) | copy-start | bytes 196612
  4.2 24.6 %all-to-all-start = ((bf16[32,48,128]{2,1,0:T(8,128)(2,1)}), bf16[32,48,128]{2,1,0:T(8,128)(2,1)S(1)}, u32[]{:S(2)}, u32[]{:S(2)}) async-start(bf16[32,48,128]{2,1,0:T(8,128)(2,1)} %mass_pass.1), calls=%async_computation | async-start | bytes 786432 | tf_op jit(solution)/shard_map/all_to_all | solution.py:429
  14.5 14.4 %copy-start.1 = (s32[256,1]{1,0:T(8,128)}, s32[256,1]{1,0:T(8,128)S(1)}, u32[]{:S(2)}) copy-start(s32[256,1]{1,0:T(8,128)S(1)} %copy.10.part_ref) | copy-start | bytes 3076
  30.5 17.3 %all-to-all-start.1 = ((bf16[8,320,128]{2,1,0:T(8,128)(2,1)}), bf16[8,320,128]{2,1,0:T(8,128)(2,1)S(1)}, u32[]{:S(2)}, u32[]{:S(2)}) async-start(bf16[8,320,128]{2,1,0:T(8,128)(2,1)} %pick.1), calls=%async_computation.1 | async-start | bytes 1310720 | tf_op jit(solution)/shard_map/all_to_all | solution.py:429
  53.4 2.0 %collective-permute-start.8 = (bf16[8,256,128]{2,1,0:T(8,128)(2,1)S(1)}, bf16[8,256,128]{2,1,0:T(8,128)(2,1)S(1)}, u32[]{:S(2)}, u32[]{:S(2)}) collective-permute-start(bf16[8,256,128]{2,1,0:T(8,128)(2,1)S(1)} %get-tuple-element.32), channel_id=1, source_target_pairs={{0,8},{8,0},{16,24},{24,16},{32,40},{40,32},{48,56},{56,48},{64,72... | collective-permute-start | bytes 1572872 | tf_op jit(solution)/shard_map/ppermute | solution.py:461
  60.1 2.2 %collective-permute-start.9 = (bf16[8,256,128]{2,1,0:T(8,128)(2,1)S(1)}, bf16[8,256,128]{2,1,0:T(8,128)(2,1)S(1)}, u32[]{:S(2)}, u32[]{:S(2)}) collective-permute-start(bf16[8,256,128]{2,1,0:T(8,128)(2,1)S(1)} %get-tuple-element.35), channel_id=1, source_target_pairs={{0,8},{8,0},{16,24},{24,16},{32,40},{40,32},{48,56},{56,48},{64,72... | collective-permute-start | bytes 1572872 | tf_op jit(solution)/shard_map/ppermute | solution.py:467
  60.3 14.5 %collective-permute-start.10 = (bf16[8,256,128]{2,1,0:T(8,128)(2,1)S(1)}, bf16[8,256,128]{2,1,0:T(8,128)(2,1)S(1)}, u32[]{:S(2)}, u32[]{:S(2)}) collective-permute-start(bf16[8,256,128]{2,1,0:T(8,128)(2,1)S(1)} %add_convert_fusion.1), channel_id=1, source_target_pairs={{0,128},{8,136},{16,144},{24,152},{32,160},{40,168},{48,176},{56,1... | collective-permute-start | bytes 1572872 | tf_op jit(solution)/shard_map/ppermute | solution.py:463
  74.9 57.3 %copy-start.2 = (s32[256,1]{1,0:T(8,128)S(1)}, s32[256,1]{1,0:T(8,128)}, u32[]{:S(2)}) copy-start(s32[256,1]{1,0:T(8,128)} %copy-done.1) | copy-start | bytes 3076
  96.3 38.8 %all-to-all-start.3 = ((bf16[8,256,128]{2,1,0:T(8,128)(2,1)}), bf16[8,256,128]{2,1,0:T(8,128)(2,1)S(1)}, u32[]{:S(2)}, u32[]{:S(2)}) async-start(bf16[8,256,128]{2,1,0:T(8,128)(2,1)} %final_pass.1), calls=%async_computation.3 | async-start | bytes 1048576 | tf_op jit(solution)/shard_map/all_to_all | solution.py:429
  99.8 1.3 collective-permute-start
  101.1 15.2 %collective-permute-start.1 = (bf16[64,128]{1,0:T(8,128)(2,1)S(1)}, bf16[64,128]{1,0:T(8,128)(2,1)S(1)}, u32[]{:S(2)}, u32[]{:S(2)}) collective-permute-start(bf16[64,128]{1,0:T(8,128)(2,1)S(1)} %pad_maximum_fusion.3), channel_id=1, source_target_pairs={{0,64},{8,72},{16,80},{24,88},{32,96},{40,104},{48,112},{56,120},{... | collective-permute-start | bytes 49160 | tf_op jit(solution)/shard_map/ppermute | solution.py:433
  116.3 5.1 %collective-permute-start.2 = (bf16[128,128]{1,0:T(8,128)(2,1)S(1)}, bf16[128,128]{1,0:T(8,128)(2,1)S(1)}, u32[]{:S(2)}, u32[]{:S(2)}) collective-permute-start(bf16[128,128]{1,0:T(8,128)(2,1)S(1)} %pad_maximum_fusion.2), channel_id=1, source_target_pairs={{0,32},{8,40},{16,48},{24,56},{32,0},{40,8},{48,16},{56,24},{64,96... | collective-permute-start | bytes 98312 | tf_op jit(solution)/shard_map/ppermute | solution.py:433
  121.4 4.3 %collective-permute-start.3 = (bf16[256,128]{1,0:T(8,128)(2,1)S(1)}, bf16[256,128]{1,0:T(8,128)(2,1)S(1)}, u32[]{:S(2)}, u32[]{:S(2)}) collective-permute-start(bf16[256,128]{1,0:T(8,128)(2,1)S(1)} %pad_maximum_fusion.1), channel_id=1, source_target_pairs={{0,16},{8,24},{16,0},{24,8},{32,48},{40,56},{48,32},{56,40},{64,80... | collective-permute-start | bytes 196616 | tf_op jit(solution)/shard_map/ppermute | solution.py:433
  125.7 6.5 %collective-permute-start.4 = (bf16[512,128]{1,0:T(8,128)(2,1)S(1)}, bf16[512,128]{1,0:T(8,128)(2,1)S(1)}, u32[]{:S(2)}, u32[]{:S(2)}) collective-permute-start(bf16[512,128]{1,0:T(8,128)(2,1)S(1)} %pad_maximum_fusion.own_ref), channel_id=1, source_target_pairs={{0,128},{8,136},{16,144},{24,152},{32,160},{40,168},{48,176},{56,1... | collective-permute-start | bytes 393224 | tf_op jit(solution)/shard_map/ppermute | solution.py:472
  133.3 6.6 %collective-permute-start.5 = (f32[256,128]{1,0:T(8,128)S(1)}, f32[256,128]{1,0:T(8,128)S(1)}, u32[]{:S(2)}, u32[]{:S(2)}) collective-permute-start(f32[256,128]{1,0:T(8,128)S(1)} %row_pass.1), channel_id=1, source_target_pairs={{0,1},{1,0},{2,3},{3,2},{4,5},{5,4},{6,7},{7,6},{8,9},{9,8},{10,11... | collective-permute-start | bytes 393224 | tf_op jit(solution)/shard_map/ppermute | solution.py:438
  135.2 12.6 %collective-permute-start.13 = (bf16[4,256,128]{2,1,0:T(8,128)(2,1)S(1)}, bf16[4,256,128]{2,1,0:T(8,128)(2,1)S(1)}, u32[]{:S(2)}, u32[]{:S(2)}) collective-permute-start(bf16[4,256,128]{2,1,0:T(8,128)(2,1)S(1)} %get-tuple-element.36), channel_id=1, source_target_pairs={{0,128},{8,136},{16,144},{24,152},{32,160},{40,168},{48,176},{56,1... | collective-permute-start | bytes 786440 | tf_op jit(solution)/shard_map/ppermute | solution.py:478
  136.5 11.3 %collective-permute-start.11 = (bf16[4,256,128]{2,1,0:T(8,128)(2,1)S(1)}, bf16[4,256,128]{2,1,0:T(8,128)(2,1)S(1)}, u32[]{:S(2)}, u32[]{:S(2)}) collective-permute-start(bf16[4,256,128]{2,1,0:T(8,128)(2,1)S(1)} %get-tuple-element.37), channel_id=1, source_target_pairs={{0,128},{8,136},{16,144},{24,152},{32,160},{40,168},{48,176},{56,1... | collective-permute-start | bytes 786440 | tf_op jit(solution)/shard_map/ppermute | solution.py:479
  137.3 14.8 %collective-permute-start.15 = (bf16[8,256,128]{2,1,0:T(8,128)(2,1)S(1)}, bf16[8,256,128]{2,1,0:T(8,128)(2,1)S(1)}, u32[]{:S(2)}, u32[]{:S(2)}) collective-permute-start(bf16[8,256,128]{2,1,0:T(8,128)(2,1)S(1)} %all-to-all-done.3.refs_0_), channel_id=1, source_target_pairs={{0,8},{8,0},{16,24},{24,16},{32,40},{40,32},{48,56},{56,48},{64,72... | collective-permute-start | bytes 1572872 | tf_op jit(solution)/shard_map/ppermute | solution.py:485
  139.9 6.6 %collective-permute-start.6 = (f32[256,128]{1,0:T(8,128)S(1)}, f32[256,128]{1,0:T(8,128)S(1)}, u32[]{:S(2)}, u32[]{:S(2)}) collective-permute-start(f32[256,128]{1,0:T(8,128)S(1)} %add.23), channel_id=1, source_target_pairs={{0,4},{1,5},{2,6},{3,7},{4,0},{5,1},{6,2},{7,3},{8,12},{9,13},{10,... | collective-permute-start | bytes 393224 | tf_op jit(solution)/shard_map/ppermute | solution.py:438
  146.4 5.1 %collective-permute-start.7 = (f32[256,128]{1,0:T(8,128)S(1)}, f32[256,128]{1,0:T(8,128)S(1)}, u32[]{:S(2)}, u32[]{:S(2)}) collective-permute-start(f32[256,128]{1,0:T(8,128)S(1)} %add.24), channel_id=1, source_target_pairs={{0,2},{1,3},{2,0},{3,1},{4,6},{5,7},{6,4},{7,5},{8,10},{9,11},{10,... | collective-permute-start | bytes 393224 | tf_op jit(solution)/shard_map/ppermute | solution.py:438
  147.8 6.0 %collective-permute-start.14 = (bf16[4,256,128]{2,1,0:T(8,128)(2,1)S(1)}, bf16[4,256,128]{2,1,0:T(8,128)(2,1)S(1)}, u32[]{:S(2)}, u32[]{:S(2)}) collective-permute-start(bf16[4,256,128]{2,1,0:T(8,128)(2,1)S(1)} %collective-permute-done.13.refs_0_), channel_id=1, source_target_pairs={{0,8},{8,0},{16,24},{24,16},{32,40},{40,32},{48,56},{56,48},{64,72... | collective-permute-start | bytes 786440 | tf_op jit(solution)/shard_map/ppermute | solution.py:486
  147.8 7.3 %collective-permute-start.12 = (bf16[4,256,128]{2,1,0:T(8,128)(2,1)S(1)}, bf16[4,256,128]{2,1,0:T(8,128)(2,1)S(1)}, u32[]{:S(2)}, u32[]{:S(2)}) collective-permute-start(bf16[4,256,128]{2,1,0:T(8,128)(2,1)S(1)} %collective-permute-done.11.refs_0_), channel_id=1, source_target_pairs={{0,8},{8,0},{16,24},{24,16},{32,40},{40,32},{48,56},{56,48},{64,72... | collective-permute-start | bytes 786440 | tf_op jit(solution)/shard_map/ppermute | solution.py:487
  (3 other events, 36.1 us)
